TPU v7x, 32 devices: a whole 2x2x4 slice. The times are simulated.
32 devices in a mesh: groups: 2 (over x), wide: 16 (over z, y, core).
Axes of the slice: x: 2, y: 2, z: 4, core: 2. Of those that a mesh axis runs over, the one named last changes fastest.
Arguments:
- prefix_hidden: bfloat16 [32, 256, 8192], P(('groups', 'wide')), parts along dimension 0, may hold values from -6 to 6
- prefix_lengths: int32 [32], P(('groups', 'wide')), parts along dimension 0, may hold values from 64 to 256
- action_noise: float32 [32, 50, 32], P(('groups', 'wide')), parts along dimension 0, may hold values from -4 to 4
- prefix_gain: float32 [8192], replicated, may hold values from 0.1 to 1.9
- key_weight: bfloat16 [8192, 512], P('wide'), may hold values from -0.0625 to 0.0625
- value_weight: bfloat16 [8192, 512], P('wide'), may hold values from -0.0625 to 0.0625
- input_weight: float32 [32, 1024], replicated, may hold values from -1 to 1
- expert_gain: float32 [1024], replicated, may hold values from 0.1 to 1.9
- expert_query: bfloat16 [1024, 1024], P('wide'), may hold values from -0.1875 to 0.1875
- expert_key: bfloat16 [1024, 512], P('wide'), may hold values from -5.3125 to 5.3125
- expert_value: bfloat16 [1024, 512], P('wide'), may hold values from -0.1875 to 0.1875
- expert_output: bfloat16 [1024, 1024], P('wide'), may hold values from -0.1875 to 0.1875
- final_gain: float32 [1024], replicated, may hold values from 0.1 to 1.9
- output_weight: bfloat16 [1024, 32], replicated, may hold values from -0.1875 to 0.1875
Outputs:
- actions: float32 [32, 50, 32], P(('groups', 'wide')), parts along dimension 0
There are 2 independent parts, one for each index of `groups`. A program takes and returns all parts, laid end to end along the dimension named above; an argument that names none is the same for every part. Nothing has to cross between parts.
Inputs may be any that keep to these rules, and one draw needn't show every extreme that they name: `prefix_lengths`: positions at or after a sample's length are padding and take no part.
All inputs are finite; a program needn't handle non-finite values.
Results may differ from a plain program's by a relative error of at most 0.0075.
Values may be sent and summed in bfloat16 or wider, within the bound.
No kernel may reach another device: no remote copies, remote signals or barrier semaphores. Data moves between devices by JAX's collectives and lax.ppermute only.
A program may use at most 128 MiB of HBM per device.

v0:
```python
import jax
import jax.numpy as jnp
from jax import lax
from jax.sharding import PartitionSpec as P

HEAD = 128
STEPS = 4


rope_base = 1000000.0
norm_eps = 1e-06


def normalize(values, norm_gain):
    mean_square = jnp.mean(values * values, axis=-1, keepdims=True)
    return values * lax.rsqrt(mean_square + norm_eps) * norm_gain


def rotate(values, positions):
    half_width = values.shape[-1] // 2
    inv_freqs = rope_base ** (-jnp.arange(half_width, dtype=jnp.float32) * 2.0 / values.shape[-1])
    angles = positions[:, None] * inv_freqs[None, :]
    cosine = jnp.cos(angles)[:, None, :]
    sine_part = jnp.sin(angles)[:, None, :]
    first_half = values[..., :half_width]
    second = values[..., half_width:]
    return jnp.concatenate(
        [first_half * cosine - second * sine_part, second * cosine + first_half * sine_part], -1
    )


def time_embedding(time_value, embed_width):
    half_width = embed_width // 2
    fraction = jnp.arange(half_width, dtype=jnp.float32) / (half_width - 1)
    period = 0.004 * (4.0 / 0.004) ** fraction
    angles = time_value * (2.0 * jnp.pi) / period
    return jnp.concatenate([jnp.sin(angles), jnp.cos(angles)])


def attend(queries, key_cache, value_cache, action_keys, action_values, is_valid):
    span_rows = queries.shape[0]
    groups = key_cache.shape[1] // HEAD
    group_ratio = queries.shape[1] // key_cache.shape[1]
    query_heads = queries.reshape(span_rows, groups, group_ratio, HEAD)
    prefix_keys = key_cache.reshape(-1, groups, HEAD)
    prefix_values = value_cache.reshape(-1, groups, HEAD)
    own_keys = action_keys.reshape(span_rows, groups, HEAD)
    own_values = action_values.reshape(span_rows, groups, HEAD)
    prefix_scores = jnp.einsum(
        "cgrh,pgh->grcp", query_heads, prefix_keys, preferred_element_type=jnp.float32
    )
    prefix_scores = jnp.where(is_valid[None, None, None, :], prefix_scores, -1e30)
    own_scores = jnp.einsum(
        "cgrh,ngh->grcn", query_heads, own_keys, preferred_element_type=jnp.float32
    )
    row_max = jnp.maximum(jnp.max(prefix_scores, -1), jnp.max(own_scores, -1))[..., None]
    prefix_exp = jnp.exp(prefix_scores - row_max)
    own_exp = jnp.exp(own_scores - row_max)
    prob_total = jnp.sum(prefix_exp, -1, keepdims=True) + jnp.sum(own_exp, -1, keepdims=True)
    prefix_prob = (prefix_exp / prob_total).astype(jnp.bfloat16)
    own_prob = (own_exp / prob_total).astype(jnp.bfloat16)
    attn_mixed = jnp.einsum(
        "grcp,pgh->cgrh", prefix_prob, prefix_values, preferred_element_type=jnp.float32
    )
    attn_mixed = attn_mixed + jnp.einsum(
        "grcn,ngh->cgrh", own_prob, own_values, preferred_element_type=jnp.float32
    )
    return attn_mixed.reshape(span_rows, -1).astype(jnp.bfloat16)


def expert_steps(
    noise_rows,
    length,
    input_weight,
    expert_gain,
    query_w,
    key_w,
    value_w,
    output_w,
    final_gain,
    output_weight,
    key_cache,
    value_cache,
):
    span_rows = noise_rows.shape[0]
    is_valid = jnp.arange(key_cache.shape[0], dtype=jnp.int32) < length
    positions = length.astype(jnp.float32) + jnp.arange(span_rows, dtype=jnp.float32)
    action_state = noise_rows
    for step_idx in range(STEPS):
        time_value = 1.0 - step_idx / STEPS
        hidden = jnp.dot(
            action_state,
            input_weight,
            precision=lax.Precision.HIGHEST,
            preferred_element_type=jnp.float32,
        )
        hidden = hidden + time_embedding(time_value, input_weight.shape[1])[None, :]
        normed = normalize(hidden, expert_gain).astype(jnp.bfloat16)
        raw_queries = jnp.dot(normed, query_w, preferred_element_type=jnp.float32)
        queries = rotate(raw_queries.reshape(span_rows, -1, HEAD), positions).reshape(span_rows, -1)
        queries = (queries * HEAD ** (-0.5)).astype(jnp.bfloat16)
        raw_keys = jnp.dot(normed, key_w, preferred_element_type=jnp.float32)
        action_keys = (
            rotate(raw_keys.reshape(span_rows, -1, HEAD), positions)
            .reshape(span_rows, -1)
            .astype(jnp.bfloat16)
        )
        action_values = jnp.dot(normed, value_w, preferred_element_type=jnp.float32).astype(
            jnp.bfloat16
        )
        attn_mixed = attend(queries, key_cache, value_cache, action_keys, action_values, is_valid)
        hidden = hidden + jnp.dot(attn_mixed, output_w, preferred_element_type=jnp.float32)
        final_normed = normalize(hidden, final_gain).astype(jnp.bfloat16)
        velocity = jnp.dot(final_normed, output_weight, preferred_element_type=jnp.float32)
        action_state = action_state - velocity / STEPS
    return action_state


def shards(
    prefix_hidden,
    prefix_lengths,
    action_noise,
    prefix_gain,
    key_weight,
    value_weight,
    input_weight,
    expert_gain,
    expert_query,
    expert_key,
    expert_value,
    expert_output,
    final_gain,
    output_weight,
):
    gathered = (
        lax.all_gather(expert_query, "wide", axis=0, tiled=True),
        lax.all_gather(expert_key, "wide", axis=0, tiled=True),
        lax.all_gather(expert_value, "wide", axis=0, tiled=True),
        lax.all_gather(expert_output, "wide", axis=0, tiled=True),
    )
    hidden = prefix_hidden[0]
    row_count = hidden.shape[0]
    normed = normalize(hidden.astype(jnp.float32), prefix_gain).astype(jnp.bfloat16)
    stacked = jnp.stack([key_weight, value_weight], 0)
    projected = jnp.einsum(
        "pd,kdc->pkc",
        normed,
        lax.all_gather(stacked, "wide", axis=1, tiled=True),
        preferred_element_type=jnp.float32,
    )
    positions = jnp.arange(row_count, dtype=jnp.float32)
    key_cache = (
        rotate(projected[:, 0].reshape(row_count, -1, HEAD), positions)
        .reshape(row_count, -1)
        .astype(jnp.bfloat16)
    )
    value_cache = projected[:, 1].astype(jnp.bfloat16)
    query_w, key_w, value_w, output_w = gathered
    action_state = expert_steps(
        action_noise[0],
        prefix_lengths[0],
        input_weight,
        expert_gain,
        query_w,
        key_w,
        value_w,
        output_w,
        final_gain,
        output_weight,
        key_cache,
        value_cache,
    )
    return action_state[None]


def solution(mesh):
    placed = (
        P(("groups", "wide"), None, None),
        P(("groups", "wide")),
        P(("groups", "wide"), None, None),
        P(),
        P("wide", None),
        P("wide", None),
        P(),
        P(),
        P("wide", None),
        P("wide", None),
        P("wide", None),
        P("wide", None),
        P(),
        P(),
    )
    return jax.shard_map(
        shards,
        mesh=mesh,
        in_specs=placed,
        out_specs=P(("groups", "wide"), None, None),
        check_vma=False,
    )
```

profile of v0, /device:TPU:0, one launch (start us, length us, event | category | flops | bytes accessed | tf_op | source)
XLA Modules:
  0.0 368.0 jit_solution(7898720133912089493)
XLA Ops:
  8.8 2.3 pad_maximum_fusion
  12.0 3.1 fusion
  19.0 31.2 %all-gather.10.cloned.1.call-done = bf16[1024,512]{1,0:T(8,128)(2,1)} async-done(((bf16[64,512]{1,0:T(8,128)(2,1)}), bf16[1024,512]{1,0:T(8,128)(2,1)}) %all-gather.10.cloned.1.call-update) | async-done | bytes 1048592 | tf_op jit(solution)/shard_map/all_gather | solution.py:137
  50.2 1.5 fusion.107
  51.9 37.4 %all-gather.12.cloned.1.call-done = bf16[1024,512]{1,0:T(8,128)(2,1)} async-done(((bf16[64,512]{1,0:T(8,128)(2,1)}), bf16[1024,512]{1,0:T(8,128)(2,1)}) %all-gather.12.cloned.1.call-update) | async-done | bytes 1048592 | tf_op jit(solution)/shard_map/all_gather | solution.py:138
  89.2 1.5 convolution_convert_fusion.3
  91.4 40.4 %all-gather.8.cloned.1.call-done = bf16[1024,1024]{1,0:T(8,128)(2,1)} async-done(((bf16[64,1024]{1,0:T(8,128)(2,1)}), bf16[1024,1024]{1,0:T(8,128)(2,1)}) %all-gather.8.cloned.1.call-update) | async-done | bytes 2097168 | tf_op jit(solution)/shard_map/all_gather | solution.py:136
  131.9 2.1 fusion.106
  134.6 124.5 %all-gather.6.cloned.1.call-done = bf16[2,8192,512]{2,1,0:T(8,128)(2,1)} async-done(((bf16[2,512,512]{2,1,0:T(8,128)(2,1)}), bf16[2,8192,512]{2,1,0:T(8,128)(2,1)}) %all-gather.6.cloned.1.call-update) | async-done | bytes 16777232 | tf_op jit(solution)/shard_map/all_gather | solution.py:148
  259.1 9.5 %fusion.4 = f32[256,2,512]{2,0,1:T(8,128)S(1)} fusion(bf16[2,8192,512]{2,1,0:T(8,128)(2,1)} %all-gather.6.cloned.1.call-done, bf16[1,256,8192]{2,1,0:T(8,128)(2,1)} %param.14, f32[8192]{0:T(1024)S(1)} %copy-done.58, f32[256]{0:T(256)S(1)} %add_rsqrt_fusion), kind=kOutput, calls=%fused_computation.6 | convolution fusion | flops 4303355904 | bytes 22053888 | tf_op jit(solution)/shard_map/pd,kdc->pkc/dot_general | solution.py:145
  271.2 29.5 %all-gather.14.cloned.1.call-done = bf16[1024,1024]{1,0:T(8,128)(2,1)} async-done(((bf16[64,1024]{1,0:T(8,128)(2,1)}), bf16[1024,1024]{1,0:T(8,128)(2,1)}) %all-gather.14.cloned.1.call-update) | async-done | bytes 2097168 | tf_op jit(solution)/shard_map/all_gather | solution.py:139
  300.8 2.2 multiply_reduce_fusion.6
  306.0 1.7 fusion.100
  308.6 1.6 reshape.311
  315.5 2.1 fusion.31
  318.5 1.5 reshape.312
  322.0 1.6 convert_element_type.174
  323.6 2.2 multiply_reduce_fusion.4
  331.1 1.6 reshape.314
  337.2 2.1 fusion.32
  340.2 1.5 reshape.315
  343.7 1.6 convert_element_type.184
  345.3 2.2 multiply_reduce_fusion.2
  354.5 2.3 fusion.33
  (245 shorter events, 45.8 us)
Async XLA Ops:
  6.5 9.1 %copy-start = (f32[32,1024]{1,0:T(8,128)S(1)}, f32[32,1024]{1,0:T(8,128)}, u32[]{:S(2)}) copy-start(f32[32,1024]{1,0:T(8,128)} %param.20) | copy-start | bytes 393220
  6.5 43.7 %all-gather.10.cloned.1.call-start = ((), (), s32[]{:S(2)}) async-start(), calls=%async_computation.2 | async-start | bytes 1114112 | tf_op jit(solution)/shard_map/all_gather | solution.py:137
  7.3 82.0 %all-gather.12.cloned.1.call-start = ((), (), s32[]{:S(2)}) async-start(), calls=%async_computation.3 | async-start | bytes 1114112 | tf_op jit(solution)/shard_map/all_gather | solution.py:138
  8.0 123.8 %all-gather.8.cloned.1.call-start = ((), (), s32[]{:S(2)}) async-start(), calls=%async_computation.1 | async-start | bytes 2228224 | tf_op jit(solution)/shard_map/all_gather | solution.py:136
  8.7 250.4 %all-gather.6.cloned.1.call-start = ((), (), s32[]{:S(2)}) async-start(), calls=%async_computation | async-start | bytes 17825792 | tf_op jit(solution)/shard_map/all_gather | solution.py:148
  11.1 289.7 %all-gather.14.cloned.1.call-start = ((), (), s32[]{:S(2)}) async-start(), calls=%async_computation.4 | async-start | bytes 2228224 | tf_op jit(solution)/shard_map/all_gather | solution.py:139
  12.0 6.9 %copy-start.41 = (f32[1024]{0:T(1024)S(1)}, f32[1024]{0:T(1024)}, u32[]{:S(2)}) copy-start(f32[1024]{0:T(1024)} %param.21) | copy-start | bytes 12292
  16.1 117.8 %copy-start.17 = (f32[50,1024]{1,0:T(8,128)}, f32[50,1024]{1,0:T(8,128)S(1)}, u32[]{:S(2)}) copy-start(f32[50,1024]{1,0:T(8,128)S(1)} %get-tuple-element.38) | copy-start | bytes 614404
  17.0 117.0 %copy-start.7 = (f32[50,64]{1,0:T(8,128)}, f32[50,64]{1,0:T(8,128)S(1)}, u32[]{:S(2)}) copy-start(f32[50,64]{1,0:T(8,128)S(1)} %get-tuple-element.33) | copy-start | bytes 38404
  17.0 117.0 %copy-start.12 = (f32[50,64]{1,0:T(8,128)}, f32[50,64]{1,0:T(8,128)S(1)}, u32[]{:S(2)}) copy-start(f32[50,64]{1,0:T(8,128)S(1)} %get-tuple-element.34) | copy-start | bytes 38404
  17.0 252.6 %copy-start.53 = (pred[256]{0:T(512)(128)(4,1)}, pred[256]{0:T(512)(128)(4,1)S(1)}, u32[]{:S(2)}) copy-start(pred[256]{0:T(512)(128)(4,1)S(1)} %iota_compare_fusion) | copy-start | bytes 772
  91.4 167.7 %copy-start.58 = (f32[8192]{0:T(1024)S(1)}, f32[8192]{0:T(1024)}, u32[]{:S(2)}) copy-start(f32[8192]{0:T(1024)} %param.17) | copy-start | bytes 98308
  270.1 30.6 %copy-start.18 = (f32[50,1024]{1,0:T(8,128)S(1)}, f32[50,1024]{1,0:T(8,128)}, u32[]{:S(2)}) copy-start(f32[50,1024]{1,0:T(8,128)} %copy-done.17) | copy-start | bytes 614404
  270.8 32.2 %copy-start.30 = (bf16[1024,32]{0,1:T(8,128)(2,1)S(1)}, bf16[1024,32]{0,1:T(8,128)(2,1)}, u32[]{:S(2)}) copy-start(bf16[1024,32]{0,1:T(8,128)(2,1)} %param.27) | copy-start | bytes 196612
  270.8 32.2 %copy-start.45 = (f32[1,50,32]{1,2,0:T(8,128)S(1)}, f32[1,50,32]{1,2,0:T(8,128)}, u32[]{:S(2)}) copy-start(f32[1,50,32]{1,2,0:T(8,128)} %param.16) | copy-start | bytes 19204
  270.8 32.2 %copy-start.46 = (f32[1024]{0:T(1024)S(1)}, f32[1024]{0:T(1024)}, u32[]{:S(2)}) copy-start(f32[1024]{0:T(1024)} %param.26) | copy-start | bytes 12292
  270.8 32.4 %copy-start.52 = (f32[1024]{0:T(1024)S(1)}, f32[1024]{0:T(1024)}, u32[]{:S(2)}) copy-start(f32[1024]{0:T(1024)} %pad_maximum_fusion.2) | copy-start | bytes 12292
  271.1 32.7 %copy-start.42 = (f32[1024]{0:T(1024)S(1)}, f32[1024]{0:T(1024)}, u32[]{:S(2)}) copy-start(f32[1024]{0:T(1024)} %param.21) | copy-start | bytes 12292
  271.1 33.4 %copy-start.1 = (bf16[1024,1024]{1,0:T(8,128)(2,1)S(1)}, bf16[1024,1024]{1,0:T(8,128)(2,1)}, u32[]{:S(2)}) copy-start(bf16[1024,1024]{1,0:T(8,128)(2,1)} %all-gather.8.cloned.1.call-done) | copy-start | bytes 6291460
  310.2 7.4 %copy-start.3 = (bf16[1024,512]{1,0:T(8,128)(2,1)S(1)}, bf16[1024,512]{1,0:T(8,128)(2,1)}, u32[]{:S(2)}) copy-start(bf16[1024,512]{1,0:T(8,128)(2,1)} %all-gather.12.cloned.1.call-done) | copy-start | bytes 3145732
  310.2 7.4 %copy-start.26 = (bf16[50,1024]{1,0:T(8,128)(2,1)S(1)}, bf16[50,1024]{1,0:T(8,128)(2,1)}, u32[]{:S(2)}) copy-start(bf16[50,1024]{1,0:T(8,128)(2,1)} %copy-done.25) | copy-start | bytes 307204
  332.6 6.7 %copy-start.28 = (bf16[50,1024]{1,0:T(8,128)(2,1)S(1)}, bf16[50,1024]{1,0:T(8,128)(2,1)}, u32[]{:S(2)}) copy-start(bf16[50,1024]{1,0:T(8,128)(2,1)} %copy-done.27) | copy-start | bytes 307204
  354.5 5.5 %copy-start.2 = (bf16[1024,1024]{1,0:T(8,128)(2,1)S(1)}, bf16[1024,1024]{1,0:T(8,128)(2,1)}, u32[]{:S(2)}) copy-start(bf16[1024,1024]{1,0:T(8,128)(2,1)} %all-gather.14.cloned.1.call-done) | copy-start | bytes 6291460
  354.5 5.5 %copy-start.20 = (f32[50,1024]{1,0:T(8,128)S(1)}, f32[50,1024]{1,0:T(8,128)}, u32[]{:S(2)}) copy-start(f32[50,1024]{1,0:T(8,128)} %copy-done.19) | copy-start | bytes 614404
  (40 other events, 77.0 us)
Sparse Core Ops, SparseCore 0:
  9.5 40.6 all-gather.9
  52.4 36.8 all-gather.11
  91.4 40.4 all-gather.7
  133.9 125.1 all-gather.5
  261.1 39.6 all-gather.13
where the time goes:
time: 369 us; the launch traced here: 368 us
  waiting for transfers between devices  266 us (72%)
  matrix products  50.5 us (14%)
  local copies, waits for them, and re-layouts  20.1 us (5%)
  other arithmetic  16.4 us (4%)
  between operations  15.1 us (4%)
    all_gather x1, waiting for transfers between devices, shards(): lax.all_gather(stacked, 'wide', axis=1, tiled=True)  124 us
    all_gather x1, waiting for transfers between devices, shards(): lax.all_gather(expert_query, 'wide', axis=0, tiled=True)  40.4 us
    all_gather x1, waiting for transfers between devices, shards(): lax.all_gather(expert_value, 'wide', axis=0, tiled=True)  37.4 us
    all_gather x1, waiting for transfers between devices, shards(): lax.all_gather(expert_key, 'wide', axis=0, tiled=True)  31.2 us
    all_gather x1, waiting for transfers between devices, shards(): lax.all_gather(expert_output, 'wide', axis=0, tiled=True)  29.5 us
    dot_general x1, matrix products, shards(): jnp.einsum('pd,kdc->pkc', normed, lax.all_gather(stacked, 'wide', axis=1,...  9.54 us
  transfers between devices with their start and end apart: 5, of which 5 were waited for; matrix products, arithmetic and copies ran while one was open for 7% of the time, Pallas kernels for 0%

commit v1 on v0

v1 whole, which is shorter than its diff:
```python
import functools

import jax
import jax.numpy as jnp
from jax import lax
from jax.experimental import pallas as pl
from jax.experimental.pallas import tpu as pltpu
from jax.sharding import PartitionSpec as P

HEAD = 128
STEPS = 4

rope_base = 1000000.0
norm_eps = 1e-06

ANY = pl.BlockSpec(memory_space=pl.ANY)
SMEM = pl.BlockSpec(memory_space=pltpu.SMEM)
VMEM = pl.BlockSpec(memory_space=pltpu.VMEM)


def rope_tables(positions, scale=1.0):
    half_width = HEAD // 2
    inv_freqs = rope_base ** (-jnp.arange(half_width, dtype=jnp.float32) * 2.0 / HEAD)
    angles = positions[:, None] * inv_freqs[None, :]
    cosine = jnp.cos(angles) * scale
    sine_part = jnp.sin(angles) * scale
    return (
        jnp.concatenate([cosine, cosine], -1),
        jnp.concatenate([-sine_part, sine_part], -1),
    )


def time_embedding(time_value, embed_width):
    half_width = embed_width // 2
    fraction = jnp.arange(half_width, dtype=jnp.float32) / (half_width - 1)
    period = 0.004 * (4.0 / 0.004) ** fraction
    angles = time_value * (2.0 * jnp.pi) / period
    return jnp.concatenate([jnp.sin(angles), jnp.cos(angles)])


def norm_kernel(picks, hidden_ref, gain_ref, *outs, chips, width):
    rows = hidden_ref[...].astype(jnp.float32)
    scale = lax.rsqrt(jnp.mean(rows * rows, axis=-1, keepdims=True) + norm_eps)
    for which, out in enumerate(outs):
        for chip in range(chips):
            start = pl.multiple_of((chip * 4 + picks[which]) * width, width)
            part = hidden_ref[:, pl.ds(start, width)].astype(jnp.float32)
            part = part * scale * gain_ref[:, pl.ds(start, width)]
            out[:, chip * width : (chip + 1) * width] = part.astype(jnp.bfloat16)


def norm_parts(hidden, gain, picks, chips):
    row_count, depth = hidden.shape
    width = depth // chips // 4
    if width % HEAD:
        wide = hidden.astype(jnp.float32)
        scale = lax.rsqrt(jnp.mean(wide * wide, axis=-1, keepdims=True) + norm_eps)
        parts = (wide * scale * gain).astype(jnp.bfloat16).reshape(row_count, chips, 4, width)
        return tuple(
            lax.dynamic_index_in_dim(parts, picks[k], 2, keepdims=False).reshape(row_count, -1)
            for k in range(4)
        )
    step = 64
    shape = jax.ShapeDtypeStruct((row_count, depth // 4), jnp.bfloat16)
    return pl.pallas_call(
        functools.partial(norm_kernel, chips=chips, width=width),
        grid_spec=pltpu.PrefetchScalarGridSpec(
            num_scalar_prefetch=1,
            grid=(row_count // step,),
            in_specs=[
                pl.BlockSpec((step, depth), lambda i, p: (i, 0)),
                pl.BlockSpec((1, depth), lambda i, p: (0, 0)),
            ],
            out_specs=[pl.BlockSpec((step, depth // 4), lambda i, p: (i, 0))] * 4,
        ),
        out_shape=[shape] * 4,
        name="prefix_norm",
    )(picks, hidden, gain[None, :])


def project_kernel(spots, first, second, *refs, count, width):
    pieces = refs[:count]
    first_out, second_out, weight, sems = refs[count:]
    copies = []
    for k, piece in enumerate(pieces):
        start = pl.multiple_of(spots[k] * width, width)
        copy = pltpu.make_async_copy(piece, weight.at[pl.ds(start, width)], sems.at[k])
        copy.start()
        copies.append(copy)
    for copy in copies:
        copy.wait()
    first_out[...] = jnp.dot(first[...], weight[...], preferred_element_type=jnp.float32)
    second_out[...] = jnp.dot(second[...], weight[...], preferred_element_type=jnp.float32)


def project(spots, first, second, pieces):
    width, columns = pieces[0].shape
    shape = jax.ShapeDtypeStruct((first.shape[0], columns), jnp.float32)
    return pl.pallas_call(
        functools.partial(project_kernel, count=len(pieces), width=width),
        in_specs=[SMEM, VMEM, VMEM] + [ANY] * len(pieces),
        out_specs=[VMEM, VMEM],
        out_shape=[shape, shape],
        scratch_shapes=[
            pltpu.VMEM((width * len(pieces), columns), jnp.bfloat16),
            pltpu.SemaphoreType.DMA((len(pieces),)),
        ],
        name="prefix_project",
    )(spots, first, second, *pieces)


def turn(values, cosine, sine):
    return values * cosine + pltpu.roll(values, HEAD // 2, 1) * sine


def expert_kernel(
    info,
    noise,
    input_weight,
    embed,
    expert_gain,
    final_gain,
    output_weight,
    query_cos,
    query_sin,
    action_cos,
    action_sin,
    prefix_cos,
    prefix_sin,
    kept,
    paired,
    twinned,
    *refs,
    span,
    heads,
    groups,
    proj_count,
    proj_rows,
    out_count,
    out_rows,
):
    proj_pieces = refs[:proj_count]
    out_pieces = refs[proj_count : proj_count + out_count]
    actions, proj, mix, key_cache, value_cache, joined, sems = refs[proj_count + out_count :]
    copies = []
    for k, piece in enumerate(proj_pieces):
        start = pl.multiple_of(info[1 + k] * proj_rows, proj_rows)
        copies.append(
            pltpu.make_async_copy(piece, proj.at[pl.ds(start, proj_rows)], sems.at[k])
        )
    late = []
    for k, piece in enumerate(out_pieces):
        for part in range(2):
            slot = 2 * k + part
            start = pl.multiple_of(info[1 + proj_count + slot] * out_rows, out_rows)
            late.append(
                pltpu.make_async_copy(
                    piece.at[pl.ds(part * out_rows, out_rows)],
                    mix.at[pl.ds(start, out_rows)],
                    sems.at[proj_count + slot],
                )
            )
    for copy in copies + late:
        copy.start()
    length = info[0]
    kv_width = groups * HEAD
    for g in range(groups):
        cut = slice(g * HEAD, (g + 1) * HEAD)
        raw = kept[:, cut] + paired[:, cut] + twinned[:, cut].astype(jnp.float32)
        key_cache[:, cut] = turn(raw, prefix_cos[...], prefix_sin[...]).astype(jnp.bfloat16)
        cut2 = slice(kv_width + g * HEAD, kv_width + (g + 1) * HEAD)
        raw = kept[:, cut2] + paired[:, cut2] + twinned[:, cut2].astype(jnp.float32)
        value_cache[:, cut] = raw.astype(jnp.bfloat16)
    for copy in copies + late:
        copy.wait()
    ratio = heads // groups
    rows = noise.shape[0]
    query_width = heads * HEAD
    contract = (((1,), (1,)), ((), ()))
    prefix_ok = lax.broadcasted_iota(jnp.int32, (1, key_cache.shape[0]), 1) < length
    own_ok = lax.broadcasted_iota(jnp.int32, (1, rows), 1) < span
    actions[...] = noise[...]

    def step(k, carry):
        state = actions[...]
        hidden = jnp.dot(
            state,
            input_weight[...],
            precision=lax.Precision.HIGHEST,
            preferred_element_type=jnp.float32,
        )
        hidden = hidden + embed[pl.ds(k, 1), :]
        square = jnp.mean(hidden * hidden, axis=-1, keepdims=True)
        normed = (hidden * lax.rsqrt(square + norm_eps) * expert_gain[...]).astype(jnp.bfloat16)
        raw = jnp.dot(normed, proj[...], preferred_element_type=jnp.float32)
        for g in range(groups):
            cut = slice(g * HEAD, (g + 1) * HEAD)
            own_keys = turn(
                raw[:, query_width + g * HEAD : query_width + (g + 1) * HEAD],
                action_cos[...],
                action_sin[...],
            ).astype(jnp.bfloat16)
            base = query_width + kv_width
            own_values = raw[:, base + g * HEAD : base + (g + 1) * HEAD].astype(jnp.bfloat16)
            queries = jnp.concatenate(
                [
                    turn(
                        raw[:, (g * ratio + r) * HEAD : (g * ratio + r + 1) * HEAD],
                        query_cos[...],
                        query_sin[...],
                    ).astype(jnp.bfloat16)
                    for r in range(ratio)
                ],
                0,
            )
            far = lax.dot_general(
                queries, key_cache[:, cut], contract, preferred_element_type=jnp.float32
            )
            near = lax.dot_general(queries, own_keys, contract, preferred_element_type=jnp.float32)
            far = jnp.where(prefix_ok, far, -1e30)
            near = jnp.where(own_ok, near, -1e30)
            row_max = jnp.maximum(
                jnp.max(far, -1, keepdims=True), jnp.max(near, -1, keepdims=True)
            )
            far = jnp.exp(far - row_max)
            near = jnp.exp(near - row_max)
            total = jnp.sum(far, -1, keepdims=True) + jnp.sum(near, -1, keepdims=True)
            inverse = 1.0 / total
            far = (far * inverse).astype(jnp.bfloat16)
            near = (near * inverse).astype(jnp.bfloat16)
            mixed = jnp.dot(far, value_cache[:, cut], preferred_element_type=jnp.float32)
            mixed = mixed + jnp.dot(near, own_values, preferred_element_type=jnp.float32)
            mixed = mixed.astype(jnp.bfloat16)
            for r in range(ratio):
                h = g * ratio + r
                joined[:, h * HEAD : (h + 1) * HEAD] = mixed[r * rows : (r + 1) * rows]
        hidden = hidden + jnp.dot(joined[...], mix[...], preferred_element_type=jnp.float32)
        square = jnp.mean(hidden * hidden, axis=-1, keepdims=True)
        normed = (hidden * lax.rsqrt(square + norm_eps) * final_gain[...]).astype(jnp.bfloat16)
        velocity = jnp.dot(normed, output_weight[...], preferred_element_type=jnp.float32)
        actions[...] = state - velocity / STEPS
        return carry

    lax.fori_loop(0, STEPS, step, 0)


def expert(info, dense, proj_pieces, out_pieces, span, groups):
    proj_rows, proj_width = proj_pieces[0].shape
    out_rows = out_pieces[0].shape[0] // 2
    noise = dense[0]
    prefix = dense[12].shape[0]
    proj_depth = proj_rows * len(proj_pieces)
    out_depth = out_rows * 2 * len(out_pieces)
    out_width = out_pieces[0].shape[1]
    heads = out_depth // HEAD
    return pl.pallas_call(
        functools.partial(
            expert_kernel,
            span=span,
            heads=heads,
            groups=groups,
            proj_count=len(proj_pieces),
            proj_rows=proj_rows,
            out_count=len(out_pieces),
            out_rows=out_rows,
        ),
        in_specs=[SMEM] + [VMEM] * len(dense) + [ANY] * (len(proj_pieces) + len(out_pieces)),
        out_specs=VMEM,
        out_shape=jax.ShapeDtypeStruct(noise.shape, jnp.float32),
        scratch_shapes=[
            pltpu.VMEM((proj_depth, proj_width), jnp.bfloat16),
            pltpu.VMEM((out_depth, out_width), jnp.bfloat16),
            pltpu.VMEM((prefix, groups * HEAD), jnp.bfloat16),
            pltpu.VMEM((prefix, groups * HEAD), jnp.bfloat16),
            pltpu.VMEM((noise.shape[0], heads * HEAD), jnp.bfloat16),
            pltpu.SemaphoreType.DMA((len(proj_pieces) + 2 * len(out_pieces),)),
        ],
        name="expert_steps",
    )(info, *dense, *proj_pieces, *out_pieces)


def shards(
    prefix_hidden,
    prefix_lengths,
    action_noise,
    prefix_gain,
    key_weight,
    value_weight,
    input_weight,
    expert_gain,
    expert_query,
    expert_key,
    expert_value,
    expert_output,
    final_gain,
    output_weight,
    *,
    group_count,
    wide_count,
):
    chips = wide_count // 2
    columns = chips // 2
    place = lax.axis_index("wide")
    core = place % 2
    row = place // 2 % 2
    column = place // 4
    twin = lax.axis_index("groups") % 2
    ring = [(w, (w + 4) % wide_count) for w in range(wide_count)]
    across = [(w, w ^ 2) for w in range(wide_count)]
    beside = [(w, w ^ 1) for w in range(wide_count)]
    facing = [(g, g ^ 1) for g in range(group_count)]
    corner = [
        (g * wide_count + w, (g ^ 1) * wide_count + (w ^ 1))
        for g in range(group_count)
        for w in range(wide_count)
    ]

    def round_ring(piece):
        slots = [piece]
        for _ in range(columns - 1):
            slots.append(lax.ppermute(slots[-1], "wide", ring))
        return slots

    def over(piece):
        return lax.ppermute(piece, "wide", across)

    def swap(piece):
        return lax.ppermute(piece, "wide", beside)

    half = key_weight.shape[0] // 2
    mine = jnp.concatenate(
        [
            lax.dynamic_slice_in_dim(key_weight, twin * half, half, 0),
            lax.dynamic_slice_in_dim(value_weight, twin * half, half, 0),
        ],
        1,
    )
    kv_slots = round_ring(mine)
    kv_pieces = kv_slots + [over(piece) for piece in kv_slots]

    own = core * 2 + twin
    picks = jnp.stack([own, own ^ 2, own ^ 1, own ^ 3]).astype(jnp.int32)
    kept, to_core, to_twin, to_corner = norm_parts(
        prefix_hidden[0], prefix_gain, picks, chips
    )
    from_twin = lax.ppermute(to_twin, "groups", facing)
    from_corner = lax.ppermute(to_corner, ("groups", "wide"), corner)
    from_core = swap(to_core)

    proj_slots = round_ring(jnp.concatenate([expert_query, expert_key, expert_value], 1))
    proj_pieces = proj_slots + [over(piece) for piece in proj_slots]
    proj_pieces = proj_pieces + [swap(piece) for piece in proj_pieces]
    out_pieces = round_ring(jnp.concatenate([expert_output, over(expert_output)], 0))
    out_pieces = out_pieces + [swap(piece) for piece in out_pieces]

    ring_columns = [(column - s) % columns for s in range(columns)]
    near_spots = [c * 2 + row for c in ring_columns] + [c * 2 + 1 - row for c in ring_columns]
    spots = jnp.stack(near_spots).astype(jnp.int32)
    own_part, core_part = project(spots, kept, from_core, kv_pieces)
    twin_part, corner_part = project(spots, from_twin, from_corner, kv_pieces)
    own_paired = swap(core_part)
    twin_sum = (twin_part + swap(corner_part)).astype(jnp.bfloat16)
    twinned = lax.ppermute(twin_sum, "groups", facing)

    proj_spots = [s * 2 + core for s in near_spots] + [s * 2 + 1 - core for s in near_spots]
    out_spots = []
    for side in (core, 1 - core):
        for c in ring_columns:
            out_spots += [(c * 2 + row) * 2 + side, (c * 2 + 1 - row) * 2 + side]
    length = prefix_lengths[0]
    info = jnp.stack([length] + proj_spots + out_spots).astype(jnp.int32)

    span, _ = action_noise.shape[1:]
    rows = -(-span // 16) * 16
    noise = jnp.pad(action_noise[0], ((0, rows - span), (0, 0)))
    embed = jnp.stack(
        [time_embedding(1.0 - k / STEPS, input_weight.shape[1]) for k in range(STEPS)]
    )
    positions = length.astype(jnp.float32) + jnp.arange(rows, dtype=jnp.float32)
    query_cos, query_sin = rope_tables(positions, HEAD ** (-0.5))
    action_cos, action_sin = rope_tables(positions)
    prefix_cos, prefix_sin = rope_tables(
        jnp.arange(prefix_hidden.shape[1], dtype=jnp.float32)
    )
    dense = (
        noise,
        input_weight,
        embed,
        expert_gain[None, :],
        final_gain[None, :],
        output_weight,
        query_cos,
        query_sin,
        action_cos,
        action_sin,
        prefix_cos,
        prefix_sin,
        own_part,
        own_paired,
        twinned,
    )
    groups = key_weight.shape[1] // HEAD
    actions = expert(info, dense, proj_pieces, out_pieces, span, groups)
    return actions[None, :span]


def solution(mesh):
    placed = (
        P(("groups", "wide"), None, None),
        P(("groups", "wide")),
        P(("groups", "wide"), None, None),
        P(),
        P("wide", None),
        P("wide", None),
        P(),
        P(),
        P("wide", None),
        P("wide", None),
        P("wide", None),
        P("wide", None),
        P(),
        P(),
    )
    return jax.shard_map(
        functools.partial(
            shards, group_count=mesh.shape["groups"], wide_count=mesh.shape["wide"]
        ),
        mesh=mesh,
        in_specs=placed,
        out_specs=P(("groups", "wide"), None, None),
        check_vma=False,
    )
```

time: 369 us -> 180 us (0.49)
  waiting for transfers between devices: 266 us -> 95 us
  matrix products: 50.5 us -> 0 us
  Pallas kernels: 0 us -> 39.6 us
  starting transfers between devices: 0.16 us -> 22.2 us
  between operations: 15.1 us -> 1.15 us
  local copies, waits for them, and re-layouts: 20.1 us -> 10.5 us
  other arithmetic: 16.4 us -> 11.3 us
    all_gather x5 -> x0, waiting for transfers between devices: 263 us -> none  [the longest x1 124 us: shards(): lax.all_gather(stacked, 'wide', axis=1, tiled=True)]
    ppermute x0 -> x36, waiting for transfers between devices: none -> 95 us  [the longest x9 49.6 us: round_ring(): slots.append(lax.ppermute(slots[-1], 'wide', ring))]
    dot_general x41 -> x0, matrix products: 50.5 us -> none  [the longest x1 9.54 us: shards(): jnp.einsum('pd,kdc->pkc', normed, lax.all_gather(stacked, 'wide', axis=1,...]
    pallas_call x0 -> x4, Pallas kernels: none -> 39.6 us  [the longest x1 19.4 us: expert(): pl.pallas_call(functools.partial(expert_kernel, span=span, heads=heads, g...]
    ppermute x0 -> x36, starting transfers between devices: none -> 22.2 us  [the longest x9 9.75 us: over(): return lax.ppermute(piece, 'wide', across)]
    reshape x12 -> x0, local copies, waits for them, and re-layouts: 7.68 us -> none  [the longest x4 4.41 us: attend(): own_values = action_values.reshape(span_rows, groups, HEAD)]
    reduce_sum x9 -> x0, other arithmetic: 6.5 us -> none  [the longest x4 3.15 us: attend(): jnp.sum(prefix_exp, -1, keepdims=True) + jnp.sum(own_exp, -1, keepdims=True)]
    convert_element_type x13 -> x0, local copies, waits for them, and re-layouts: 5.04 us -> none  [the longest x8 4.89 us: attend(): return attn_mixed.reshape(span_rows, -1).astype(jnp.bfloat16)]
  transfers between devices with their start and end apart: 5 -> 36, of which waited for: 5 -> 12; matrix products, arithmetic and copies ran while one was open for 7% -> 9% of each run, Pallas kernels for 0% -> 11%
where the time goes in v1:
time: 180 us
  waiting for transfers between devices  95 us (53%)
  Pallas kernels  39.6 us (22%)
  starting transfers between devices  22.2 us (12%)
  other arithmetic  11.3 us (6%)
  local copies, waits for them, and re-layouts  10.5 us (6%)
    ppermute x9, waiting for transfers between devices, round_ring(): slots.append(lax.ppermute(slots[-1], 'wide', ring))  49.6 us
    ppermute x9, waiting for transfers between devices, over(): return lax.ppermute(piece, 'wide', across)  25.2 us
    pallas_call x1, Pallas kernels, expert(): pl.pallas_call(functools.partial(expert_kernel, span=span, heads=heads, g...  19.4 us
    ppermute x1, waiting for transfers between devices, shards(): from_twin = lax.ppermute(to_twin, 'groups', facing)  15.5 us
    pallas_call x2, Pallas kernels, project(): pl.pallas_call(functools.partial(project_kernel, count=len(pieces), width...  14.2 us
    ppermute x9, starting transfers between devices, over(): return lax.ppermute(piece, 'wide', across)  9.75 us
    ppermute x9, starting transfers between devices, round_ring(): slots.append(lax.ppermute(slots[-1], 'wide', ring))  6.35 us
    pallas_call x1, Pallas kernels, norm_parts(): pl.pallas_call(functools.partial(norm_kernel, chips=chips, width=width),...  6.05 us
  transfers between devices with their start and end apart: 36, of which 12 were waited for; matrix products, arithmetic and copies ran while one was open for 9% of the time, Pallas kernels for 11%

profile of v1, /device:TPU:0, one launch (start us, length us, event | category | flops | bytes accessed | tf_op | source)
XLA Modules:
  0.0 179.7 jit_solution(2289576809550030821)
XLA Ops:
  1.2 3.1 %collective-permute-start.1 = (bf16[256,1024]{1,0:T(8,128)(2,1)S(1)}, bf16[256,1024]{1,0:T(8,128)(2,1)S(1)}, u32[]{:S(2)}, u32[]{:S(2)}) collective-permute-start(bf16[256,1024]{1,0:T(8,128)(2,1)S(1)} %pad_maximum_fusion.refs_0_), channel_id=1, source_target_pairs={{0,4},{1,5},{2,6},{3,7},{4,8},{5,9},{6,10},{7,11},{8,12},{9,13},{1... | collective-permute-start | bytes 1572872 | tf_op jit(solution)/shard_map/ppermute | solution.py:321
  4.3 13.9 %collective-permute-done.1.refs_1_ = bf16[256,1024]{1,0:T(8,128)(2,1)S(1)} collective-permute-done((bf16[256,1024]{1,0:T(8,128)(2,1)S(1)}, bf16[256,1024]{1,0:T(8,128)(2,1)S(1)}, u32[]{:S(2)}, u32[]{:S(2)}) %collective-permute-start.1) | collective-permute-done | bytes 524320 | tf_op jit(solution)/shard_map/ppermute | solution.py:321
  19.0 6.0 %prefix_norm.1 = (bf16[256,2048]{1,0:T(8,128)(2,1)}, bf16[256,2048]{1,0:T(8,128)(2,1)}, bf16[256,2048]{1,0:T(8,128)(2,1)}, bf16[256,2048]{1,0:T(8,128)(2,1)}) custom-call(s32[4]{0:T(128)} %pad_add_fusion.picks, bf16[256,8192]{1,0:T(8,128)(2,1)} %bitcast.48, f32[1,8192]{1,0:T(1,128)} %bitcast.50), custom_call_target="tpu_custom_call" | custom-call | tf_op jit(solution)/shard_map/prefix_norm/pallas_call | solution.py:65
  26.6 1.5 collective-permute-start.4
  29.3 3.9 %collective-permute-done.2.refs_2_ = bf16[256,1024]{1,0:T(8,128)(2,1)S(1)} collective-permute-done((bf16[256,1024]{1,0:T(8,128)(2,1)S(1)}, bf16[256,1024]{1,0:T(8,128)(2,1)S(1)}, u32[]{:S(2)}, u32[]{:S(2)}) %collective-permute-start.2) | collective-permute-done | bytes 524320 | tf_op jit(solution)/shard_map/ppermute | solution.py:321
  34.5 9.0 %collective-permute-done.28 = bf16[64,1024]{1,0:T(8,128)(2,1)S(1)} collective-permute-done((bf16[64,1024]{1,0:T(8,128)(2,1)S(1)}, bf16[64,1024]{1,0:T(8,128)(2,1)S(1)}, u32[]{:S(2)}, u32[]{:S(2)}) %collective-permute-start.28) | collective-permute-done | bytes 131104 | tf_op jit(solution)/shard_map/ppermute | solution.py:325
  44.7 8.7 %collective-permute-done.13.refs_1_ = bf16[64,2048]{1,0:T(8,128)(2,1)S(1)} collective-permute-done((bf16[64,2048]{1,0:T(8,128)(2,1)}, bf16[64,2048]{1,0:T(8,128)(2,1)S(1)}, u32[]{:S(2)}, u32[]{:S(2)}) %collective-permute-start.13) | collective-permute-done | bytes 262176 | tf_op jit(solution)/shard_map/ppermute | solution.py:321
  53.4 1.5 collective-permute-start.5
  55.5 1.6 collective-permute-start.7
  57.6 15.5 %collective-permute-done.9.first = bf16[256,2048]{1,0:T(8,128)(2,1)S(1)} collective-permute-done((bf16[256,2048]{1,0:T(8,128)(2,1)}, bf16[256,2048]{1,0:T(8,128)(2,1)S(1)}, u32[]{:S(2)}, u32[]{:S(2)}) %collective-permute-start.9) | collective-permute-done | bytes 1048608 | tf_op jit(solution)/shard_map/ppermute | solution.py:346
  74.5 5.0 %collective-permute-done.6.refs_6_ = bf16[256,1024]{1,0:T(8,128)(2,1)S(1)} collective-permute-done((bf16[256,1024]{1,0:T(8,128)(2,1)S(1)}, bf16[256,1024]{1,0:T(8,128)(2,1)S(1)}, u32[]{:S(2)}, u32[]{:S(2)}) %collective-permute-start.6) | collective-permute-done | bytes 524320 | tf_op jit(solution)/shard_map/ppermute | solution.py:325
  79.5 11.2 %collective-permute-done.7.refs_7_ = bf16[256,1024]{1,0:T(8,128)(2,1)S(1)} collective-permute-done((bf16[256,1024]{1,0:T(8,128)(2,1)S(1)}, bf16[256,1024]{1,0:T(8,128)(2,1)S(1)}, u32[]{:S(2)}, u32[]{:S(2)}) %collective-permute-start.7) | collective-permute-done | bytes 524320 | tf_op jit(solution)/shard_map/ppermute | solution.py:325
  92.3 7.1 %prefix_project.3 = (f32[256,1024]{1,0:T(8,128)}, f32[256,1024]{1,0:T(8,128)}) custom-call(s32[8]{0:T(128)} %stack.178.spots, bf16[256,2048]{1,0:T(8,128)(2,1)} %copy-done.9, bf16[256,2048]{1,0:T(8,128)(2,1)} %copy-done.8, bf16[256,1024]{1,0:T(8,128)(2,1)} %copy-done, bf16[256,1024]{1,0:T(8,128)(2,1)} %copy-done.1, bf16[256,1024]{1,0:T(8,128)(2,1)} %copy-done.2, ...), custom_call_target="tpu_custom_call" | custom-call | tf_op jit(solution)/shard_map/prefix_project/pallas_call | solution.py:99
  100.4 1.5 collective-permute-start.17
  102.2 7.3 %collective-permute-done.14.refs_2_ = bf16[64,2048]{1,0:T(8,128)(2,1)} collective-permute-done((bf16[64,2048]{1,0:T(8,128)(2,1)}, bf16[64,2048]{1,0:T(8,128)(2,1)}, u32[]{:S(2)}, u32[]{:S(2)}) %collective-permute-start.14) | collective-permute-done | bytes 262176 | tf_op jit(solution)/shard_map/ppermute | solution.py:321
  114.0 7.0 %collective-permute-done.30.refs_18_ = bf16[128,1024]{1,0:T(8,128)(2,1)} collective-permute-done((bf16[128,1024]{1,0:T(8,128)(2,1)}, bf16[128,1024]{1,0:T(8,128)(2,1)}, u32[]{:S(2)}, u32[]{:S(2)}) %collective-permute-start.30) | collective-permute-done | bytes 262176 | tf_op jit(solution)/shard_map/ppermute | solution.py:321
  121.0 1.5 collective-permute-start.18
  123.6 7.1 %prefix_project.2 = (f32[256,1024]{1,0:T(8,128)}, f32[256,1024]{1,0:T(8,128)}) custom-call(s32[8]{0:T(128)} %stack.178.spots, bf16[256,2048]{1,0:T(8,128)(2,1)} %get-tuple-element.13.first, bf16[256,2048]{1,0:T(8,128)(2,1)} %collective-permute-done.second, bf16[256,1024]{1,0:T(8,128)(2,1)} %copy-done, bf16[256,1024]{1,0:T(8,128)(2,1)} %copy-done.1, ...), custom_call_target="tpu_custom_call" | custom-call | tf_op jit(solution)/shard_map/prefix_project/pallas_call | solution.py:99
  132.2 1.5 pad_maximum_fusion.3
  135.6 8.8 %collective-permute-done.31.refs_19_ = bf16[128,1024]{1,0:T(8,128)(2,1)} collective-permute-done((bf16[128,1024]{1,0:T(8,128)(2,1)}, bf16[128,1024]{1,0:T(8,128)(2,1)}, u32[]{:S(2)}, u32[]{:S(2)}) %collective-permute-start.31) | collective-permute-done | bytes 262176 | tf_op jit(solution)/shard_map/ppermute | solution.py:321
  144.4 1.8 %collective-permute-start.12 = (bf16[256,1024]{1,0:T(8,128)(2,1)}, bf16[256,1024]{1,0:T(8,128)(2,1)S(1)}, u32[]{:S(2)}, u32[]{:S(2)}) collective-permute-start(bf16[256,1024]{1,0:T(8,128)(2,1)} %add_convert_fusion), channel_id=1, source_target_pairs={{0,16},{16,0},{1,17},{17,1},{2,18},{18,2},{3,19},{19,3},{4,20},{20... | collective-permute-start | bytes 1572872 | tf_op jit(solution)/shard_map/ppermute | solution.py:363
  149.4 1.7 copy.16.output_weight
  154.0 4.1 %collective-permute-done.12.twinned = bf16[256,1024]{1,0:T(8,128)(2,1)S(1)} collective-permute-done((bf16[256,1024]{1,0:T(8,128)(2,1)}, bf16[256,1024]{1,0:T(8,128)(2,1)S(1)}, u32[]{:S(2)}, u32[]{:S(2)}) %collective-permute-start.12) | collective-permute-done | bytes 524320 | tf_op jit(solution)/shard_map/ppermute | solution.py:363
  158.9 19.4 %expert_steps.1 = f32[64,32]{1,0:T(8,128)} custom-call(s32[33]{0:T(128)} %stack.164.info, f32[64,32]{1,0:T(8,128)} %pad.4.noise, f32[32,1024]{1,0:T(8,128)} %input_weight.1, f32[4,1024]{1,0:T(4,128)} %pad_maximum_fusion.7.embed, f32[1,1024]{1,0:T(1,128)} %bitcast.55, f32[1,1024]{1,0:T(1,128)} %bitcast.56, bf16[1024,32]{1,0:T(8,128)(2,1)} %copy.16.output_weight, ...), custom_call_target="tpu_custom_call" | custom-call | tf_op jit(solution)/shard_map/expert_steps/pallas_call | solution.py:256
  (134 shorter events, 28.7 us)
Async XLA Ops:
  1.2 17.1 %collective-permute-start.1 = (bf16[256,1024]{1,0:T(8,128)(2,1)S(1)}, bf16[256,1024]{1,0:T(8,128)(2,1)S(1)}, u32[]{:S(2)}, u32[]{:S(2)}) collective-permute-start(bf16[256,1024]{1,0:T(8,128)(2,1)S(1)} %pad_maximum_fusion.refs_0_), channel_id=1, source_target_pairs={{0,4},{1,5},{2,6},{3,7},{4,8},{5,9},{6,10},{7,11},{8,12},{9,13},{1... | collective-permute-start | bytes 1572872 | tf_op jit(solution)/shard_map/ppermute | solution.py:321
  18.3 14.9 %collective-permute-start.2 = (bf16[256,1024]{1,0:T(8,128)(2,1)S(1)}, bf16[256,1024]{1,0:T(8,128)(2,1)S(1)}, u32[]{:S(2)}, u32[]{:S(2)}) collective-permute-start(bf16[256,1024]{1,0:T(8,128)(2,1)S(1)} %collective-permute-done.1.refs_1_), channel_id=1, source_target_pairs={{0,4},{1,5},{2,6},{3,7},{4,8},{5,9},{6,10},{7,11},{8,12},{9,13},{1... | collective-permute-start | bytes 1572872 | tf_op jit(solution)/shard_map/ppermute | solution.py:321
  25.0 32.0 %collective-permute-start.10 = (bf16[256,2048]{1,0:T(8,128)(2,1)}, bf16[256,2048]{1,0:T(8,128)(2,1)S(1)}, u32[]{:S(2)}, u32[]{:S(2)}) collective-permute-start(bf16[256,2048]{1,0:T(8,128)(2,1)} %get-tuple-element.18), channel_id=1, source_target_pairs={{0,17},{1,16},{2,19},{3,18},{4,21},{5,20},{6,23},{7,22},{8,25},{9,... | collective-permute-start | bytes 3145736 | tf_op jit(solution)/shard_map/ppermute | solution.py:347
  25.2 48.0 %collective-permute-start.9 = (bf16[256,2048]{1,0:T(8,128)(2,1)}, bf16[256,2048]{1,0:T(8,128)(2,1)S(1)}, u32[]{:S(2)}, u32[]{:S(2)}) collective-permute-start(bf16[256,2048]{1,0:T(8,128)(2,1)} %get-tuple-element.17), channel_id=1, source_target_pairs={{0,16},{16,0},{1,17},{17,1},{2,18},{18,2},{3,19},{19,3},{4,20},{20... | collective-permute-start | bytes 3145736 | tf_op jit(solution)/shard_map/ppermute | solution.py:346
  26.6 28.4 %collective-permute-start.4 = (bf16[256,1024]{1,0:T(8,128)(2,1)S(1)}, bf16[256,1024]{1,0:T(8,128)(2,1)S(1)}, u32[]{:S(2)}, u32[]{:S(2)}) collective-permute-start(bf16[256,1024]{1,0:T(8,128)(2,1)S(1)} %pad_maximum_fusion.refs_0_), channel_id=1, source_target_pairs={{0,2},{1,3},{2,0},{3,1},{4,6},{5,7},{6,4},{7,5},{8,10},{9,11},{10,... | collective-permute-start | bytes 1572872 | tf_op jit(solution)/shard_map/ppermute | solution.py:325
  28.1 15.5 %collective-permute-start.28 = (bf16[64,1024]{1,0:T(8,128)(2,1)S(1)}, bf16[64,1024]{1,0:T(8,128)(2,1)S(1)}, u32[]{:S(2)}, u32[]{:S(2)}) collective-permute-start(bf16[64,1024]{1,0:T(8,128)(2,1)S(1)} %copy-done.20), channel_id=1, source_target_pairs={{0,2},{1,3},{2,0},{3,1},{4,6},{5,7},{6,4},{7,5},{8,10},{9,11},{10,... | collective-permute-start | bytes 393224 | tf_op jit(solution)/shard_map/ppermute | solution.py:325
  33.2 22.3 %collective-permute-start.3 = (bf16[256,1024]{1,0:T(8,128)(2,1)S(1)}, bf16[256,1024]{1,0:T(8,128)(2,1)S(1)}, u32[]{:S(2)}, u32[]{:S(2)}) collective-permute-start(bf16[256,1024]{1,0:T(8,128)(2,1)S(1)} %collective-permute-done.2.refs_2_), channel_id=1, source_target_pairs={{0,4},{1,5},{2,6},{3,7},{4,8},{5,9},{6,10},{7,11},{8,12},{9,13},{1... | collective-permute-start | bytes 1572872 | tf_op jit(solution)/shard_map/ppermute | solution.py:321
  53.4 20.5 %collective-permute-start.5 = (bf16[256,1024]{1,0:T(8,128)(2,1)S(1)}, bf16[256,1024]{1,0:T(8,128)(2,1)S(1)}, u32[]{:S(2)}, u32[]{:S(2)}) collective-permute-start(bf16[256,1024]{1,0:T(8,128)(2,1)S(1)} %collective-permute-done.1.refs_1_), channel_id=1, source_target_pairs={{0,2},{1,3},{2,0},{3,1},{4,6},{5,7},{6,4},{7,5},{8,10},{9,11},{10,... | collective-permute-start | bytes 1572872 | tf_op jit(solution)/shard_map/ppermute | solution.py:325
  54.9 24.5 %collective-permute-start.6 = (bf16[256,1024]{1,0:T(8,128)(2,1)S(1)}, bf16[256,1024]{1,0:T(8,128)(2,1)S(1)}, u32[]{:S(2)}, u32[]{:S(2)}) collective-permute-start(bf16[256,1024]{1,0:T(8,128)(2,1)S(1)} %collective-permute-done.2.refs_2_), channel_id=1, source_target_pairs={{0,2},{1,3},{2,0},{3,1},{4,6},{5,7},{6,4},{7,5},{8,10},{9,11},{10,... | collective-permute-start | bytes 1572872 | tf_op jit(solution)/shard_map/ppermute | solution.py:325
  55.5 35.2 %collective-permute-start.7 = (bf16[256,1024]{1,0:T(8,128)(2,1)S(1)}, bf16[256,1024]{1,0:T(8,128)(2,1)S(1)}, u32[]{:S(2)}, u32[]{:S(2)}) collective-permute-start(bf16[256,1024]{1,0:T(8,128)(2,1)S(1)} %collective-permute-done.3.refs_3_), channel_id=1, source_target_pairs={{0,2},{1,3},{2,0},{3,1},{4,6},{5,7},{6,4},{7,5},{8,10},{9,11},{10,... | collective-permute-start | bytes 1572872 | tf_op jit(solution)/shard_map/ppermute | solution.py:325
  57.1 42.3 %collective-permute-start.16 = (bf16[64,2048]{1,0:T(8,128)(2,1)}, bf16[64,2048]{1,0:T(8,128)(2,1)}, u32[]{:S(2)}, u32[]{:S(2)}) collective-permute-start(bf16[64,2048]{1,0:T(8,128)(2,1)} %constant_dynamic-update-slice_fusion.refs_0_), channel_id=1, source_target_pairs={{0,2},{1,3},{2,0},{3,1},{4,6},{5,7},{6,4},{7,5},{8,10},{9,11},{10,... | collective-permute-start | bytes 786440 | tf_op jit(solution)/shard_map/ppermute | solution.py:325
  73.2 26.3 %collective-permute-start.20 = (bf16[64,2048]{1,0:T(8,128)(2,1)}, bf16[64,2048]{1,0:T(8,128)(2,1)}, u32[]{:S(2)}, u32[]{:S(2)}) collective-permute-start(bf16[64,2048]{1,0:T(8,128)(2,1)} %constant_dynamic-update-slice_fusion.refs_0_), channel_id=1, source_target_pairs={{0,1},{1,0},{2,3},{3,2},{4,5},{5,4},{6,7},{7,6},{8,9},{9,8},{10,11... | collective-permute-start | bytes 786440 | tf_op jit(solution)/shard_map/ppermute | solution.py:328
  74.0 48.5 %collective-permute-start = (bf16[256,2048]{1,0:T(8,128)(2,1)}, bf16[256,2048]{1,0:T(8,128)(2,1)}, u32[]{:S(2)}, u32[]{:S(2)}) collective-permute-start(bf16[256,2048]{1,0:T(8,128)(2,1)} %get-tuple-element.14), channel_id=1, source_target_pairs={{0,1},{1,0},{2,3},{3,2},{4,5},{5,4},{6,7},{7,6},{8,9},{9,8},{10,11... | collective-permute-start | bytes 3145736 | tf_op jit(solution)/shard_map/ppermute | solution.py:328
  79.5 20.9 %collective-permute-start.29 = (bf16[128,1024]{1,0:T(8,128)(2,1)S(1)}, bf16[128,1024]{1,0:T(8,128)(2,1)}, u32[]{:S(2)}, u32[]{:S(2)}) collective-permute-start(bf16[128,1024]{1,0:T(8,128)(2,1)S(1)} %constant_dynamic-update-slice_fusion.3.refs_16_), channel_id=1, source_target_pairs={{0,4},{1,5},{2,6},{3,7},{4,8},{5,9},{6,10},{7,11},{8,12},{9,13},{1... | collective-permute-start | bytes 786440 | tf_op jit(solution)/shard_map/ppermute | solution.py:321
  99.5 35.2 %collective-permute-start.11 = (f32[256,1024]{1,0:T(8,128)}, f32[256,1024]{1,0:T(8,128)S(1)}, u32[]{:S(2)}, u32[]{:S(2)}) collective-permute-start(f32[256,1024]{1,0:T(8,128)} %get-tuple-element.20), channel_id=1, source_target_pairs={{0,1},{1,0},{2,3},{3,2},{4,5},{5,4},{6,7},{7,6},{8,9},{9,8},{10,11... | collective-permute-start | bytes 3145736 | tf_op jit(solution)/shard_map/ppermute | solution.py:328
  110.1 12.4 %collective-permute-start.33 = (bf16[128,1024]{1,0:T(8,128)(2,1)}, bf16[128,1024]{1,0:T(8,128)(2,1)}, u32[]{:S(2)}, u32[]{:S(2)}) collective-permute-start(bf16[128,1024]{1,0:T(8,128)(2,1)} %collective-permute-done.29.refs_17_), channel_id=1, source_target_pairs={{0,1},{1,0},{2,3},{3,2},{4,5},{5,4},{6,7},{7,6},{8,9},{9,8},{10,11... | collective-permute-start | bytes 786440 | tf_op jit(solution)/shard_map/ppermute | solution.py:328
  111.4 19.3 %collective-permute-start.15 = (bf16[64,2048]{1,0:T(8,128)(2,1)}, bf16[64,2048]{1,0:T(8,128)(2,1)S(1)}, u32[]{:S(2)}, u32[]{:S(2)}) collective-permute-start(bf16[64,2048]{1,0:T(8,128)(2,1)} %collective-permute-done.14.refs_2_), channel_id=1, source_target_pairs={{0,4},{1,5},{2,6},{3,7},{4,8},{5,9},{6,10},{7,11},{8,12},{9,13},{1... | collective-permute-start | bytes 786440 | tf_op jit(solution)/shard_map/ppermute | solution.py:321
  121.0 12.7 %collective-permute-start.18 = (bf16[64,2048]{1,0:T(8,128)(2,1)}, bf16[64,2048]{1,0:T(8,128)(2,1)}, u32[]{:S(2)}, u32[]{:S(2)}) collective-permute-start(bf16[64,2048]{1,0:T(8,128)(2,1)} %collective-permute-done.14.refs_2_), channel_id=1, source_target_pairs={{0,2},{1,3},{2,0},{3,1},{4,6},{5,7},{6,4},{7,5},{8,10},{9,11},{10,... | collective-permute-start | bytes 786440 | tf_op jit(solution)/shard_map/ppermute | solution.py:325
  122.5 11.7 %collective-permute-start.25 = (bf16[64,2048]{1,0:T(8,128)(2,1)}, bf16[64,2048]{1,0:T(8,128)(2,1)}, u32[]{:S(2)}, u32[]{:S(2)}) collective-permute-start(bf16[64,2048]{1,0:T(8,128)(2,1)} %collective-permute-done.17.refs_5_), channel_id=1, source_target_pairs={{0,1},{1,0},{2,3},{3,2},{4,5},{5,4},{6,7},{7,6},{8,9},{9,8},{10,11... | collective-permute-start | bytes 786440 | tf_op jit(solution)/shard_map/ppermute | solution.py:328
  131.4 22.6 %collective-permute-start.8 = (f32[256,1024]{1,0:T(8,128)}, f32[256,1024]{1,0:T(8,128)S(1)}, u32[]{:S(2)}, u32[]{:S(2)}) collective-permute-start(f32[256,1024]{1,0:T(8,128)} %get-tuple-element.16), channel_id=1, source_target_pairs={{0,1},{1,0},{2,3},{3,2},{4,5},{5,4},{6,7},{7,6},{8,9},{9,8},{10,11... | collective-permute-start | bytes 3145736 | tf_op jit(solution)/shard_map/ppermute | solution.py:328
  133.7 13.7 %collective-permute-start.34 = (bf16[128,1024]{1,0:T(8,128)(2,1)}, bf16[128,1024]{1,0:T(8,128)(2,1)}, u32[]{:S(2)}, u32[]{:S(2)}) collective-permute-start(bf16[128,1024]{1,0:T(8,128)(2,1)} %collective-permute-done.30.refs_18_), channel_id=1, source_target_pairs={{0,1},{1,0},{2,3},{3,2},{4,5},{5,4},{6,7},{7,6},{8,9},{9,8},{10,11... | collective-permute-start | bytes 786440 | tf_op jit(solution)/shard_map/ppermute | solution.py:328
  134.2 13.3 %collective-permute-start.19 = (bf16[64,2048]{1,0:T(8,128)(2,1)}, bf16[64,2048]{1,0:T(8,128)(2,1)}, u32[]{:S(2)}, u32[]{:S(2)}) collective-permute-start(bf16[64,2048]{1,0:T(8,128)(2,1)} %copy-done.15), channel_id=1, source_target_pairs={{0,2},{1,3},{2,0},{3,1},{4,6},{5,7},{6,4},{7,5},{8,10},{9,11},{10,... | collective-permute-start | bytes 786440 | tf_op jit(solution)/shard_map/ppermute | solution.py:325
  134.7 13.3 %collective-permute-start.23 = (bf16[64,2048]{1,0:T(8,128)(2,1)}, bf16[64,2048]{1,0:T(8,128)(2,1)}, u32[]{:S(2)}, u32[]{:S(2)}) collective-permute-start(bf16[64,2048]{1,0:T(8,128)(2,1)} %copy-done.15), channel_id=1, source_target_pairs={{0,1},{1,0},{2,3},{3,2},{4,5},{5,4},{6,7},{7,6},{8,9},{9,8},{10,11... | collective-permute-start | bytes 786440 | tf_op jit(solution)/shard_map/ppermute | solution.py:328
  144.4 13.7 %collective-permute-start.12 = (bf16[256,1024]{1,0:T(8,128)(2,1)}, bf16[256,1024]{1,0:T(8,128)(2,1)S(1)}, u32[]{:S(2)}, u32[]{:S(2)}) collective-permute-start(bf16[256,1024]{1,0:T(8,128)(2,1)} %add_convert_fusion), channel_id=1, source_target_pairs={{0,16},{16,0},{1,17},{17,1},{2,18},{18,2},{3,19},{19,3},{4,20},{20... | collective-permute-start | bytes 1572872 | tf_op jit(solution)/shard_map/ppermute | solution.py:363
  (37 other events, 824.6 us)

commit v2 on v1

v2 whole, which is shorter than its diff:
```python
import functools

import jax
import jax.numpy as jnp
from jax import lax
from jax.experimental import pallas as pl
from jax.experimental.pallas import tpu as pltpu
from jax.sharding import PartitionSpec as P


HEAD = 128
STEPS = 4

rope_base = 1000000.0
norm_eps = 1e-06


ANY = pl.BlockSpec(memory_space=pl.ANY)
SMEM = pl.BlockSpec(memory_space=pltpu.SMEM)
VMEM = pl.BlockSpec(memory_space=pltpu.VMEM)


def rope_tables(positions, scale=1.0):
    half_width = HEAD // 2
    inv_freqs = rope_base ** (-jnp.arange(half_width, dtype=jnp.float32) * 2.0 / HEAD)
    angles = positions[:, None] * inv_freqs[None, :]
    cosine = jnp.cos(angles) * scale
    sine_part = jnp.sin(angles) * scale
    return (
        jnp.concatenate([cosine, cosine], -1),
        jnp.concatenate([-sine_part, sine_part], -1),
    )


def time_embedding(time_value, embed_width):
    half_width = embed_width // 2
    fraction = jnp.arange(half_width, dtype=jnp.float32) / (half_width - 1)
    period = 0.004 * (4.0 / 0.004) ** fraction
    angles = time_value * (2.0 * jnp.pi) / period
    return jnp.concatenate([jnp.sin(angles), jnp.cos(angles)])


def places():
    place = lax.axis_index("wide")
    core = lax.rem(place, 2)
    row = lax.rem(lax.div(place, 2), 2)
    column = lax.div(place, 4)
    twin = lax.rem(lax.axis_index("groups"), 2)
    return core, row, column, twin


def chip_spots(row, column, columns):
    ring = [lax.rem(column + (columns - s), columns) for s in range(columns)]
    return [c * 2 + row for c in ring] + [c * 2 + (1 - row) for c in ring]


def pick_kernel(hidden, out, sems, *, flip, chips, width):
    core, _, _, twin = places()
    core = 1 - core if flip & 2 else core
    twin = 1 - twin if flip & 1 else twin
    part = core * 2 + twin
    copies = []
    for chip in range(chips):
        start = pl.multiple_of((chip * 4 + part) * width, width)
        copies.append(
            pltpu.make_async_copy(
                hidden.at[:, pl.ds(start, width)],
                out.at[:, pl.ds(chip * width, width)],
                sems.at[chip],
            )
        )
    for copy in copies:
        copy.start()
    for copy in copies:
        copy.wait()


def pick(hidden, flip, chips):
    row_count, depth = hidden.shape
    width = depth // chips // 4
    if width % HEAD:
        core, _, _, twin = places()
        part = (core * 2 + twin) ^ flip
        parts = hidden.reshape(row_count, chips, 4, width)
        return lax.dynamic_index_in_dim(parts, part, 2, keepdims=False).reshape(row_count, -1)
    return pl.pallas_call(
        functools.partial(pick_kernel, flip=flip, chips=chips, width=width),
        in_specs=[ANY],
        out_specs=VMEM,
        out_shape=jax.ShapeDtypeStruct((row_count, depth // 4), jnp.bfloat16),
        scratch_shapes=[pltpu.SemaphoreType.DMA((chips,))],
        name="pick_columns",
    )(hidden)


def own_kernel(hidden, kept, row_scale, *, chips, width):
    core, _, _, twin = places()
    part = core * 2 + twin
    rows = hidden[...].astype(jnp.float32)
    row_scale[...] = lax.rsqrt(jnp.mean(rows * rows, axis=-1, keepdims=True) + norm_eps)
    for chip in range(chips):
        start = pl.multiple_of((chip * 4 + part) * width, width)
        kept[:, chip * width : (chip + 1) * width] = hidden[:, pl.ds(start, width)]


def own_part_and_scale(hidden, chips):
    row_count, depth = hidden.shape
    width = depth // chips // 4
    if width % HEAD:
        rows = hidden.astype(jnp.float32)
        scale = lax.rsqrt(jnp.mean(rows * rows, axis=-1, keepdims=True) + norm_eps)
        return pick(hidden, 0, chips), scale
    step = 64
    return pl.pallas_call(
        functools.partial(own_kernel, chips=chips, width=width),
        grid=(row_count // step,),
        in_specs=[pl.BlockSpec((step, depth), lambda i: (i, 0))],
        out_specs=[
            pl.BlockSpec((step, depth // 4), lambda i: (i, 0)),
            pl.BlockSpec((step, 1), lambda i: (i, 0)),
        ],
        out_shape=[
            jax.ShapeDtypeStruct((row_count, depth // 4), jnp.bfloat16),
            jax.ShapeDtypeStruct((row_count, 1), jnp.float32),
        ],
        name="own_part",
    )(hidden)


def project_kernel(first, second, *refs, count, width, columns):
    keys = refs[:count]
    values = refs[count : 2 * count]
    first_out, second_out, rows, weight, sems = refs[2 * count :]
    _, row, column, _ = places()
    spots = chip_spots(row, column, columns)
    half = first.shape[0]
    split = weight.shape[1] // 2
    row_copies = [
        pltpu.make_async_copy(first, rows.at[pl.ds(0, half)], sems.at[2 * count]),
        pltpu.make_async_copy(second, rows.at[pl.ds(half, half)], sems.at[2 * count + 1]),
    ]
    copies = []
    for side, pieces in enumerate((keys, values)):
        for k, piece in enumerate(pieces):
            start = pl.multiple_of(spots[k] * width, width)
            copies.append(
                pltpu.make_async_copy(
                    piece,
                    weight.at[pl.ds(start, width), pl.ds(side * split, split)],
                    sems.at[side * count + k],
                )
            )
    for copy in row_copies + copies:
        copy.start()
    for copy in row_copies:
        copy.wait()
    for side in range(2):
        for copy in copies[side * count : (side + 1) * count]:
            copy.wait()
        cut = slice(side * split, (side + 1) * split)
        for out, start in ((first_out, 0), (second_out, half)):
            out[:, cut] = jnp.dot(
                rows[start : start + half], weight[:, cut], preferred_element_type=jnp.float32
            )


def project(first, second, keys, values, columns):
    width, split = keys[0].shape
    half, depth = first.shape
    count = len(keys)
    shape = jax.ShapeDtypeStruct((half, 2 * split), jnp.float32)
    return pl.pallas_call(
        functools.partial(project_kernel, count=count, width=width, columns=columns),
        in_specs=[ANY] * (2 + 2 * count),
        out_specs=[VMEM, VMEM],
        out_shape=[shape, shape],
        scratch_shapes=[
            pltpu.VMEM((2 * half, depth), jnp.bfloat16),
            pltpu.VMEM((depth, 2 * split), jnp.bfloat16),
            pltpu.SemaphoreType.DMA((2 * count + 2,)),
        ],
        name="prefix_project",
    )(first, second, *keys, *values)


def turn(values, cosine, sine):
    return values * cosine + pltpu.roll(values, HEAD // 2, 1) * sine


def expert_kernel(
    lengths,
    noise,
    input_weight,
    embed,
    expert_gain,
    final_gain,
    output_weight,
    query_cos,
    query_sin,
    action_cos,
    action_sin,
    prefix_cos,
    prefix_sin,
    row_scale,
    kept,
    paired,
    twinned,
    *refs,
    columns,
    span,
    heads,
    groups,
    proj_count,
    proj_rows,
    out_count,
    out_rows,
):
    proj_pieces = refs[:proj_count]
    out_pieces = refs[proj_count : proj_count + out_count]
    (actions, proj, mix, key_cache, value_cache, joined, state_ref, turned, sems) = refs[
        proj_count + out_count :
    ]
    core, row, column, _ = places()
    spots = chip_spots(row, column, columns)
    copies = []
    late = []
    for side in range(2):
        half = 1 - core if side else core
        for k, spot in enumerate(spots):
            piece = proj_pieces[side * len(spots) + k]
            start = pl.multiple_of((spot * 2 + half) * proj_rows, proj_rows)
            copies.append(
                pltpu.make_async_copy(
                    piece, proj.at[pl.ds(start, proj_rows)], sems.at[len(copies)]
                )
            )
        for k, spot in enumerate(spots):
            cross, slot = divmod(k, columns)
            piece = out_pieces[side * columns + slot]
            start = pl.multiple_of((spot * 2 + half) * out_rows, out_rows)
            late.append(
                pltpu.make_async_copy(
                    piece.at[pl.ds(cross * out_rows, out_rows)],
                    mix.at[pl.ds(start, out_rows)],
                    sems.at[proj_count + len(late)],
                )
            )
    for copy in copies + late:
        copy.start()
    length = lengths[0]
    kv_width = groups * HEAD
    for g in range(groups):
        cut = slice(g * HEAD, (g + 1) * HEAD)
        raw = kept[:, cut] + paired[:, cut] + twinned[:, cut].astype(jnp.float32)
        raw = raw * row_scale[...]
        key_cache[:, cut] = turn(raw, prefix_cos[...], prefix_sin[...]).astype(jnp.bfloat16)
        cut2 = slice(kv_width + g * HEAD, kv_width + (g + 1) * HEAD)
        raw = kept[:, cut2] + paired[:, cut2] + twinned[:, cut2].astype(jnp.float32)
        value_cache[:, cut] = (raw * row_scale[...]).astype(jnp.bfloat16)
    for copy in copies + late:
        copy.wait()
    ratio = heads // groups
    rows = joined.shape[0]
    query_width = heads * HEAD
    contract = (((1,), (1,)), ((), ()))
    prefix_ok = lax.broadcasted_iota(jnp.int32, (1, key_cache.shape[0]), 1) < length
    own_ok = lax.broadcasted_iota(jnp.int32, (1, rows), 1) < span
    turned[...] = jnp.zeros_like(turned)
    turned[:, :span] = noise[...]
    state_ref[...] = turned[...].T

    def step(k, carry):
        state = state_ref[...]
        hidden = jnp.dot(
            state,
            input_weight[...],
            precision=lax.Precision.HIGHEST,
            preferred_element_type=jnp.float32,
        )
        hidden = hidden + embed[pl.ds(k, 1), :]
        square = jnp.mean(hidden * hidden, axis=-1, keepdims=True)
        normed = (hidden * lax.rsqrt(square + norm_eps) * expert_gain[...]).astype(jnp.bfloat16)
        raw = jnp.dot(normed, proj[...], preferred_element_type=jnp.float32)
        for g in range(groups):
            cut = slice(g * HEAD, (g + 1) * HEAD)
            own_keys = turn(
                raw[:, query_width + g * HEAD : query_width + (g + 1) * HEAD],
                action_cos[...],
                action_sin[...],
            ).astype(jnp.bfloat16)
            base = query_width + kv_width
            own_values = raw[:, base + g * HEAD : base + (g + 1) * HEAD].astype(jnp.bfloat16)
            queries = jnp.concatenate(
                [
                    turn(
                        raw[:, (g * ratio + r) * HEAD : (g * ratio + r + 1) * HEAD],
                        query_cos[...],
                        query_sin[...],
                    ).astype(jnp.bfloat16)
                    for r in range(ratio)
                ],
                0,
            )
            far = lax.dot_general(
                queries, key_cache[:, cut], contract, preferred_element_type=jnp.float32
            )
            near = lax.dot_general(queries, own_keys, contract, preferred_element_type=jnp.float32)
            far = jnp.where(prefix_ok, far, -1e30)
            near = jnp.where(own_ok, near, -1e30)
            row_max = jnp.maximum(
                jnp.max(far, -1, keepdims=True), jnp.max(near, -1, keepdims=True)
            )
            far = jnp.exp(far - row_max)
            near = jnp.exp(near - row_max)
            total = jnp.sum(far, -1, keepdims=True) + jnp.sum(near, -1, keepdims=True)
            inverse = 1.0 / total
            far = (far * inverse).astype(jnp.bfloat16)
            near = (near * inverse).astype(jnp.bfloat16)
            mixed = jnp.dot(far, value_cache[:, cut], preferred_element_type=jnp.float32)
            mixed = mixed + jnp.dot(near, own_values, preferred_element_type=jnp.float32)
            mixed = mixed.astype(jnp.bfloat16)
            for r in range(ratio):
                h = g * ratio + r
                joined[:, h * HEAD : (h + 1) * HEAD] = mixed[r * rows : (r + 1) * rows]
        hidden = hidden + jnp.dot(joined[...], mix[...], preferred_element_type=jnp.float32)
        square = jnp.mean(hidden * hidden, axis=-1, keepdims=True)
        normed = (hidden * lax.rsqrt(square + norm_eps) * final_gain[...]).astype(jnp.bfloat16)
        velocity = lax.dot_general(
            normed, output_weight[...], contract, preferred_element_type=jnp.float32
        )
        state_ref[...] = state - velocity / STEPS
        return carry

    lax.fori_loop(0, STEPS, step, 0)
    turned[...] = state_ref[...].T
    actions[...] = turned[:, :span]


def expert(lengths, dense, proj_pieces, out_pieces, columns, span, groups):
    proj_rows, proj_width = proj_pieces[0].shape
    out_rows = out_pieces[0].shape[0] // 2
    noise = dense[0]
    rows = dense[6].shape[0]
    prefix = dense[12].shape[0]
    proj_depth = proj_rows * len(proj_pieces)
    out_depth = out_rows * 2 * len(out_pieces)
    out_width = out_pieces[0].shape[1]
    heads = out_depth // HEAD
    return pl.pallas_call(
        functools.partial(
            expert_kernel,
            columns=columns,
            span=span,
            heads=heads,
            groups=groups,
            proj_count=len(proj_pieces),
            proj_rows=proj_rows,
            out_count=len(out_pieces),
            out_rows=out_rows,
        ),
        in_specs=[SMEM] + [VMEM] * len(dense) + [ANY] * (len(proj_pieces) + len(out_pieces)),
        out_specs=VMEM,
        out_shape=jax.ShapeDtypeStruct(noise.shape, jnp.float32),
        scratch_shapes=[
            pltpu.VMEM((proj_depth, proj_width), jnp.bfloat16),
            pltpu.VMEM((out_depth, out_width), jnp.bfloat16),
            pltpu.VMEM((prefix, groups * HEAD), jnp.bfloat16),
            pltpu.VMEM((prefix, groups * HEAD), jnp.bfloat16),
            pltpu.VMEM((rows, heads * HEAD), jnp.bfloat16),
            pltpu.VMEM((rows, noise.shape[0]), jnp.float32),
            pltpu.VMEM((noise.shape[0], rows), jnp.float32),
            pltpu.SemaphoreType.DMA((len(proj_pieces) + 2 * len(out_pieces),)),
        ],
        name="expert_steps",
    )(lengths, *dense, *proj_pieces, *out_pieces)


def shards(
    prefix_hidden,
    prefix_lengths,
    action_noise,
    prefix_gain,
    key_weight,
    value_weight,
    input_weight,
    expert_gain,
    expert_query,
    expert_key,
    expert_value,
    expert_output,
    final_gain,
    output_weight,
    *,
    group_count,
    wide_count,
):
    chips = wide_count // 2
    columns = chips // 2
    _, _, _, twin = places()
    ring = [(w, (w + 4) % wide_count) for w in range(wide_count)]
    across = [(w, w ^ 2) for w in range(wide_count)]
    beside = [(w, w ^ 1) for w in range(wide_count)]
    facing = [(g, g ^ 1) for g in range(group_count)]
    corner = [
        (g * wide_count + w, (g ^ 1) * wide_count + (w ^ 1))
        for g in range(group_count)
        for w in range(wide_count)
    ]

    def round_ring(piece):
        slots = [piece]
        for _ in range(1, columns):
            slots.append(lax.ppermute(slots[-1], "wide", ring))
        return slots

    def over(slots):
        return [lax.ppermute(slot, "wide", across) for slot in slots]

    def swap(pieces):
        return [lax.ppermute(piece, "wide", beside) for piece in pieces]

    hidden = prefix_hidden[0]
    to_corner = pick(hidden, 3, chips)
    from_corner = lax.ppermute(to_corner, ("groups", "wide"), corner)
    to_twin = pick(hidden, 1, chips)
    from_twin = lax.ppermute(to_twin, "groups", facing)
    to_core = pick(hidden, 2, chips)
    from_core = lax.ppermute(to_core, "wide", beside)
    kept, row_scale = own_part_and_scale(hidden, chips)

    half = key_weight.shape[0] // 2
    place = lax.axis_index("wide")
    gain = lax.dynamic_slice_in_dim(prefix_gain, (place * 2 + twin) * half, half, 0)

    def scaled(weight):
        part = lax.dynamic_slice_in_dim(weight, twin * half, half, 0)
        return (part.astype(jnp.float32) * gain[:, None]).astype(jnp.bfloat16)

    key_slots = round_ring(scaled(key_weight))
    value_slots = round_ring(scaled(value_weight))
    key_pieces = key_slots + over(key_slots)
    value_pieces = value_slots + over(value_slots)

    proj_own = jnp.concatenate([expert_query, expert_key, expert_value], 1)
    length = prefix_lengths[0]
    span = action_noise.shape[1]
    rows = -(-span // 16) * 16
    embed = jnp.stack(
        [time_embedding(1.0 - k / STEPS, input_weight.shape[1]) for k in range(STEPS)]
    )
    positions = length.astype(jnp.float32) + jnp.arange(rows, dtype=jnp.float32)
    tables = (
        embed,
        *rope_tables(positions, HEAD ** (-0.5)),
        *rope_tables(positions),
        *rope_tables(jnp.arange(hidden.shape[0], dtype=jnp.float32)),
    )
    kept, tables = lax.optimization_barrier((kept, tables))

    proj_slots = round_ring(proj_own)
    proj_pieces = proj_slots + over(proj_slots)
    proj_pieces = proj_pieces + swap(proj_pieces)
    out_own = jnp.concatenate([expert_output] + over([expert_output]), 0)
    out_pieces = round_ring(out_own)
    out_pieces = out_pieces + swap(out_pieces)

    corner_part, twin_part = project(
        from_corner, from_twin, key_pieces, value_pieces, columns
    )
    core_part, own_part = project(from_core, kept, key_pieces, value_pieces, columns)
    corner_paired = lax.ppermute(corner_part, "wide", beside)
    twin_sum = (twin_part + corner_paired).astype(jnp.bfloat16)
    twinned = lax.ppermute(twin_sum, "groups", facing)
    own_paired = lax.ppermute(core_part, "wide", beside)

    dense = (
        action_noise[0].T,
        input_weight,
        tables[0],
        expert_gain[None, :],
        final_gain[None, :],
        output_weight.T,
        *tables[1:],
        row_scale,
        own_part,
        own_paired,
        twinned,
    )
    groups = key_weight.shape[1] // HEAD
    actions = expert(
        prefix_lengths, dense, proj_pieces, out_pieces, columns, span, groups
    )
    return actions.T[None]


def solution(mesh):
    placed = (
        P(("groups", "wide"), None, None),
        P(("groups", "wide")),
        P(("groups", "wide"), None, None),
        P(),
        P("wide", None),
        P("wide", None),
        P(),
        P(),
        P("wide", None),
        P("wide", None),
        P("wide", None),
        P("wide", None),
        P(),
        P(),
    )

    def whole(*arrays):
        return shards(
            *arrays, group_count=mesh.shape["groups"], wide_count=mesh.shape["wide"]
        )

    return jax.shard_map(
        whole,
        mesh=mesh,
        in_specs=placed,
        out_specs=P(("groups", "wide"), None, None),
        check_vma=False,
    )
```

time: 180 us -> 163 us (0.906)
  waiting for transfers between devices: 95 us -> 68.5 us
  starting transfers between devices: 22.2 us -> 31.6 us
  Pallas kernels: 39.6 us -> 43.1 us
  local copies, waits for them, and re-layouts: 10.5 us -> 8.41 us
    ppermute x9 -> x12, waiting for transfers between devices: 49.6 us -> 28.7 us  [round_ring(): slots.append(lax.ppermute(slots[-1], 'wide', ring))]
    ppermute x1, waiting for transfers between devices: 15.5 us -> 7.25 us  [shards(): from_twin = lax.ppermute(to_twin, 'groups', facing)]
    ppermute x1, waiting for transfers between devices: 4.1 us -> 10.9 us  [shards(): twinned = lax.ppermute(twin_sum, 'groups', facing)]
    ppermute x9 -> x12, starting transfers between devices: 6.35 us -> 12.6 us  [round_ring(): slots.append(lax.ppermute(slots[-1], 'wide', ring))]
    ppermute x24 -> x28, starting transfers between devices: 12.5 us -> 17.4 us  [the longest x13 15.3 us: over(): return [lax.ppermute(slot, 'wide', across) for slot in slots]]
    ppermute x24 -> x28, waiting for transfers between devices: 25.7 us -> 21.7 us  [the longest x13 19.8 us: over(): return [lax.ppermute(slot, 'wide', across) for slot in slots]]
    pallas_call x4 -> x7, Pallas kernels: 39.6 us -> 43.1 us  [the longest x1 20 us: expert(): pl.pallas_call(functools.partial(expert_kernel, columns=columns, span=spa...]
    ppermute x1, starting transfers between devices: 1.8 us -> 0.01 us  [shards(): twinned = lax.ppermute(twin_sum, 'groups', facing)]
  transfers between devices with their start and end apart: 36 -> 43, of which waited for: 12 -> 18; matrix products, arithmetic and copies ran while one was open for 9% -> 8% of each run, Pallas kernels for 11% -> 14%
where the time goes in v2:
time: 163 us
  waiting for transfers between devices  68.5 us (42%)
  Pallas kernels  43.1 us (26%)
  starting transfers between devices  31.6 us (19%)
  other arithmetic  9.69 us (6%)
  local copies, waits for them, and re-layouts  8.41 us (5%)
    ppermute x12, waiting for transfers between devices, round_ring(): slots.append(lax.ppermute(slots[-1], 'wide', ring))  28.7 us
    pallas_call x1, Pallas kernels, expert(): pl.pallas_call(functools.partial(expert_kernel, columns=columns, span=spa...  20 us
    ppermute x13, waiting for transfers between devices, over(): return [lax.ppermute(slot, 'wide', across) for slot in slots]  19.8 us
    ppermute x13, starting transfers between devices, over(): return [lax.ppermute(slot, 'wide', across) for slot in slots]  15.3 us
    ppermute x12, starting transfers between devices, round_ring(): slots.append(lax.ppermute(slots[-1], 'wide', ring))  12.6 us
    pallas_call x2, Pallas kernels, project(): pl.pallas_call(functools.partial(project_kernel, count=count, width=width...  11.6 us
    ppermute x1, waiting for transfers between devices, shards(): twinned = lax.ppermute(twin_sum, 'groups', facing)  10.9 us
    ppermute x1, waiting for transfers between devices, shards(): from_twin = lax.ppermute(to_twin, 'groups', facing)  7.25 us
  transfers between devices with their start and end apart: 43, of which 18 were waited for; matrix products, arithmetic and copies ran while one was open for 8% of the time, Pallas kernels for 14%

profile of v2, /device:TPU:0, one launch (start us, length us, event | category | flops | bytes accessed | tf_op | source)
XLA Modules:
  0.0 162.7 jit_solution(15042083855214095953)
XLA Ops:
  2.0 3.1 %collective-permute-start.8 = (bf16[256,512]{1,0:T(8,128)(2,1)S(1)}, bf16[256,512]{1,0:T(8,128)(2,1)S(1)}, u32[]{:S(2)}, u32[]{:S(2)}) collective-permute-start(bf16[256,512]{1,0:T(8,128)(2,1)S(1)} %get-tuple-element.33.refs_8_), channel_id=1, source_target_pairs={{0,4},{1,5},{2,6},{3,7},{4,8},{5,9},{6,10},{7,11},{8,12},{9,13},{1... | collective-permute-start | bytes 786440 | tf_op jit(solution)/shard_map/ppermute | solution.py:413
  12.8 8.5 %collective-permute-done.35 = bf16[64,1024]{1,0:T(8,128)(2,1)S(1)} collective-permute-done((bf16[64,1024]{1,0:T(8,128)(2,1)}, bf16[64,1024]{1,0:T(8,128)(2,1)S(1)}, u32[]{:S(2)}, u32[]{:S(2)}) %collective-permute-start.35) | collective-permute-done | bytes 131104 | tf_op jit(solution)/shard_map/ppermute | solution.py:417
  24.4 1.6 collective-permute-start.9
  26.0 2.3 %pick_columns.4 = bf16[256,2048]{1,0:T(8,128)(2,1)} custom-call(bf16[256,8192]{1,0:T(8,128)(2,1)} %bitcast.15), custom_call_target="tpu_custom_call" | custom-call | tf_op jit(solution)/shard_map/pick_columns/pallas_call | solution.py:86
  29.0 3.4 %collective-permute-done.20.refs_1_ = bf16[64,2048]{1,0:T(8,128)(2,1)} collective-permute-done((bf16[64,2048]{1,0:T(8,128)(2,1)S(1)}, bf16[64,2048]{1,0:T(8,128)(2,1)}, u32[]{:S(2)}, u32[]{:S(2)}) %collective-permute-start.20) | collective-permute-done | bytes 262176 | tf_op jit(solution)/shard_map/ppermute | solution.py:413
  32.4 2.4 %pick_columns.5 = bf16[256,2048]{1,0:T(8,128)(2,1)} custom-call(bf16[256,8192]{1,0:T(8,128)(2,1)} %bitcast.16), custom_call_target="tpu_custom_call" | custom-call | tf_op jit(solution)/shard_map/pick_columns/pallas_call | solution.py:86
  37.0 1.6 collective-permute-start.5
  43.6 2.2 %collective-permute-start.13 = (bf16[256,512]{1,0:T(8,128)(2,1)S(1)}, bf16[256,512]{1,0:T(8,128)(2,1)S(1)}, u32[]{:S(2)}, u32[]{:S(2)}) collective-permute-start(bf16[256,512]{1,0:T(8,128)(2,1)S(1)} %collective-permute-done.9.refs_10_), channel_id=1, source_target_pairs={{0,2},{1,3},{2,0},{3,1},{4,6},{5,7},{6,4},{7,5},{8,10},{9,11},{10,... | collective-permute-start | bytes 786440 | tf_op jit(solution)/shard_map/ppermute | solution.py:417
  46.6 5.4 %collective-permute-done.10.refs_11_ = bf16[256,512]{1,0:T(8,128)(2,1)S(1)} collective-permute-done((bf16[256,512]{1,0:T(8,128)(2,1)S(1)}, bf16[256,512]{1,0:T(8,128)(2,1)S(1)}, u32[]{:S(2)}, u32[]{:S(2)}) %collective-permute-start.10) | collective-permute-done | bytes 262176 | tf_op jit(solution)/shard_map/ppermute | solution.py:413
  57.6 2.3 %pick_columns.3 = bf16[256,2048]{1,0:T(8,128)(2,1)} custom-call(bf16[256,8192]{1,0:T(8,128)(2,1)} %bitcast.17), custom_call_target="tpu_custom_call" | custom-call | tf_op jit(solution)/shard_map/pick_columns/pallas_call | solution.py:86
  61.2 4.6 %collective-permute-done.14.refs_15_ = bf16[256,512]{1,0:T(8,128)(2,1)S(1)} collective-permute-done((bf16[256,512]{1,0:T(8,128)(2,1)S(1)}, bf16[256,512]{1,0:T(8,128)(2,1)S(1)}, u32[]{:S(2)}, u32[]{:S(2)}) %collective-permute-start.14) | collective-permute-done | bytes 262176 | tf_op jit(solution)/shard_map/ppermute | solution.py:417
  66.8 1.8 %collective-permute-done.7.refs_7_ = bf16[256,512]{1,0:T(8,128)(2,1)S(1)} collective-permute-done((bf16[256,512]{1,0:T(8,128)(2,1)S(1)}, bf16[256,512]{1,0:T(8,128)(2,1)S(1)}, u32[]{:S(2)}, u32[]{:S(2)}) %collective-permute-start.7) | collective-permute-done | bytes 262176 | tf_op jit(solution)/shard_map/ppermute | solution.py:417
  69.4 7.3 %collective-permute-done.17.second = bf16[256,2048]{1,0:T(8,128)(2,1)} collective-permute-done((bf16[256,2048]{1,0:T(8,128)(2,1)}, bf16[256,2048]{1,0:T(8,128)(2,1)}, u32[]{:S(2)}, u32[]{:S(2)}) %collective-permute-start.17) | collective-permute-done | bytes 1048608 | tf_op jit(solution)/shard_map/ppermute | solution.py:426
  77.1 5.8 %prefix_project.3 = (f32[256,1024]{1,0:T(8,128)}, f32[256,1024]{1,0:T(8,128)}) custom-call(bf16[256,2048]{1,0:T(8,128)(2,1)} %collective-permute-done.16.first, bf16[256,2048]{1,0:T(8,128)(2,1)} %collective-permute-done.17.second, bf16[256,512]{1,0:T(8,128)(2,1)} %copy-done.1, bf16[256,512]{1,0:T(8,128)(2,1)} %copy-done.4, bf16[256,512]{1,0:T(8,128)(2,1)} %copy-done.8, ...), custom_call_target="tpu_custom_call" | custom-call | tf_op jit(solution)/shard_map/prefix_project/pallas_call | solution.py:172
  84.5 2.5 %collective-permute-done.21.refs_2_ = bf16[64,2048]{1,0:T(8,128)(2,1)} collective-permute-done((bf16[64,2048]{1,0:T(8,128)(2,1)}, bf16[64,2048]{1,0:T(8,128)(2,1)}, u32[]{:S(2)}, u32[]{:S(2)}) %collective-permute-start.21) | collective-permute-done | bytes 262176 | tf_op jit(solution)/shard_map/ppermute | solution.py:413
  89.2 3.6 %collective-permute-done.24.refs_5_ = bf16[64,2048]{1,0:T(8,128)(2,1)} collective-permute-done((bf16[64,2048]{1,0:T(8,128)(2,1)}, bf16[64,2048]{1,0:T(8,128)(2,1)}, u32[]{:S(2)}, u32[]{:S(2)}) %collective-permute-start.24) | collective-permute-done | bytes 262176 | tf_op jit(solution)/shard_map/ppermute | solution.py:417
  94.3 1.6 %collective-permute-start.22 = (bf16[64,2048]{1,0:T(8,128)(2,1)}, bf16[64,2048]{1,0:T(8,128)(2,1)S(1)}, u32[]{:S(2)}, u32[]{:S(2)}) collective-permute-start(bf16[64,2048]{1,0:T(8,128)(2,1)} %collective-permute-done.21.refs_2_), channel_id=1, source_target_pairs={{0,4},{1,5},{2,6},{3,7},{4,8},{5,9},{6,10},{7,11},{8,12},{9,13},{1... | collective-permute-start | bytes 786440 | tf_op jit(solution)/shard_map/ppermute | solution.py:413
  96.0 1.9 %pad_maximum_fusion = (f32[256,128]{1,0:T(8,128)}, f32[256,128]{1,0:T(8,128)}) fusion(f32[256,64]{1,0:T(8,128)} %get-tuple-element.43, f32[256,64]{1,0:T(8,128)} %get-tuple-element.42, f32[256,64]{1,0:T(8,128)S(1)} %get-tuple-element.41), kind=kLoop, calls=%fused_computation.3 | loop fusion | flops 65536 | bytes 458752 | tf_op jit(solution)/shard_map/concatenate | solution.py:30
  97.9 6.2 %collective-permute-done.37.refs_18_ = bf16[128,1024]{1,0:T(8,128)(2,1)S(1)} collective-permute-done((bf16[128,1024]{1,0:T(8,128)(2,1)}, bf16[128,1024]{1,0:T(8,128)(2,1)S(1)}, u32[]{:S(2)}, u32[]{:S(2)}) %collective-permute-start.37) | collective-permute-done | bytes 262176 | tf_op jit(solution)/shard_map/ppermute | solution.py:413
  106.6 4.4 %own_part.1 = (bf16[256,2048]{1,0:T(8,128)(2,1)}, f32[256,1]{1,0:T(8,128)}) custom-call(bf16[256,8192]{1,0:T(8,128)(2,1)} %bitcast.18), custom_call_target="tpu_custom_call" | custom-call | tf_op jit(solution)/shard_map/own_part/pallas_call | solution.py:114
  111.0 5.8 %prefix_project.2 = (f32[256,1024]{1,0:T(8,128)}, f32[256,1024]{1,0:T(8,128)}) custom-call(bf16[256,2048]{1,0:T(8,128)(2,1)} %collective-permute-done.first, bf16[256,2048]{1,0:T(8,128)(2,1)} %get-tuple-element.28.second, bf16[256,512]{1,0:T(8,128)(2,1)} %copy-done.1, bf16[256,512]{1,0:T(8,128)(2,1)} %copy-done.4, bf16[256,512]{1,0:T(8,128)(2,1)} %copy-done.8, ...), custom_call_target="tpu_custom_call" | custom-call | tf_op jit(solution)/shard_map/prefix_project/pallas_call | solution.py:172
  119.7 8.6 %collective-permute-done.38.refs_19_ = bf16[128,1024]{1,0:T(8,128)(2,1)S(1)} collective-permute-done((bf16[128,1024]{1,0:T(8,128)(2,1)}, bf16[128,1024]{1,0:T(8,128)(2,1)S(1)}, u32[]{:S(2)}, u32[]{:S(2)}) %collective-permute-start.38) | collective-permute-done | bytes 262176 | tf_op jit(solution)/shard_map/ppermute | solution.py:413
  130.9 10.9 %collective-permute-done.19.twinned = bf16[256,1024]{1,0:T(8,128)(2,1)S(1)} collective-permute-done((bf16[256,1024]{1,0:T(8,128)(2,1)S(1)}, bf16[256,1024]{1,0:T(8,128)(2,1)S(1)}, u32[]{:S(2)}, u32[]{:S(2)}) %collective-permute-start.19) | collective-permute-done | bytes 524320 | tf_op jit(solution)/shard_map/ppermute | solution.py:473
  142.6 20.0 %expert_steps.1 = f32[32,50]{1,0:T(8,128)} custom-call(s32[1]{0:T(128)S(6)} %copy.18.lengths, f32[32,50]{1,0:T(8,128)} %bitcast.20, f32[32,1024]{1,0:T(8,128)} %input_weight.1, f32[4,1024]{1,0:T(4,128)} %pad_maximum_fusion.6.embed, f32[1,1024]{1,0:T(1,128)} %bitcast.25, f32[1,1024]{1,0:T(1,128)} %bitcast.26, bf16[32,1024]{1,0:T(8,128)(2,1)} %bitcast.19, ...), custom_call_target="tpu_custom_call" | custom-call | tf_op jit(solution)/shard_map/expert_steps/pallas_call | solution.py:349
  (165 shorter events, 43.7 us)
Async XLA Ops:
  2.0 20.9 %collective-permute-start.8 = (bf16[256,512]{1,0:T(8,128)(2,1)S(1)}, bf16[256,512]{1,0:T(8,128)(2,1)S(1)}, u32[]{:S(2)}, u32[]{:S(2)}) collective-permute-start(bf16[256,512]{1,0:T(8,128)(2,1)S(1)} %get-tuple-element.33.refs_8_), channel_id=1, source_target_pairs={{0,4},{1,5},{2,6},{3,7},{4,8},{5,9},{6,10},{7,11},{8,12},{9,13},{1... | collective-permute-start | bytes 786440 | tf_op jit(solution)/shard_map/ppermute | solution.py:413
  5.1 23.2 %collective-permute-start.11 = (bf16[256,512]{1,0:T(8,128)(2,1)S(1)}, bf16[256,512]{1,0:T(8,128)(2,1)S(1)}, u32[]{:S(2)}, u32[]{:S(2)}) collective-permute-start(bf16[256,512]{1,0:T(8,128)(2,1)S(1)} %get-tuple-element.33.refs_8_), channel_id=1, source_target_pairs={{0,2},{1,3},{2,0},{3,1},{4,6},{5,7},{6,4},{7,5},{8,10},{9,11},{10,... | collective-permute-start | bytes 786440 | tf_op jit(solution)/shard_map/ppermute | solution.py:417
  6.6 17.8 %collective-permute-start.1 = (bf16[256,512]{1,0:T(8,128)(2,1)S(1)}, bf16[256,512]{1,0:T(8,128)(2,1)S(1)}, u32[]{:S(2)}, u32[]{:S(2)}) collective-permute-start(bf16[256,512]{1,0:T(8,128)(2,1)S(1)} %get-tuple-element.34.refs_0_), channel_id=1, source_target_pairs={{0,4},{1,5},{2,6},{3,7},{4,8},{5,9},{6,10},{7,11},{8,12},{9,13},{1... | collective-permute-start | bytes 786440 | tf_op jit(solution)/shard_map/ppermute | solution.py:413
  8.2 20.2 %collective-permute-start.4 = (bf16[256,512]{1,0:T(8,128)(2,1)S(1)}, bf16[256,512]{1,0:T(8,128)(2,1)S(1)}, u32[]{:S(2)}, u32[]{:S(2)}) collective-permute-start(bf16[256,512]{1,0:T(8,128)(2,1)S(1)} %get-tuple-element.34.refs_0_), channel_id=1, source_target_pairs={{0,2},{1,3},{2,0},{3,1},{4,6},{5,7},{6,4},{7,5},{8,10},{9,11},{10,... | collective-permute-start | bytes 786440 | tf_op jit(solution)/shard_map/ppermute | solution.py:417
  8.7 12.6 %collective-permute-start.35 = (bf16[64,1024]{1,0:T(8,128)(2,1)}, bf16[64,1024]{1,0:T(8,128)(2,1)S(1)}, u32[]{:S(2)}, u32[]{:S(2)}) collective-permute-start(bf16[64,1024]{1,0:T(8,128)(2,1)} %param.25), channel_id=1, source_target_pairs={{0,2},{1,3},{2,0},{3,1},{4,6},{5,7},{6,4},{7,5},{8,10},{9,11},{10,... | collective-permute-start | bytes 393224 | tf_op jit(solution)/shard_map/ppermute | solution.py:417
  22.8 12.6 %collective-permute-start.23 = (bf16[64,2048]{1,0:T(8,128)(2,1)S(1)}, bf16[64,2048]{1,0:T(8,128)(2,1)S(1)}, u32[]{:S(2)}, u32[]{:S(2)}) collective-permute-start(bf16[64,2048]{1,0:T(8,128)(2,1)S(1)} %constant_dynamic-update-slice_fusion.refs_0_), channel_id=1, source_target_pairs={{0,2},{1,3},{2,0},{3,1},{4,6},{5,7},{6,4},{7,5},{8,10},{9,11},{10,... | collective-permute-start | bytes 786440 | tf_op jit(solution)/shard_map/ppermute | solution.py:417
  24.4 12.6 %collective-permute-start.9 = (bf16[256,512]{1,0:T(8,128)(2,1)S(1)}, bf16[256,512]{1,0:T(8,128)(2,1)S(1)}, u32[]{:S(2)}, u32[]{:S(2)}) collective-permute-start(bf16[256,512]{1,0:T(8,128)(2,1)S(1)} %collective-permute-done.8.refs_9_), channel_id=1, source_target_pairs={{0,4},{1,5},{2,6},{3,7},{4,8},{5,9},{6,10},{7,11},{8,12},{9,13},{1... | collective-permute-start | bytes 786440 | tf_op jit(solution)/shard_map/ppermute | solution.py:413
  28.3 40.3 %collective-permute-start.16 = (bf16[256,2048]{1,0:T(8,128)(2,1)}, bf16[256,2048]{1,0:T(8,128)(2,1)}, u32[]{:S(2)}, u32[]{:S(2)}) collective-permute-start(bf16[256,2048]{1,0:T(8,128)(2,1)} %pick_columns.4), channel_id=1, source_target_pairs={{0,17},{1,16},{2,19},{3,18},{4,21},{5,20},{6,23},{7,22},{8,25},{9,... | collective-permute-start | bytes 3145736 | tf_op jit(solution)/shard_map/ppermute | solution.py:424
  28.4 12.8 %collective-permute-start.12 = (bf16[256,512]{1,0:T(8,128)(2,1)S(1)}, bf16[256,512]{1,0:T(8,128)(2,1)S(1)}, u32[]{:S(2)}, u32[]{:S(2)}) collective-permute-start(bf16[256,512]{1,0:T(8,128)(2,1)S(1)} %collective-permute-done.8.refs_9_), channel_id=1, source_target_pairs={{0,2},{1,3},{2,0},{3,1},{4,6},{5,7},{6,4},{7,5},{8,10},{9,11},{10,... | collective-permute-start | bytes 786440 | tf_op jit(solution)/shard_map/ppermute | solution.py:417
  35.5 41.2 %collective-permute-start.17 = (bf16[256,2048]{1,0:T(8,128)(2,1)}, bf16[256,2048]{1,0:T(8,128)(2,1)}, u32[]{:S(2)}, u32[]{:S(2)}) collective-permute-start(bf16[256,2048]{1,0:T(8,128)(2,1)} %pick_columns.5), channel_id=1, source_target_pairs={{0,16},{16,0},{1,17},{17,1},{2,18},{18,2},{3,19},{19,3},{4,20},{20... | collective-permute-start | bytes 3145736 | tf_op jit(solution)/shard_map/ppermute | solution.py:426
  41.2 13.6 %collective-permute-start.3 = (bf16[256,512]{1,0:T(8,128)(2,1)S(1)}, bf16[256,512]{1,0:T(8,128)(2,1)S(1)}, u32[]{:S(2)}, u32[]{:S(2)}) collective-permute-start(bf16[256,512]{1,0:T(8,128)(2,1)S(1)} %collective-permute-done.2.refs_2_), channel_id=1, source_target_pairs={{0,4},{1,5},{2,6},{3,7},{4,8},{5,9},{6,10},{7,11},{8,12},{9,13},{1... | collective-permute-start | bytes 786440 | tf_op jit(solution)/shard_map/ppermute | solution.py:413
  43.6 13.4 %collective-permute-start.13 = (bf16[256,512]{1,0:T(8,128)(2,1)S(1)}, bf16[256,512]{1,0:T(8,128)(2,1)S(1)}, u32[]{:S(2)}, u32[]{:S(2)}) collective-permute-start(bf16[256,512]{1,0:T(8,128)(2,1)S(1)} %collective-permute-done.9.refs_10_), channel_id=1, source_target_pairs={{0,2},{1,3},{2,0},{3,1},{4,6},{5,7},{6,4},{7,5},{8,10},{9,11},{10,... | collective-permute-start | bytes 786440 | tf_op jit(solution)/shard_map/ppermute | solution.py:417
  57.1 11.5 %collective-permute-start.7 = (bf16[256,512]{1,0:T(8,128)(2,1)S(1)}, bf16[256,512]{1,0:T(8,128)(2,1)S(1)}, u32[]{:S(2)}, u32[]{:S(2)}) collective-permute-start(bf16[256,512]{1,0:T(8,128)(2,1)S(1)} %collective-permute-done.3.refs_3_), channel_id=1, source_target_pairs={{0,2},{1,3},{2,0},{3,1},{4,6},{5,7},{6,4},{7,5},{8,10},{9,11},{10,... | collective-permute-start | bytes 786440 | tf_op jit(solution)/shard_map/ppermute | solution.py:417
  61.2 21.7 %collective-permute-start.27 = (bf16[64,2048]{1,0:T(8,128)(2,1)}, bf16[64,2048]{1,0:T(8,128)(2,1)S(1)}, u32[]{:S(2)}, u32[]{:S(2)}) collective-permute-start(bf16[64,2048]{1,0:T(8,128)(2,1)} %copy-done.19), channel_id=1, source_target_pairs={{0,1},{1,0},{2,3},{3,2},{4,5},{5,4},{6,7},{7,6},{8,9},{9,8},{10,11... | collective-permute-start | bytes 786440 | tf_op jit(solution)/shard_map/ppermute | solution.py:420
  65.8 39.6 %collective-permute-start = (bf16[256,2048]{1,0:T(8,128)(2,1)}, bf16[256,2048]{1,0:T(8,128)(2,1)}, u32[]{:S(2)}, u32[]{:S(2)}) collective-permute-start(bf16[256,2048]{1,0:T(8,128)(2,1)} %pick_columns.3), channel_id=1, source_target_pairs={{0,1},{1,0},{2,3},{3,2},{4,5},{5,4},{6,7},{7,6},{8,9},{9,8},{10,11... | collective-permute-start | bytes 3145736 | tf_op jit(solution)/shard_map/ppermute | solution.py:428
  68.6 15.1 %collective-permute-start.36 = (bf16[128,1024]{1,0:T(8,128)(2,1)S(1)}, bf16[128,1024]{1,0:T(8,128)(2,1)}, u32[]{:S(2)}, u32[]{:S(2)}) collective-permute-start(bf16[128,1024]{1,0:T(8,128)(2,1)S(1)} %constant_dynamic-update-slice_fusion.3.refs_16_), channel_id=1, source_target_pairs={{0,4},{1,5},{2,6},{3,7},{4,8},{5,9},{6,10},{7,11},{8,12},{9,13},{1... | collective-permute-start | bytes 786440 | tf_op jit(solution)/shard_map/ppermute | solution.py:413
  68.6 15.7 %collective-permute-start.39 = (bf16[128,1024]{1,0:T(8,128)(2,1)S(1)}, bf16[128,1024]{1,0:T(8,128)(2,1)}, u32[]{:S(2)}, u32[]{:S(2)}) collective-permute-start(bf16[128,1024]{1,0:T(8,128)(2,1)S(1)} %constant_dynamic-update-slice_fusion.3.refs_16_), channel_id=1, source_target_pairs={{0,1},{1,0},{2,3},{3,2},{4,5},{5,4},{6,7},{7,6},{8,9},{9,8},{10,11... | collective-permute-start | bytes 786440 | tf_op jit(solution)/shard_map/ppermute | solution.py:420
  83.7 35.8 %collective-permute-start.18 = (f32[256,1024]{1,0:T(8,128)}, f32[256,1024]{1,0:T(8,128)S(1)}, u32[]{:S(2)}, u32[]{:S(2)}) collective-permute-start(f32[256,1024]{1,0:T(8,128)} %get-tuple-element.32), channel_id=1, source_target_pairs={{0,1},{1,0},{2,3},{3,2},{4,5},{5,4},{6,7},{7,6},{8,9},{9,8},{10,11... | collective-permute-start | bytes 3145736 | tf_op jit(solution)/shard_map/ppermute | solution.py:471
  94.3 22.5 %collective-permute-start.22 = (bf16[64,2048]{1,0:T(8,128)(2,1)}, bf16[64,2048]{1,0:T(8,128)(2,1)S(1)}, u32[]{:S(2)}, u32[]{:S(2)}) collective-permute-start(bf16[64,2048]{1,0:T(8,128)(2,1)} %collective-permute-done.21.refs_2_), channel_id=1, source_target_pairs={{0,4},{1,5},{2,6},{3,7},{4,8},{5,9},{6,10},{7,11},{8,12},{9,13},{1... | collective-permute-start | bytes 786440 | tf_op jit(solution)/shard_map/ppermute | solution.py:413
  104.0 13.5 %collective-permute-start.25 = (bf16[64,2048]{1,0:T(8,128)(2,1)}, bf16[64,2048]{1,0:T(8,128)(2,1)}, u32[]{:S(2)}, u32[]{:S(2)}) collective-permute-start(bf16[64,2048]{1,0:T(8,128)(2,1)} %collective-permute-done.21.refs_2_), channel_id=1, source_target_pairs={{0,2},{1,3},{2,0},{3,1},{4,6},{5,7},{6,4},{7,5},{8,10},{9,11},{10,... | collective-permute-start | bytes 786440 | tf_op jit(solution)/shard_map/ppermute | solution.py:417
  105.4 12.1 %collective-permute-start.29 = (bf16[64,2048]{1,0:T(8,128)(2,1)}, bf16[64,2048]{1,0:T(8,128)(2,1)}, u32[]{:S(2)}, u32[]{:S(2)}) collective-permute-start(bf16[64,2048]{1,0:T(8,128)(2,1)} %collective-permute-done.21.refs_2_), channel_id=1, source_target_pairs={{0,1},{1,0},{2,3},{3,2},{4,5},{5,4},{6,7},{7,6},{8,9},{9,8},{10,11... | collective-permute-start | bytes 786440 | tf_op jit(solution)/shard_map/ppermute | solution.py:420
  105.4 12.7 %collective-permute-start.32 = (bf16[64,2048]{1,0:T(8,128)(2,1)}, bf16[64,2048]{1,0:T(8,128)(2,1)}, u32[]{:S(2)}, u32[]{:S(2)}) collective-permute-start(bf16[64,2048]{1,0:T(8,128)(2,1)} %collective-permute-done.24.refs_5_), channel_id=1, source_target_pairs={{0,1},{1,0},{2,3},{3,2},{4,5},{5,4},{6,7},{7,6},{8,9},{9,8},{10,11... | collective-permute-start | bytes 786440 | tf_op jit(solution)/shard_map/ppermute | solution.py:420
  117.6 13.3 %collective-permute-start.15 = (f32[256,1024]{1,0:T(8,128)}, f32[256,1024]{1,0:T(8,128)S(1)}, u32[]{:S(2)}, u32[]{:S(2)}) collective-permute-start(f32[256,1024]{1,0:T(8,128)} %get-tuple-element.30), channel_id=1, source_target_pairs={{0,1},{1,0},{2,3},{3,2},{4,5},{5,4},{6,7},{7,6},{8,9},{9,8},{10,11... | collective-permute-start | bytes 3145736 | tf_op jit(solution)/shard_map/ppermute | solution.py:474
  128.3 13.5 %collective-permute-start.19 = (bf16[256,1024]{1,0:T(8,128)(2,1)S(1)}, bf16[256,1024]{1,0:T(8,128)(2,1)S(1)}, u32[]{:S(2)}, u32[]{:S(2)}) collective-permute-start(bf16[256,1024]{1,0:T(8,128)(2,1)S(1)} %add_convert_fusion), channel_id=1, source_target_pairs={{0,16},{16,0},{1,17},{17,1},{2,18},{18,2},{3,19},{19,3},{4,20},{20... | collective-permute-start | bytes 1572872 | tf_op jit(solution)/shard_map/ppermute | solution.py:473
  (55 other events, 803.2 us)

commit v3 on v2

--- a/solution.py
+++ b/solution.py
@@ -20,24 +20,31 @@
 VMEM = pl.BlockSpec(memory_space=pltpu.VMEM)
 
 
-def rope_tables(positions, scale=1.0):
+def near_memory(pieces):
+    return [pltpu.with_memory_space_constraint(piece, pltpu.VMEM) for piece in pieces]
+
+
+def room(mebibytes):
+    return pltpu.CompilerParams(vmem_limit_bytes=mebibytes << 20)
+
+
+def rope_tables(positions):
     half_width = HEAD // 2
-    inv_freqs = rope_base ** (-jnp.arange(half_width, dtype=jnp.float32) * 2.0 / HEAD)
-    angles = positions[:, None] * inv_freqs[None, :]
-    cosine = jnp.cos(angles) * scale
-    sine_part = jnp.sin(angles) * scale
-    return (
-        jnp.concatenate([cosine, cosine], -1),
-        jnp.concatenate([-sine_part, sine_part], -1),
-    )
-
-
-def time_embedding(time_value, embed_width):
+    lane = lax.broadcasted_iota(jnp.int32, (1, HEAD), 1)
+    band = (lane % half_width).astype(jnp.float32)
+    angles = positions[:, None] * rope_base ** (-band * 2.0 / HEAD)
+    sign = jnp.where(lane < half_width, -1.0, 1.0)
+    return jnp.cos(angles), jnp.sin(angles) * sign
+
+
+def time_embeddings(embed_width):
     half_width = embed_width // 2
-    fraction = jnp.arange(half_width, dtype=jnp.float32) / (half_width - 1)
+    lane = lax.broadcasted_iota(jnp.int32, (1, embed_width), 1)
+    step = lax.broadcasted_iota(jnp.int32, (STEPS, 1), 0).astype(jnp.float32)
+    fraction = (lane % half_width).astype(jnp.float32) / (half_width - 1)
     period = 0.004 * (4.0 / 0.004) ** fraction
-    angles = time_value * (2.0 * jnp.pi) / period
-    return jnp.concatenate([jnp.sin(angles), jnp.cos(angles)])
+    angles = (1.0 - step / STEPS) * (2.0 * jnp.pi) / period
+    return jnp.where(lane < half_width, jnp.sin(angles), jnp.cos(angles))
 
 
 def places():
@@ -54,24 +61,30 @@
     return [c * 2 + row for c in ring] + [c * 2 + (1 - row) for c in ring]
 
 
-def pick_kernel(hidden, out, sems, *, flip, chips, width):
+def pick_kernel(hidden, out, staged, sems, *, flip, chips, width):
     core, _, _, twin = places()
     core = 1 - core if flip & 2 else core
     twin = 1 - twin if flip & 1 else twin
     part = core * 2 + twin
-    copies = []
+    inward = []
+    outward = []
     for chip in range(chips):
         start = pl.multiple_of((chip * 4 + part) * width, width)
-        copies.append(
+        here = pl.ds(chip * width, width)
+        inward.append(
             pltpu.make_async_copy(
-                hidden.at[:, pl.ds(start, width)],
-                out.at[:, pl.ds(chip * width, width)],
-                sems.at[chip],
+                hidden.at[:, pl.ds(start, width)], staged.at[:, here], sems.at[chip]
             )
         )
-    for copy in copies:
+        outward.append(
+            pltpu.make_async_copy(staged.at[:, here], out.at[:, here], sems.at[chips + chip])
+        )
+    for copy in inward:
         copy.start()
-    for copy in copies:
+    for first, second in zip(inward, outward):
+        first.wait()
+        second.start()
+    for copy in outward:
         copy.wait()
 
 
@@ -86,9 +99,13 @@
     return pl.pallas_call(
         functools.partial(pick_kernel, flip=flip, chips=chips, width=width),
         in_specs=[ANY],
-        out_specs=VMEM,
+        out_specs=ANY,
         out_shape=jax.ShapeDtypeStruct((row_count, depth // 4), jnp.bfloat16),
-        scratch_shapes=[pltpu.SemaphoreType.DMA((chips,))],
+        scratch_shapes=[
+            pltpu.VMEM((row_count, depth // 4), jnp.bfloat16),
+            pltpu.SemaphoreType.DMA((2 * chips,)),
+        ],
+        compiler_params=room(4),
         name="pick_columns",
     )(hidden)
 
@@ -123,6 +140,7 @@
             jax.ShapeDtypeStruct((row_count, depth // 4), jnp.bfloat16),
             jax.ShapeDtypeStruct((row_count, 1), jnp.float32),
         ],
+        compiler_params=room(8),
         name="own_part",
     )(hidden)
 
@@ -171,7 +189,7 @@
     shape = jax.ShapeDtypeStruct((half, 2 * split), jnp.float32)
     return pl.pallas_call(
         functools.partial(project_kernel, count=count, width=width, columns=columns),
-        in_specs=[ANY] * (2 + 2 * count),
+        in_specs=[ANY] * 2 + [VMEM] * (2 * count),
         out_specs=[VMEM, VMEM],
         out_shape=[shape, shape],
         scratch_shapes=[
@@ -179,12 +197,26 @@
             pltpu.VMEM((depth, 2 * split), jnp.bfloat16),
             pltpu.SemaphoreType.DMA((2 * count + 2,)),
         ],
+        compiler_params=room(14),
         name="prefix_project",
-    )(first, second, *keys, *values)
+    )(first, second, *near_memory(keys), *near_memory(values))
 
 
 def turn(values, cosine, sine):
     return values * cosine + pltpu.roll(values, HEAD // 2, 1) * sine
+
+
+SUMS = 3
+LEFT_PARTS = (0, 0, 1, 0, 1, 2)
+RIGHT_PARTS = (0, 1, 0, 2, 1, 0)
+
+
+def three_parts(values):
+    first = values.astype(jnp.bfloat16)
+    rest = values - first.astype(jnp.float32)
+    second = rest.astype(jnp.bfloat16)
+    third = (rest - second.astype(jnp.float32)).astype(jnp.bfloat16)
+    return first, second, third
 
 
 def expert_kernel(
@@ -195,16 +227,9 @@
     expert_gain,
     final_gain,
     output_weight,
-    query_cos,
-    query_sin,
-    action_cos,
-    action_sin,
-    prefix_cos,
-    prefix_sin,
+    cosine,
+    sine,
     row_scale,
-    kept,
-    paired,
-    twinned,
     *refs,
     columns,
     span,
@@ -215,110 +240,156 @@
     out_count,
     out_rows,
 ):
+    sums = refs[:SUMS]
+    refs = refs[SUMS:]
     proj_pieces = refs[:proj_count]
     out_pieces = refs[proj_count : proj_count + out_count]
-    (actions, proj, mix, key_cache, value_cache, joined, state_ref, turned, sems) = refs[
-        proj_count + out_count :
-    ]
+    (
+        actions,
+        proj,
+        mix,
+        keys,
+        values,
+        joined,
+        state_ref,
+        turned,
+        input_parts,
+        output_parts,
+        exact,
+        rounded,
+        sems,
+    ) = refs[proj_count + out_count :]
     core, row, column, _ = places()
     spots = chip_spots(row, column, columns)
-    copies = []
+    prefix = row_scale.shape[0]
+    early = []
     late = []
     for side in range(2):
         half = 1 - core if side else core
         for k, spot in enumerate(spots):
             piece = proj_pieces[side * len(spots) + k]
             start = pl.multiple_of((spot * 2 + half) * proj_rows, proj_rows)
-            copies.append(
-                pltpu.make_async_copy(
-                    piece, proj.at[pl.ds(start, proj_rows)], sems.at[len(copies)]
-                )
-            )
+            early.append((piece, proj.at[pl.ds(start, proj_rows)]))
         for k, spot in enumerate(spots):
             cross, slot = divmod(k, columns)
             piece = out_pieces[side * columns + slot]
             start = pl.multiple_of((spot * 2 + half) * out_rows, out_rows)
             late.append(
-                pltpu.make_async_copy(
-                    piece.at[pl.ds(cross * out_rows, out_rows)],
-                    mix.at[pl.ds(start, out_rows)],
-                    sems.at[proj_count + len(late)],
-                )
+                (piece.at[pl.ds(cross * out_rows, out_rows)], mix.at[pl.ds(start, out_rows)])
             )
-    for copy in copies + late:
+    targets = [exact.at[0], exact.at[1], rounded]
+    first = list(zip(sums, targets))
+    copies = [
+        pltpu.make_async_copy(source, target, sems.at[k])
+        for k, (source, target) in enumerate(first + early + late)
+    ]
+    for copy in copies:
         copy.start()
-    length = lengths[0]
+    first, copies = copies[: len(first)], copies[len(first) :]
+    early, late = copies[: len(early)], copies[len(early) :]
+
+    width = noise.shape[0]
+    weight_parts = three_parts(input_weight[...])
+    turned[...] = jnp.zeros_like(turned)
+    for k, part in enumerate(RIGHT_PARTS):
+        cut = slice(k * width, (k + 1) * width)
+        input_parts[cut] = weight_parts[part]
+        output_parts[cut] = output_weight[...]
+        turned[cut, :span] = noise[...]
+    state_ref[...] = turned[...].T
+    rows, wide = state_ref.shape
+    action_cos = cosine[:rows]
+    action_sin = sine[:rows]
+    query_cos = action_cos * HEAD ** (-0.5)
+    query_sin = action_sin * HEAD ** (-0.5)
+    keys[:, prefix + rows :] = jnp.zeros_like(keys[:, prefix + rows :])
+    values[:, prefix + rows :] = jnp.zeros_like(values[:, prefix + rows :])
+
+    for copy in first:
+        copy.wait()
+    for side, out in enumerate((keys, values)):
+        for g in range(groups):
+            start = (side * groups + g) * HEAD
+            cut = slice(start, start + HEAD)
+            raw = exact[0, :, cut] + exact[1, :, cut]
+            raw = (raw + rounded[:, cut].astype(jnp.float32)) * row_scale[...]
+            if side == 0:
+                raw = turn(raw, cosine[rows:], sine[rows:])
+            out[g, :prefix] = raw.astype(jnp.bfloat16)
+
+    ratio = heads // groups
+    query_width = heads * HEAD
     kv_width = groups * HEAD
-    for g in range(groups):
-        cut = slice(g * HEAD, (g + 1) * HEAD)
-        raw = kept[:, cut] + paired[:, cut] + twinned[:, cut].astype(jnp.float32)
-        raw = raw * row_scale[...]
-        key_cache[:, cut] = turn(raw, prefix_cos[...], prefix_sin[...]).astype(jnp.bfloat16)
-        cut2 = slice(kv_width + g * HEAD, kv_width + (g + 1) * HEAD)
-        raw = kept[:, cut2] + paired[:, cut2] + twinned[:, cut2].astype(jnp.float32)
-        value_cache[:, cut] = (raw * row_scale[...]).astype(jnp.bfloat16)
-    for copy in copies + late:
-        copy.wait()
-    ratio = heads // groups
-    rows = joined.shape[0]
-    query_width = heads * HEAD
     contract = (((1,), (1,)), ((), ()))
-    prefix_ok = lax.broadcasted_iota(jnp.int32, (1, key_cache.shape[0]), 1) < length
-    own_ok = lax.broadcasted_iota(jnp.int32, (1, rows), 1) < span
-    turned[...] = jnp.zeros_like(turned)
-    turned[:, :span] = noise[...]
-    state_ref[...] = turned[...].T
+    place = lax.broadcasted_iota(jnp.int32, (1, keys.shape[1]), 1)
+    allowed = (place < lengths[0]) | ((place >= prefix) & (place < prefix + span))
+    lane = lax.broadcasted_iota(jnp.int32, (1, wide), 1)
+    is_second = (lane < 0)
+    is_third = is_second
+    for k, part in enumerate(LEFT_PARTS):
+        here = (lane >= k * width) & (lane < (k + 1) * width)
+        if part == 1:
+            is_second = is_second | here
+        if part == 2:
+            is_third = is_third | here
 
     def step(k, carry):
         state = state_ref[...]
+        first = state.astype(jnp.bfloat16).astype(jnp.float32)
+        rest_part = state - first
+        second = rest_part.astype(jnp.bfloat16).astype(jnp.float32)
+        third = rest_part - second
+        parts = jnp.where(is_third, third, jnp.where(is_second, second, first))
         hidden = jnp.dot(
-            state,
-            input_weight[...],
-            precision=lax.Precision.HIGHEST,
-            preferred_element_type=jnp.float32,
+            parts.astype(jnp.bfloat16), input_parts[...], preferred_element_type=jnp.float32
         )
         hidden = hidden + embed[pl.ds(k, 1), :]
         square = jnp.mean(hidden * hidden, axis=-1, keepdims=True)
         normed = (hidden * lax.rsqrt(square + norm_eps) * expert_gain[...]).astype(jnp.bfloat16)
+
+        @pl.when(k == 0)
+        def _():
+            for copy in early:
+                copy.wait()
+
         raw = jnp.dot(normed, proj[...], preferred_element_type=jnp.float32)
+
+        @pl.when(k == 0)
+        def _():
+            for copy in late:
+                copy.wait()
+
+        base = query_width + kv_width
         for g in range(groups):
-            cut = slice(g * HEAD, (g + 1) * HEAD)
-            own_keys = turn(
+            keys[g, prefix : prefix + rows] = turn(
                 raw[:, query_width + g * HEAD : query_width + (g + 1) * HEAD],
-                action_cos[...],
-                action_sin[...],
+                action_cos,
+                action_sin,
             ).astype(jnp.bfloat16)
-            base = query_width + kv_width
-            own_values = raw[:, base + g * HEAD : base + (g + 1) * HEAD].astype(jnp.bfloat16)
+            values[g, prefix : prefix + rows] = raw[
+                :, base + g * HEAD : base + (g + 1) * HEAD
+            ].astype(jnp.bfloat16)
             queries = jnp.concatenate(
                 [
                     turn(
                         raw[:, (g * ratio + r) * HEAD : (g * ratio + r + 1) * HEAD],
-                        query_cos[...],
-                        query_sin[...],
+                        query_cos,
+                        query_sin,
                     ).astype(jnp.bfloat16)
                     for r in range(ratio)
                 ],
                 0,
             )
-            far = lax.dot_general(
-                queries, key_cache[:, cut], contract, preferred_element_type=jnp.float32
+            scores = lax.dot_general(
+                queries, keys[g], contract, preferred_element_type=jnp.float32
             )
-            near = lax.dot_general(queries, own_keys, contract, preferred_element_type=jnp.float32)
-            far = jnp.where(prefix_ok, far, -1e30)
-            near = jnp.where(own_ok, near, -1e30)
-            row_max = jnp.maximum(
-                jnp.max(far, -1, keepdims=True), jnp.max(near, -1, keepdims=True)
+            scores = jnp.where(allowed, scores, -1e30)
+            scores = jnp.exp(scores - jnp.max(scores, -1, keepdims=True))
+            inverse = 1.0 / jnp.sum(scores, -1, keepdims=True)
+            mixed = jnp.dot(
+                scores.astype(jnp.bfloat16), values[g], preferred_element_type=jnp.float32
             )
-            far = jnp.exp(far - row_max)
-            near = jnp.exp(near - row_max)
-            total = jnp.sum(far, -1, keepdims=True) + jnp.sum(near, -1, keepdims=True)
-            inverse = 1.0 / total
-            far = (far * inverse).astype(jnp.bfloat16)
-            near = (near * inverse).astype(jnp.bfloat16)
-            mixed = jnp.dot(far, value_cache[:, cut], preferred_element_type=jnp.float32)
-            mixed = mixed + jnp.dot(near, own_values, preferred_element_type=jnp.float32)
-            mixed = mixed.astype(jnp.bfloat16)
+            mixed = (mixed * inverse).astype(jnp.bfloat16)
             for r in range(ratio):
                 h = g * ratio + r
                 joined[:, h * HEAD : (h + 1) * HEAD] = mixed[r * rows : (r + 1) * rows]
@@ -326,26 +397,30 @@
         square = jnp.mean(hidden * hidden, axis=-1, keepdims=True)
         normed = (hidden * lax.rsqrt(square + norm_eps) * final_gain[...]).astype(jnp.bfloat16)
         velocity = lax.dot_general(
-            normed, output_weight[...], contract, preferred_element_type=jnp.float32
+            normed, output_parts[...], contract, preferred_element_type=jnp.float32
         )
         state_ref[...] = state - velocity / STEPS
         return carry
 
     lax.fori_loop(0, STEPS, step, 0)
     turned[...] = state_ref[...].T
-    actions[...] = turned[:, :span]
-
-
-def expert(lengths, dense, proj_pieces, out_pieces, columns, span, groups):
+    actions[...] = turned[:width, :span]
+
+
+def expert(lengths, dense, sums, proj_pieces, out_pieces, columns, span):
     proj_rows, proj_width = proj_pieces[0].shape
     out_rows = out_pieces[0].shape[0] // 2
     noise = dense[0]
-    rows = dense[6].shape[0]
-    prefix = dense[12].shape[0]
+    width = noise.shape[0]
+    prefix, sum_width = sums[0].shape
+    rows = dense[6].shape[0] - prefix
+    groups = sum_width // HEAD // 2
     proj_depth = proj_rows * len(proj_pieces)
     out_depth = out_rows * 2 * len(out_pieces)
     out_width = out_pieces[0].shape[1]
     heads = out_depth // HEAD
+    total = -(-(prefix + rows) // HEAD) * HEAD
+    stack = len(LEFT_PARTS)
     return pl.pallas_call(
         functools.partial(
             expert_kernel,
@@ -358,21 +433,34 @@
             out_count=len(out_pieces),
             out_rows=out_rows,
         ),
-        in_specs=[SMEM] + [VMEM] * len(dense) + [ANY] * (len(proj_pieces) + len(out_pieces)),
+        in_specs=[SMEM]
+        + [VMEM] * len(dense)
+        + [VMEM] * (len(sums) + len(proj_pieces) + len(out_pieces)),
         out_specs=VMEM,
         out_shape=jax.ShapeDtypeStruct(noise.shape, jnp.float32),
         scratch_shapes=[
             pltpu.VMEM((proj_depth, proj_width), jnp.bfloat16),
             pltpu.VMEM((out_depth, out_width), jnp.bfloat16),
-            pltpu.VMEM((prefix, groups * HEAD), jnp.bfloat16),
-            pltpu.VMEM((prefix, groups * HEAD), jnp.bfloat16),
+            pltpu.VMEM((groups, total, HEAD), jnp.bfloat16),
+            pltpu.VMEM((groups, total, HEAD), jnp.bfloat16),
             pltpu.VMEM((rows, heads * HEAD), jnp.bfloat16),
-            pltpu.VMEM((rows, noise.shape[0]), jnp.float32),
-            pltpu.VMEM((noise.shape[0], rows), jnp.float32),
-            pltpu.SemaphoreType.DMA((len(proj_pieces) + 2 * len(out_pieces),)),
+            pltpu.VMEM((rows, stack * width), jnp.float32),
+            pltpu.VMEM((stack * width, rows), jnp.float32),
+            pltpu.VMEM((stack * width, out_width), jnp.bfloat16),
+            pltpu.VMEM((stack * width, out_width), jnp.bfloat16),
+            pltpu.VMEM((2, prefix, sum_width), jnp.float32),
+            pltpu.VMEM((prefix, sum_width), jnp.bfloat16),
+            pltpu.SemaphoreType.DMA((SUMS + len(proj_pieces) + 2 * len(out_pieces),)),
         ],
+        compiler_params=room(20),
         name="expert_steps",
-    )(lengths, *dense, *proj_pieces, *out_pieces)
+    )(
+        lengths,
+        *dense,
+        *near_memory(sums),
+        *near_memory(proj_pieces),
+        *near_memory(out_pieces),
+    )
 
 
 def shards(
@@ -442,20 +530,16 @@
     value_pieces = value_slots + over(value_slots)
 
     proj_own = jnp.concatenate([expert_query, expert_key, expert_value], 1)
-    length = prefix_lengths[0]
     span = action_noise.shape[1]
     rows = -(-span // 16) * 16
-    embed = jnp.stack(
-        [time_embedding(1.0 - k / STEPS, input_weight.shape[1]) for k in range(STEPS)]
+    positions = jnp.concatenate(
+        [
+            prefix_lengths[0].astype(jnp.float32) + jnp.arange(rows, dtype=jnp.float32),
+            jnp.arange(hidden.shape[0], dtype=jnp.float32),
+        ]
     )
-    positions = length.astype(jnp.float32) + jnp.arange(rows, dtype=jnp.float32)
-    tables = (
-        embed,
-        *rope_tables(positions, HEAD ** (-0.5)),
-        *rope_tables(positions),
-        *rope_tables(jnp.arange(hidden.shape[0], dtype=jnp.float32)),
-    )
-    kept, tables = lax.optimization_barrier((kept, tables))
+    tables = (time_embeddings(input_weight.shape[1]), *rope_tables(positions))
+    proj_own, tables = lax.optimization_barrier((proj_own, tables))
 
     proj_slots = round_ring(proj_own)
     proj_pieces = proj_slots + over(proj_slots)
@@ -471,7 +555,7 @@
     corner_paired = lax.ppermute(corner_part, "wide", beside)
     twin_sum = (twin_part + corner_paired).astype(jnp.bfloat16)
     twinned = lax.ppermute(twin_sum, "groups", facing)
-    own_paired = lax.ppermute(core_part, "wide", beside)
+    sums = (own_part, lax.ppermute(core_part, "wide", beside), twinned)
 
     dense = (
         action_noise[0].T,
@@ -482,13 +566,15 @@
         output_weight.T,
         *tables[1:],
         row_scale,
-        own_part,
-        own_paired,
-        twinned,
     )
-    groups = key_weight.shape[1] // HEAD
     actions = expert(
-        prefix_lengths, dense, proj_pieces, out_pieces, columns, span, groups
+        prefix_lengths,
+        dense,
+        sums,
+        proj_pieces,
+        out_pieces,
+        columns,
+        span,
     )
     return actions.T[None]
 

time: 163 us -> 151 us (0.926)
  Pallas kernels: 43.1 us -> 27.4 us
  waiting for transfers between devices: 68.5 us -> 83.3 us
  other arithmetic: 9.69 us -> 3.31 us
  local copies, waits for them, and re-layouts: 8.41 us -> 3.01 us
    ppermute x12, waiting for transfers between devices: 28.7 us -> 44.4 us  [round_ring(): slots.append(lax.ppermute(slots[-1], 'wide', ring))]
    pallas_call x3, Pallas kernels: 7.03 us -> 1.52 us  [pick(): pl.pallas_call(functools.partial(pick_kernel, flip=flip, chips=chips, wid...]
    pallas_call x2, Pallas kernels: 11.6 us -> 6.37 us  [project(): pl.pallas_call(functools.partial(project_kernel, count=count, width=width...]
    ppermute x13, waiting for transfers between devices: 19.8 us -> 24.4 us  [over(): return [lax.ppermute(slot, 'wide', across) for slot in slots]]
    ppermute x1, waiting for transfers between devices: 7.25 us -> 3.13 us  [shards(): from_twin = lax.ppermute(to_twin, 'groups', facing)]
    concatenate x7 -> x2, other arithmetic: 4.85 us -> 1.07 us  [the longest x1 1 us: shards(): proj_own = jnp.concatenate([expert_query, expert_key, expert_value], 1)]
    unnamed x75 -> x17, local copies, waits for them, and re-layouts: 5.8 us -> 2.24 us
    pallas_call x1, Pallas kernels: 4.43 us -> 1.25 us  [own_part_and_scale(): pl.pallas_call(functools.partial(own_kernel, chips=chips, width=width), g...]
  transfers between devices with their start and end apart: 43 -> 43, of which waited for: 18 -> 21; matrix products, arithmetic and copies ran while one was open for 8% -> 1% of each run, Pallas kernels for 14% -> 6%
where the time goes in v3:
time: 151 us
  waiting for transfers between devices  83.3 us (55%)
  starting transfers between devices  32.5 us (22%)
  Pallas kernels  27.4 us (18%)
  other arithmetic  3.31 us (2%)
  local copies, waits for them, and re-layouts  3.01 us (2%)
    ppermute x12, waiting for transfers between devices, round_ring(): slots.append(lax.ppermute(slots[-1], 'wide', ring))  44.4 us
    ppermute x13, waiting for transfers between devices, over(): return [lax.ppermute(slot, 'wide', across) for slot in slots]  24.4 us
    pallas_call x1, Pallas kernels, expert(): pl.pallas_call(functools.partial(expert_kernel, columns=columns, span=spa...  18.3 us
    ppermute x13, starting transfers between devices, over(): return [lax.ppermute(slot, 'wide', across) for slot in slots]  17 us
    ppermute x12, starting transfers between devices, round_ring(): slots.append(lax.ppermute(slots[-1], 'wide', ring))  10.2 us
    ppermute x1, waiting for transfers between devices, shards(): twinned = lax.ppermute(twin_sum, 'groups', facing)  9.46 us
    pallas_call x2, Pallas kernels, project(): pl.pallas_call(functools.partial(project_kernel, count=count, width=width...  6.37 us
    ppermute x1, waiting for transfers between devices, shards(): from_twin = lax.ppermute(to_twin, 'groups', facing)  3.13 us
  transfers between devices with their start and end apart: 43, of which 21 were waited for; matrix products, arithmetic and copies ran while one was open for 1% of the time, Pallas kernels for 6%

profile of v3, /device:TPU:0, one launch (start us, length us, event | category | flops | bytes accessed | tf_op | source)
XLA Modules:
  0.0 150.6 jit_solution(1399537793994977974)
XLA Ops:
  1.9 3.1 %collective-permute-start.8 = (bf16[256,512]{1,0:T(8,128)(2,1)S(1)}, bf16[256,512]{1,0:T(8,128)(2,1)S(1)}, u32[]{:S(2)}, u32[]{:S(2)}) collective-permute-start(bf16[256,512]{1,0:T(8,128)(2,1)S(1)} %get-tuple-element.27.refs_8_), channel_id=1, source_target_pairs={{0,4},{1,5},{2,6},{3,7},{4,8},{5,9},{6,10},{7,11},{8,12},{9,13},{1... | collective-permute-start | bytes 786440 | tf_op jit(solution)/shard_map/ppermute | solution.py:501
  6.6 1.6 %collective-permute-start.1 = (bf16[256,512]{1,0:T(8,128)(2,1)S(1)}, bf16[256,512]{1,0:T(8,128)(2,1)S(1)}, u32[]{:S(2)}, u32[]{:S(2)}) collective-permute-start(bf16[256,512]{1,0:T(8,128)(2,1)S(1)} %get-tuple-element.28.refs_0_), channel_id=1, source_target_pairs={{0,4},{1,5},{2,6},{3,7},{4,8},{5,9},{6,10},{7,11},{8,12},{9,13},{1... | collective-permute-start | bytes 786440 | tf_op jit(solution)/shard_map/ppermute | solution.py:501
  12.8 8.4 %collective-permute-done.35 = bf16[64,1024]{1,0:T(8,128)(2,1)S(1)} collective-permute-done((bf16[64,1024]{1,0:T(8,128)(2,1)}, bf16[64,1024]{1,0:T(8,128)(2,1)S(1)}, u32[]{:S(2)}, u32[]{:S(2)}) %collective-permute-start.35) | collective-permute-done | bytes 131104 | tf_op jit(solution)/shard_map/ppermute | solution.py:505
  21.2 1.6 %collective-permute-start.20 = (bf16[64,2048]{1,0:T(8,128)(2,1)S(1)}, bf16[64,2048]{1,0:T(8,128)(2,1)S(1)}, u32[]{:S(2)}, u32[]{:S(2)}) collective-permute-start(bf16[64,2048]{1,0:T(8,128)(2,1)S(1)} %pad_maximum_fusion.refs_3_), channel_id=1, source_target_pairs={{0,4},{1,5},{2,6},{3,7},{4,8},{5,9},{6,10},{7,11},{8,12},{9,13},{1... | collective-permute-start | bytes 786440 | tf_op jit(solution)/shard_map/ppermute | solution.py:501
  22.8 1.6 %collective-permute-start.9 = (bf16[256,512]{1,0:T(8,128)(2,1)S(1)}, bf16[256,512]{1,0:T(8,128)(2,1)S(1)}, u32[]{:S(2)}, u32[]{:S(2)}) collective-permute-start(bf16[256,512]{1,0:T(8,128)(2,1)S(1)} %collective-permute-done.8.refs_9_), channel_id=1, source_target_pairs={{0,4},{1,5},{2,6},{3,7},{4,8},{5,9},{6,10},{7,11},{8,12},{9,13},{1... | collective-permute-start | bytes 786440 | tf_op jit(solution)/shard_map/ppermute | solution.py:501
  24.4 2.2 %copy-done = bf16[1,256,8192]{2,1,0:T(8,128)(2,1)S(1)} copy-done((bf16[1,256,8192]{2,1,0:T(8,128)(2,1)S(1)}, bf16[1,256,8192]{2,1,0:T(8,128)(2,1)}, u32[]{:S(2)}) %copy-start) | copy-done | bytes 4194328
  29.6 2.6 %collective-permute-done.20.refs_4_ = bf16[64,2048]{1,0:T(8,128)(2,1)S(1)} collective-permute-done((bf16[64,2048]{1,0:T(8,128)(2,1)S(1)}, bf16[64,2048]{1,0:T(8,128)(2,1)S(1)}, u32[]{:S(2)}, u32[]{:S(2)}) %collective-permute-start.20) | collective-permute-done | bytes 262176 | tf_op jit(solution)/shard_map/ppermute | solution.py:501
  33.7 3.5 %collective-permute-done.9.refs_10_ = bf16[256,512]{1,0:T(8,128)(2,1)S(1)} collective-permute-done((bf16[256,512]{1,0:T(8,128)(2,1)S(1)}, bf16[256,512]{1,0:T(8,128)(2,1)S(1)}, u32[]{:S(2)}, u32[]{:S(2)}) %collective-permute-start.9) | collective-permute-done | bytes 262176 | tf_op jit(solution)/shard_map/ppermute | solution.py:501
  38.7 2.5 %collective-permute-done.2.refs_2_ = bf16[256,512]{1,0:T(8,128)(2,1)S(1)} collective-permute-done((bf16[256,512]{1,0:T(8,128)(2,1)S(1)}, bf16[256,512]{1,0:T(8,128)(2,1)S(1)}, u32[]{:S(2)}, u32[]{:S(2)}) %collective-permute-start.2) | collective-permute-done | bytes 262176 | tf_op jit(solution)/shard_map/ppermute | solution.py:501
  42.5 1.7 %collective-permute-done.5.refs_5_ = bf16[256,512]{1,0:T(8,128)(2,1)S(1)} collective-permute-done((bf16[256,512]{1,0:T(8,128)(2,1)S(1)}, bf16[256,512]{1,0:T(8,128)(2,1)S(1)}, u32[]{:S(2)}, u32[]{:S(2)}) %collective-permute-start.5) | collective-permute-done | bytes 262176 | tf_op jit(solution)/shard_map/ppermute | solution.py:505
  45.7 6.4 %collective-permute-done.10.refs_11_ = bf16[256,512]{1,0:T(8,128)(2,1)S(1)} collective-permute-done((bf16[256,512]{1,0:T(8,128)(2,1)S(1)}, bf16[256,512]{1,0:T(8,128)(2,1)S(1)}, u32[]{:S(2)}, u32[]{:S(2)}) %collective-permute-start.10) | collective-permute-done | bytes 262176 | tf_op jit(solution)/shard_map/ppermute | solution.py:501
  53.7 1.6 %collective-permute-done.3.refs_3_ = bf16[256,512]{1,0:T(8,128)(2,1)S(1)} collective-permute-done((bf16[256,512]{1,0:T(8,128)(2,1)S(1)}, bf16[256,512]{1,0:T(8,128)(2,1)S(1)}, u32[]{:S(2)}, u32[]{:S(2)}) %collective-permute-start.3) | collective-permute-done | bytes 262176 | tf_op jit(solution)/shard_map/ppermute | solution.py:501
  57.9 3.5 %collective-permute-done.6.refs_6_ = bf16[256,512]{1,0:T(8,128)(2,1)S(1)} collective-permute-done((bf16[256,512]{1,0:T(8,128)(2,1)S(1)}, bf16[256,512]{1,0:T(8,128)(2,1)S(1)}, u32[]{:S(2)}, u32[]{:S(2)}) %collective-permute-start.6) | collective-permute-done | bytes 262176 | tf_op jit(solution)/shard_map/ppermute | solution.py:505
  61.3 5.6 %collective-permute-done.14.refs_15_ = bf16[256,512]{1,0:T(8,128)(2,1)S(1)} collective-permute-done((bf16[256,512]{1,0:T(8,128)(2,1)S(1)}, bf16[256,512]{1,0:T(8,128)(2,1)S(1)}, u32[]{:S(2)}, u32[]{:S(2)}) %collective-permute-start.14) | collective-permute-done | bytes 262176 | tf_op jit(solution)/shard_map/ppermute | solution.py:505
  68.5 3.9 %collective-permute-done.7.refs_7_ = bf16[256,512]{1,0:T(8,128)(2,1)S(1)} collective-permute-done((bf16[256,512]{1,0:T(8,128)(2,1)S(1)}, bf16[256,512]{1,0:T(8,128)(2,1)S(1)}, u32[]{:S(2)}, u32[]{:S(2)}) %collective-permute-start.7) | collective-permute-done | bytes 262176 | tf_op jit(solution)/shard_map/ppermute | solution.py:505
  72.5 3.1 %collective-permute-done.17.second = bf16[256,2048]{1,0:T(8,128)(2,1)S(1)} collective-permute-done((bf16[256,2048]{1,0:T(8,128)(2,1)S(1)}, bf16[256,2048]{1,0:T(8,128)(2,1)S(1)}, u32[]{:S(2)}, u32[]{:S(2)}) %collective-permute-start.17) | collective-permute-done | bytes 1048608 | tf_op jit(solution)/shard_map/ppermute | solution.py:514
  75.7 3.2 %prefix_project.3 = (f32[256,1024]{1,0:T(8,128)S(1)}, f32[256,1024]{1,0:T(8,128)S(1)}) custom-call(bf16[256,2048]{1,0:T(8,128)(2,1)S(1)} %collective-permute-done.16.first, bf16[256,2048]{1,0:T(8,128)(2,1)S(1)} %collective-permute-done.17.second, bf16[256,512]{1,0:T(8,128)(2,1)S(1)} %get-tuple-element.28.refs_0_, ...), custom_call_target="tpu_custom_call" | custom-call | tf_op jit(solution)/shard_map/prefix_project/pallas_call | solution.py:190
  79.7 3.2 %collective-permute-done.36.refs_20_ = bf16[128,1024]{1,0:T(8,128)(2,1)S(1)} collective-permute-done((bf16[128,1024]{1,0:T(8,128)(2,1)S(1)}, bf16[128,1024]{1,0:T(8,128)(2,1)S(1)}, u32[]{:S(2)}, u32[]{:S(2)}) %collective-permute-start.36) | collective-permute-done | bytes 262176 | tf_op jit(solution)/shard_map/ppermute | solution.py:501
  84.5 5.0 %collective-permute-done.21.refs_5_ = bf16[64,2048]{1,0:T(8,128)(2,1)S(1)} collective-permute-done((bf16[64,2048]{1,0:T(8,128)(2,1)S(1)}, bf16[64,2048]{1,0:T(8,128)(2,1)S(1)}, u32[]{:S(2)}, u32[]{:S(2)}) %collective-permute-start.21) | collective-permute-done | bytes 262176 | tf_op jit(solution)/shard_map/ppermute | solution.py:501
  91.0 10.8 %collective-permute-done.37.refs_21_ = bf16[128,1024]{1,0:T(8,128)(2,1)S(1)} collective-permute-done((bf16[128,1024]{1,0:T(8,128)(2,1)S(1)}, bf16[128,1024]{1,0:T(8,128)(2,1)S(1)}, u32[]{:S(2)}, u32[]{:S(2)}) %collective-permute-start.37) | collective-permute-done | bytes 262176 | tf_op jit(solution)/shard_map/ppermute | solution.py:501
  105.1 3.2 %prefix_project.2 = (f32[256,1024]{1,0:T(8,128)S(1)}, f32[256,1024]{1,0:T(8,128)S(1)}) custom-call(bf16[256,2048]{1,0:T(8,128)(2,1)S(1)} %collective-permute-done.first, bf16[256,2048]{1,0:T(8,128)(2,1)S(1)} %get-tuple-element.19.second, bf16[256,512]{1,0:T(8,128)(2,1)S(1)} %get-tuple-element.28.refs_0_, ...), custom_call_target="tpu_custom_call" | custom-call | tf_op jit(solution)/shard_map/prefix_project/pallas_call | solution.py:190
  110.1 8.8 %collective-permute-done.38.refs_22_ = bf16[128,1024]{1,0:T(8,128)(2,1)S(1)} collective-permute-done((bf16[128,1024]{1,0:T(8,128)(2,1)S(1)}, bf16[128,1024]{1,0:T(8,128)(2,1)S(1)}, u32[]{:S(2)}, u32[]{:S(2)}) %collective-permute-start.38) | collective-permute-done | bytes 262176 | tf_op jit(solution)/shard_map/ppermute | solution.py:501
  122.7 9.5 %collective-permute-done.19.refs_2_ = bf16[256,1024]{1,0:T(8,128)(2,1)S(1)} collective-permute-done((bf16[256,1024]{1,0:T(8,128)(2,1)S(1)}, bf16[256,1024]{1,0:T(8,128)(2,1)S(1)}, u32[]{:S(2)}, u32[]{:S(2)}) %collective-permute-start.19) | collective-permute-done | bytes 524320 | tf_op jit(solution)/shard_map/ppermute | solution.py:557
  132.2 18.3 %expert_steps.1 = f32[32,50]{1,0:T(8,128)} custom-call(s32[1]{0:T(128)S(6)} %copy.16.lengths, f32[32,50]{1,0:T(8,128)S(1)} %bitcast.16, f32[32,1024]{1,0:T(8,128)S(1)} %copy-done.2, f32[4,1024]{1,0:T(4,128)S(1)} %cosine_select_fusion.embed, f32[1,1024]{1,0:T(1,128)S(1)} %bitcast.17, f32[1,1024]{1,0:T(1,128)S(1)} %bitcast.18, bf16[32,1024]{1,0:T(8,128)(2,1)S(1)} %bitcast.15, ...), custom_call_target="tpu_custom_call" | custom-call | tf_op jit(solution)/shard_map/expert_steps/pallas_call | solution.py:424
  (100 shorter events, 34.8 us)
Async XLA Ops:
  1.9 20.9 %collective-permute-start.8 = (bf16[256,512]{1,0:T(8,128)(2,1)S(1)}, bf16[256,512]{1,0:T(8,128)(2,1)S(1)}, u32[]{:S(2)}, u32[]{:S(2)}) collective-permute-start(bf16[256,512]{1,0:T(8,128)(2,1)S(1)} %get-tuple-element.27.refs_8_), channel_id=1, source_target_pairs={{0,4},{1,5},{2,6},{3,7},{4,8},{5,9},{6,10},{7,11},{8,12},{9,13},{1... | collective-permute-start | bytes 786440 | tf_op jit(solution)/shard_map/ppermute | solution.py:501
  5.1 22.6 %collective-permute-start.11 = (bf16[256,512]{1,0:T(8,128)(2,1)S(1)}, bf16[256,512]{1,0:T(8,128)(2,1)S(1)}, u32[]{:S(2)}, u32[]{:S(2)}) collective-permute-start(bf16[256,512]{1,0:T(8,128)(2,1)S(1)} %get-tuple-element.27.refs_8_), channel_id=1, source_target_pairs={{0,2},{1,3},{2,0},{3,1},{4,6},{5,7},{6,4},{7,5},{8,10},{9,11},{10,... | collective-permute-start | bytes 786440 | tf_op jit(solution)/shard_map/ppermute | solution.py:505
  6.6 21.0 %collective-permute-start.1 = (bf16[256,512]{1,0:T(8,128)(2,1)S(1)}, bf16[256,512]{1,0:T(8,128)(2,1)S(1)}, u32[]{:S(2)}, u32[]{:S(2)}) collective-permute-start(bf16[256,512]{1,0:T(8,128)(2,1)S(1)} %get-tuple-element.28.refs_0_), channel_id=1, source_target_pairs={{0,4},{1,5},{2,6},{3,7},{4,8},{5,9},{6,10},{7,11},{8,12},{9,13},{1... | collective-permute-start | bytes 786440 | tf_op jit(solution)/shard_map/ppermute | solution.py:501
  8.1 21.1 %collective-permute-start.4 = (bf16[256,512]{1,0:T(8,128)(2,1)S(1)}, bf16[256,512]{1,0:T(8,128)(2,1)S(1)}, u32[]{:S(2)}, u32[]{:S(2)}) collective-permute-start(bf16[256,512]{1,0:T(8,128)(2,1)S(1)} %get-tuple-element.28.refs_0_), channel_id=1, source_target_pairs={{0,2},{1,3},{2,0},{3,1},{4,6},{5,7},{6,4},{7,5},{8,10},{9,11},{10,... | collective-permute-start | bytes 786440 | tf_op jit(solution)/shard_map/ppermute | solution.py:505
  8.7 12.6 %collective-permute-start.35 = (bf16[64,1024]{1,0:T(8,128)(2,1)}, bf16[64,1024]{1,0:T(8,128)(2,1)S(1)}, u32[]{:S(2)}, u32[]{:S(2)}) collective-permute-start(bf16[64,1024]{1,0:T(8,128)(2,1)} %param.25), channel_id=1, source_target_pairs={{0,2},{1,3},{2,0},{3,1},{4,6},{5,7},{6,4},{7,5},{8,10},{9,11},{10,... | collective-permute-start | bytes 393224 | tf_op jit(solution)/shard_map/ppermute | solution.py:505
  22.8 14.4 %collective-permute-start.9 = (bf16[256,512]{1,0:T(8,128)(2,1)S(1)}, bf16[256,512]{1,0:T(8,128)(2,1)S(1)}, u32[]{:S(2)}, u32[]{:S(2)}) collective-permute-start(bf16[256,512]{1,0:T(8,128)(2,1)S(1)} %collective-permute-done.8.refs_9_), channel_id=1, source_target_pairs={{0,4},{1,5},{2,6},{3,7},{4,8},{5,9},{6,10},{7,11},{8,12},{9,13},{1... | collective-permute-start | bytes 786440 | tf_op jit(solution)/shard_map/ppermute | solution.py:501
  27.6 44.8 %collective-permute-start.16 = (bf16[256,2048]{1,0:T(8,128)(2,1)S(1)}, bf16[256,2048]{1,0:T(8,128)(2,1)S(1)}, u32[]{:S(2)}, u32[]{:S(2)}) collective-permute-start(bf16[256,2048]{1,0:T(8,128)(2,1)S(1)} %pick_columns.4), channel_id=1, source_target_pairs={{0,17},{1,16},{2,19},{3,18},{4,21},{5,20},{6,23},{7,22},{8,25},{9,... | collective-permute-start | bytes 3145736 | tf_op jit(solution)/shard_map/ppermute | solution.py:512
  27.7 47.9 %collective-permute-start.17 = (bf16[256,2048]{1,0:T(8,128)(2,1)S(1)}, bf16[256,2048]{1,0:T(8,128)(2,1)S(1)}, u32[]{:S(2)}, u32[]{:S(2)}) collective-permute-start(bf16[256,2048]{1,0:T(8,128)(2,1)S(1)} %pick_columns.5), channel_id=1, source_target_pairs={{0,16},{16,0},{1,17},{17,1},{2,18},{18,2},{3,19},{19,3},{4,20},{20... | collective-permute-start | bytes 3145736 | tf_op jit(solution)/shard_map/ppermute | solution.py:514
  29.2 11.9 %collective-permute-start.2 = (bf16[256,512]{1,0:T(8,128)(2,1)S(1)}, bf16[256,512]{1,0:T(8,128)(2,1)S(1)}, u32[]{:S(2)}, u32[]{:S(2)}) collective-permute-start(bf16[256,512]{1,0:T(8,128)(2,1)S(1)} %collective-permute-done.1.refs_1_), channel_id=1, source_target_pairs={{0,4},{1,5},{2,6},{3,7},{4,8},{5,9},{6,10},{7,11},{8,12},{9,13},{1... | collective-permute-start | bytes 786440 | tf_op jit(solution)/shard_map/ppermute | solution.py:501
  41.2 11.0 %collective-permute-start.10 = (bf16[256,512]{1,0:T(8,128)(2,1)S(1)}, bf16[256,512]{1,0:T(8,128)(2,1)S(1)}, u32[]{:S(2)}, u32[]{:S(2)}) collective-permute-start(bf16[256,512]{1,0:T(8,128)(2,1)S(1)} %collective-permute-done.9.refs_10_), channel_id=1, source_target_pairs={{0,4},{1,5},{2,6},{3,7},{4,8},{5,9},{6,10},{7,11},{8,12},{9,13},{1... | collective-permute-start | bytes 786440 | tf_op jit(solution)/shard_map/ppermute | solution.py:501
  41.2 14.1 %collective-permute-start.3 = (bf16[256,512]{1,0:T(8,128)(2,1)S(1)}, bf16[256,512]{1,0:T(8,128)(2,1)S(1)}, u32[]{:S(2)}, u32[]{:S(2)}) collective-permute-start(bf16[256,512]{1,0:T(8,128)(2,1)S(1)} %collective-permute-done.2.refs_2_), channel_id=1, source_target_pairs={{0,4},{1,5},{2,6},{3,7},{4,8},{5,9},{6,10},{7,11},{8,12},{9,13},{1... | collective-permute-start | bytes 786440 | tf_op jit(solution)/shard_map/ppermute | solution.py:501
  44.2 12.6 %collective-permute-start.13 = (bf16[256,512]{1,0:T(8,128)(2,1)S(1)}, bf16[256,512]{1,0:T(8,128)(2,1)S(1)}, u32[]{:S(2)}, u32[]{:S(2)}) collective-permute-start(bf16[256,512]{1,0:T(8,128)(2,1)S(1)} %collective-permute-done.9.refs_10_), channel_id=1, source_target_pairs={{0,2},{1,3},{2,0},{3,1},{4,6},{5,7},{6,4},{7,5},{8,10},{9,11},{10,... | collective-permute-start | bytes 786440 | tf_op jit(solution)/shard_map/ppermute | solution.py:505
  55.3 11.7 %collective-permute-start.14 = (bf16[256,512]{1,0:T(8,128)(2,1)S(1)}, bf16[256,512]{1,0:T(8,128)(2,1)S(1)}, u32[]{:S(2)}, u32[]{:S(2)}) collective-permute-start(bf16[256,512]{1,0:T(8,128)(2,1)S(1)} %collective-permute-done.10.refs_11_), channel_id=1, source_target_pairs={{0,2},{1,3},{2,0},{3,1},{4,6},{5,7},{6,4},{7,5},{8,10},{9,11},{10,... | collective-permute-start | bytes 786440 | tf_op jit(solution)/shard_map/ppermute | solution.py:505
  56.8 15.5 %collective-permute-start.7 = (bf16[256,512]{1,0:T(8,128)(2,1)S(1)}, bf16[256,512]{1,0:T(8,128)(2,1)S(1)}, u32[]{:S(2)}, u32[]{:S(2)}) collective-permute-start(bf16[256,512]{1,0:T(8,128)(2,1)S(1)} %collective-permute-done.3.refs_3_), channel_id=1, source_target_pairs={{0,2},{1,3},{2,0},{3,1},{4,6},{5,7},{6,4},{7,5},{8,10},{9,11},{10,... | collective-permute-start | bytes 786440 | tf_op jit(solution)/shard_map/ppermute | solution.py:505
  61.3 42.0 %collective-permute-start = (bf16[256,2048]{1,0:T(8,128)(2,1)S(1)}, bf16[256,2048]{1,0:T(8,128)(2,1)S(1)}, u32[]{:S(2)}, u32[]{:S(2)}) collective-permute-start(bf16[256,2048]{1,0:T(8,128)(2,1)S(1)} %pick_columns.3), channel_id=1, source_target_pairs={{0,1},{1,0},{2,3},{3,2},{4,5},{5,4},{6,7},{7,6},{8,9},{9,8},{10,11... | collective-permute-start | bytes 3145736 | tf_op jit(solution)/shard_map/ppermute | solution.py:516
  67.0 11.9 %collective-permute-start.23 = (bf16[64,2048]{1,0:T(8,128)(2,1)S(1)}, bf16[64,2048]{1,0:T(8,128)(2,1)S(1)}, u32[]{:S(2)}, u32[]{:S(2)}) collective-permute-start(bf16[64,2048]{1,0:T(8,128)(2,1)S(1)} %pad_maximum_fusion.refs_3_), channel_id=1, source_target_pairs={{0,2},{1,3},{2,0},{3,1},{4,6},{5,7},{6,4},{7,5},{8,10},{9,11},{10,... | collective-permute-start | bytes 786440 | tf_op jit(solution)/shard_map/ppermute | solution.py:505
  78.9 30.9 %collective-permute-start.18 = (f32[256,1024]{1,0:T(8,128)S(1)}, f32[256,1024]{1,0:T(8,128)S(1)}, u32[]{:S(2)}, u32[]{:S(2)}) collective-permute-start(f32[256,1024]{1,0:T(8,128)S(1)} %get-tuple-element.23), channel_id=1, source_target_pairs={{0,1},{1,0},{2,3},{3,2},{4,5},{5,4},{6,7},{7,6},{8,9},{9,8},{10,11... | collective-permute-start | bytes 3145736 | tf_op jit(solution)/shard_map/ppermute | solution.py:555
  90.8 12.5 %collective-permute-start.40 = (bf16[128,1024]{1,0:T(8,128)(2,1)S(1)}, bf16[128,1024]{1,0:T(8,128)(2,1)S(1)}, u32[]{:S(2)}, u32[]{:S(2)}) collective-permute-start(bf16[128,1024]{1,0:T(8,128)(2,1)S(1)} %collective-permute-done.36.refs_20_), channel_id=1, source_target_pairs={{0,1},{1,0},{2,3},{3,2},{4,5},{5,4},{6,7},{7,6},{8,9},{9,8},{10,11... | collective-permute-start | bytes 786440 | tf_op jit(solution)/shard_map/ppermute | solution.py:508
  91.0 17.4 %collective-permute-start.22 = (bf16[64,2048]{1,0:T(8,128)(2,1)S(1)}, bf16[64,2048]{1,0:T(8,128)(2,1)S(1)}, u32[]{:S(2)}, u32[]{:S(2)}) collective-permute-start(bf16[64,2048]{1,0:T(8,128)(2,1)S(1)} %collective-permute-done.21.refs_5_), channel_id=1, source_target_pairs={{0,4},{1,5},{2,6},{3,7},{4,8},{5,9},{6,10},{7,11},{8,12},{9,13},{1... | collective-permute-start | bytes 786440 | tf_op jit(solution)/shard_map/ppermute | solution.py:501
  108.4 14.4 %collective-permute-start.15 = (f32[256,1024]{1,0:T(8,128)S(1)}, f32[256,1024]{1,0:T(8,128)S(1)}, u32[]{:S(2)}, u32[]{:S(2)}) collective-permute-start(f32[256,1024]{1,0:T(8,128)S(1)} %get-tuple-element.21), channel_id=1, source_target_pairs={{0,1},{1,0},{2,3},{3,2},{4,5},{5,4},{6,7},{7,6},{8,9},{9,8},{10,11... | collective-permute-start | bytes 3145736 | tf_op jit(solution)/shard_map/ppermute | solution.py:558
  108.7 11.7 %collective-permute-start.41 = (bf16[128,1024]{1,0:T(8,128)(2,1)S(1)}, bf16[128,1024]{1,0:T(8,128)(2,1)S(1)}, u32[]{:S(2)}, u32[]{:S(2)}) collective-permute-start(bf16[128,1024]{1,0:T(8,128)(2,1)S(1)} %collective-permute-done.37.refs_21_), channel_id=1, source_target_pairs={{0,1},{1,0},{2,3},{3,2},{4,5},{5,4},{6,7},{7,6},{8,9},{9,8},{10,11... | collective-permute-start | bytes 786440 | tf_op jit(solution)/shard_map/ppermute | solution.py:508
  109.0 11.4 %collective-permute-start.26 = (bf16[64,2048]{1,0:T(8,128)(2,1)S(1)}, bf16[64,2048]{1,0:T(8,128)(2,1)S(1)}, u32[]{:S(2)}, u32[]{:S(2)}) collective-permute-start(bf16[64,2048]{1,0:T(8,128)(2,1)S(1)} %collective-permute-done.22.refs_6_), channel_id=1, source_target_pairs={{0,2},{1,3},{2,0},{3,1},{4,6},{5,7},{6,4},{7,5},{8,10},{9,11},{10,... | collective-permute-start | bytes 786440 | tf_op jit(solution)/shard_map/ppermute | solution.py:505
  109.8 11.2 %collective-permute-start.30 = (bf16[64,2048]{1,0:T(8,128)(2,1)S(1)}, bf16[64,2048]{1,0:T(8,128)(2,1)S(1)}, u32[]{:S(2)}, u32[]{:S(2)}) collective-permute-start(bf16[64,2048]{1,0:T(8,128)(2,1)S(1)} %collective-permute-done.22.refs_6_), channel_id=1, source_target_pairs={{0,1},{1,0},{2,3},{3,2},{4,5},{5,4},{6,7},{7,6},{8,9},{9,8},{10,11... | collective-permute-start | bytes 786440 | tf_op jit(solution)/shard_map/ppermute | solution.py:508
  118.9 13.2 %collective-permute-start.19 = (bf16[256,1024]{1,0:T(8,128)(2,1)S(1)}, bf16[256,1024]{1,0:T(8,128)(2,1)S(1)}, u32[]{:S(2)}, u32[]{:S(2)}) collective-permute-start(bf16[256,1024]{1,0:T(8,128)(2,1)S(1)} %add_convert_fusion), channel_id=1, source_target_pairs={{0,16},{16,0},{1,17},{17,1},{2,18},{18,2},{3,19},{19,3},{4,20},{20... | collective-permute-start | bytes 1572872 | tf_op jit(solution)/shard_map/ppermute | solution.py:557
  (27 other events, 361.6 us)

commit v4 on v3

--- a/solution.py
+++ b/solution.py
@@ -206,9 +206,9 @@
     return values * cosine + pltpu.roll(values, HEAD // 2, 1) * sine
 
 
-SUMS = 3
 LEFT_PARTS = (0, 0, 1, 0, 1, 2)
 RIGHT_PARTS = (0, 1, 0, 2, 1, 0)
+LOG2_E = 1.4426950408889634
 
 
 def three_parts(values):
@@ -219,75 +219,71 @@
     return first, second, third
 
 
-def expert_kernel(
-    lengths,
-    noise,
-    input_weight,
-    embed,
-    expert_gain,
-    final_gain,
-    output_weight,
-    cosine,
-    sine,
-    row_scale,
-    *refs,
-    columns,
-    span,
-    heads,
-    groups,
-    proj_count,
-    proj_rows,
-    out_count,
-    out_rows,
+def weight_moves(pieces, columns, places_of, targets):
+    core, spots = places_of
+    proj, mix = targets
+    moves = []
+    proj_pieces, out_pieces = pieces
+    for (side, k), piece in proj_pieces.items():
+        rows = piece.shape[0]
+        half = 1 - core if side else core
+        start = pl.multiple_of((spots[k] * 2 + half) * rows, rows)
+        moves.append((piece, proj.at[pl.ds(start, rows)]))
+    for (side, slot), piece in out_pieces.items():
+        rows = piece.shape[0] // 2
+        half = 1 - core if side else core
+        for cross in range(2):
+            start = pl.multiple_of((spots[cross * columns + slot] * 2 + half) * rows, rows)
+            moves.append((piece.at[pl.ds(cross * rows, rows)], mix.at[pl.ds(start, rows)]))
+    return moves
+
+
+def cache_kernel(cosine, sine, row_scale, kept, paired, twinned, keys, values, *, rows):
+    groups = keys.shape[0]
+    prefix = row_scale.shape[0]
+    for side, out in enumerate((keys, values)):
+        for g in range(groups):
+            start = (side * groups + g) * HEAD
+            cut = slice(start, start + HEAD)
+            raw = kept[:, cut] + paired[:, cut] + twinned[:, cut].astype(jnp.float32)
+            raw = raw * row_scale[...]
+            if side == 0:
+                raw = turn(raw, cosine[rows:], sine[rows:])
+            out[g, :prefix] = raw.astype(jnp.bfloat16)
+        out[:, prefix:] = jnp.zeros_like(out[:, prefix:])
+
+
+def cache(cosine, sine, row_scale, sums, rows):
+    prefix, sum_width = sums[0].shape
+    groups = sum_width // HEAD // 2
+    total = -(-(prefix + rows) // HEAD) * HEAD
+    return pl.pallas_call(
+        functools.partial(cache_kernel, rows=rows),
+        in_specs=[VMEM] * 6,
+        out_specs=[VMEM] * 2,
+        out_shape=[pltpu.VMEM((groups, total, HEAD), jnp.bfloat16)] * 2,
+        compiler_params=room(4),
+        name="prefix_cache",
+    )(*near_memory((cosine, sine, row_scale)), *near_memory(sums))
+
+
+def prepare_kernel(
+    noise, input_weight, output_weight, *refs, columns, span, proj_slots, out_slots
 ):
-    sums = refs[:SUMS]
-    refs = refs[SUMS:]
-    proj_pieces = refs[:proj_count]
-    out_pieces = refs[proj_count : proj_count + out_count]
-    (
-        actions,
-        proj,
-        mix,
-        keys,
-        values,
-        joined,
-        state_ref,
-        turned,
-        input_parts,
-        output_parts,
-        exact,
-        rounded,
-        sems,
-    ) = refs[proj_count + out_count :]
+    proj_pieces = dict(zip(proj_slots, refs))
+    refs = refs[len(proj_slots) :]
+    out_pieces = dict(zip(out_slots, refs))
+    refs = refs[len(out_slots) :]
+    proj, mix, input_parts, output_parts, state, turned, sems = refs
     core, row, column, _ = places()
     spots = chip_spots(row, column, columns)
-    prefix = row_scale.shape[0]
-    early = []
-    late = []
-    for side in range(2):
-        half = 1 - core if side else core
-        for k, spot in enumerate(spots):
-            piece = proj_pieces[side * len(spots) + k]
-            start = pl.multiple_of((spot * 2 + half) * proj_rows, proj_rows)
-            early.append((piece, proj.at[pl.ds(start, proj_rows)]))
-        for k, spot in enumerate(spots):
-            cross, slot = divmod(k, columns)
-            piece = out_pieces[side * columns + slot]
-            start = pl.multiple_of((spot * 2 + half) * out_rows, out_rows)
-            late.append(
-                (piece.at[pl.ds(cross * out_rows, out_rows)], mix.at[pl.ds(start, out_rows)])
-            )
-    targets = [exact.at[0], exact.at[1], rounded]
-    first = list(zip(sums, targets))
+    moves = weight_moves((proj_pieces, out_pieces), columns, (core, spots), (proj, mix))
     copies = [
         pltpu.make_async_copy(source, target, sems.at[k])
-        for k, (source, target) in enumerate(first + early + late)
+        for k, (source, target) in enumerate(moves)
     ]
     for copy in copies:
         copy.start()
-    first, copies = copies[: len(first)], copies[len(first) :]
-    early, late = copies[: len(early)], copies[len(early) :]
-
     width = noise.shape[0]
     weight_parts = three_parts(input_weight[...])
     turned[...] = jnp.zeros_like(turned)
@@ -296,26 +292,90 @@
         input_parts[cut] = weight_parts[part]
         output_parts[cut] = output_weight[...]
         turned[cut, :span] = noise[...]
-    state_ref[...] = turned[...].T
-    rows, wide = state_ref.shape
+    state[...] = turned[...].T
+    for copy in copies:
+        copy.wait()
+
+
+def prepare(dense, proj_pieces, out_pieces, proj_depth, out_depth, columns, rows, span):
+    proj_width = next(iter(proj_pieces.values())).shape[1]
+    out_width = next(iter(out_pieces.values())).shape[1]
+    stack = len(LEFT_PARTS) * dense[0].shape[0]
+    moves = len(proj_pieces) + 2 * len(out_pieces)
+    shapes = [
+        pltpu.VMEM((proj_depth, proj_width), jnp.bfloat16),
+        pltpu.VMEM((out_depth, out_width), jnp.bfloat16),
+        pltpu.VMEM((stack, out_width), jnp.bfloat16),
+        pltpu.VMEM((stack, out_width), jnp.bfloat16),
+        pltpu.VMEM((rows, stack), jnp.float32),
+    ]
+    near = near_memory([*proj_pieces.values(), *out_pieces.values()])
+    return pl.pallas_call(
+        functools.partial(
+            prepare_kernel,
+            columns=columns,
+            span=span,
+            proj_slots=tuple(proj_pieces),
+            out_slots=tuple(out_pieces),
+        ),
+        in_specs=[VMEM] * (len(dense) + len(near)),
+        out_specs=[VMEM] * len(shapes),
+        out_shape=shapes,
+        scratch_shapes=[
+            pltpu.VMEM((stack, rows), jnp.float32),
+            pltpu.SemaphoreType.DMA((moves,)),
+        ],
+        compiler_params=room(8),
+        name="expert_prepare",
+    )(*dense, *near)
+
+
+def expert_kernel(
+    lengths,
+    embed,
+    expert_gain,
+    final_gain,
+    cosine,
+    sine,
+    first_proj,
+    first_mix,
+    first_keys,
+    first_values,
+    input_parts,
+    output_parts,
+    first_state,
+    *refs,
+    columns,
+    prefix,
+    width,
+    span,
+    proj_slots,
+    out_slots,
+):
+    proj_pieces = dict(zip(proj_slots, refs))
+    refs = refs[len(proj_slots) :]
+    out_pieces = dict(zip(out_slots, refs))
+    actions, proj, mix, keys, values, joined, score_ref, chance_ref, state_ref, turned, sems = refs[
+        len(out_slots) :
+    ]
+    core, row, column, _ = places()
+    spots = chip_spots(row, column, columns)
+    moves = weight_moves((proj_pieces, out_pieces), columns, (core, spots), (proj, mix))
+    copies = [
+        pltpu.make_async_copy(source, target, sems.at[k])
+        for k, (source, target) in enumerate(moves)
+    ]
+    for copy in copies:
+        copy.start()
+    early, late = copies[: len(proj_slots)], copies[len(proj_slots) :]
+    groups = keys.shape[0]
+    rows, wide = first_state.shape
+    heads = joined.shape[1] // HEAD
+    state_ref[...] = first_state[...]
     action_cos = cosine[:rows]
     action_sin = sine[:rows]
-    query_cos = action_cos * HEAD ** (-0.5)
-    query_sin = action_sin * HEAD ** (-0.5)
-    keys[:, prefix + rows :] = jnp.zeros_like(keys[:, prefix + rows :])
-    values[:, prefix + rows :] = jnp.zeros_like(values[:, prefix + rows :])
-
-    for copy in first:
-        copy.wait()
-    for side, out in enumerate((keys, values)):
-        for g in range(groups):
-            start = (side * groups + g) * HEAD
-            cut = slice(start, start + HEAD)
-            raw = exact[0, :, cut] + exact[1, :, cut]
-            raw = (raw + rounded[:, cut].astype(jnp.float32)) * row_scale[...]
-            if side == 0:
-                raw = turn(raw, cosine[rows:], sine[rows:])
-            out[g, :prefix] = raw.astype(jnp.bfloat16)
+    query_cos = action_cos * (HEAD ** (-0.5) * LOG2_E)
+    query_sin = action_sin * (HEAD ** (-0.5) * LOG2_E)
 
     ratio = heads // groups
     query_width = heads * HEAD
@@ -380,16 +440,18 @@
                 ],
                 0,
             )
-            scores = lax.dot_general(
+            cut = slice(g * ratio * rows, (g + 1) * ratio * rows)
+            score_ref[cut] = lax.dot_general(
                 queries, keys[g], contract, preferred_element_type=jnp.float32
             )
-            scores = jnp.where(allowed, scores, -1e30)
-            scores = jnp.exp(scores - jnp.max(scores, -1, keepdims=True))
-            inverse = 1.0 / jnp.sum(scores, -1, keepdims=True)
-            mixed = jnp.dot(
-                scores.astype(jnp.bfloat16), values[g], preferred_element_type=jnp.float32
-            )
-            mixed = (mixed * inverse).astype(jnp.bfloat16)
+        scores = jnp.where(allowed, score_ref[...], -1e30)
+        scores = jnp.exp2(scores - jnp.max(scores, -1, keepdims=True))
+        inverse = 1.0 / jnp.sum(scores, -1, keepdims=True)
+        chance_ref[...] = scores.astype(jnp.bfloat16)
+        for g in range(groups):
+            cut = slice(g * ratio * rows, (g + 1) * ratio * rows)
+            mixed = jnp.dot(chance_ref[cut], values[g], preferred_element_type=jnp.float32)
+            mixed = (mixed * inverse[cut]).astype(jnp.bfloat16)
             for r in range(ratio):
                 h = g * ratio + r
                 joined[:, h * HEAD : (h + 1) * HEAD] = mixed[r * rows : (r + 1) * rows]
@@ -407,60 +469,39 @@
     actions[...] = turned[:width, :span]
 
 
-def expert(lengths, dense, sums, proj_pieces, out_pieces, columns, span):
-    proj_rows, proj_width = proj_pieces[0].shape
-    out_rows = out_pieces[0].shape[0] // 2
-    noise = dense[0]
-    width = noise.shape[0]
-    prefix, sum_width = sums[0].shape
-    rows = dense[6].shape[0] - prefix
-    groups = sum_width // HEAD // 2
-    proj_depth = proj_rows * len(proj_pieces)
-    out_depth = out_rows * 2 * len(out_pieces)
-    out_width = out_pieces[0].shape[1]
-    heads = out_depth // HEAD
-    total = -(-(prefix + rows) // HEAD) * HEAD
-    stack = len(LEFT_PARTS)
+def expert(lengths, dense, prepared, proj_pieces, out_pieces, columns, prefix, width, span):
+    depth, _ = prepared[1].shape
+    rows = prepared[6].shape[0]
+    heads = depth // HEAD
+    pieces = near_memory([*proj_pieces.values(), *out_pieces.values()])
+    first = 1 + len(dense)
+    shapes = [jax.ShapeDtypeStruct((width, span), jnp.float32)]
+    shapes += [pltpu.VMEM(v.shape, v.dtype) for v in prepared[:4]]
     return pl.pallas_call(
         functools.partial(
             expert_kernel,
             columns=columns,
+            prefix=prefix,
+            width=width,
             span=span,
-            heads=heads,
-            groups=groups,
-            proj_count=len(proj_pieces),
-            proj_rows=proj_rows,
-            out_count=len(out_pieces),
-            out_rows=out_rows,
+            proj_slots=tuple(proj_pieces),
+            out_slots=tuple(out_pieces),
         ),
-        in_specs=[SMEM]
-        + [VMEM] * len(dense)
-        + [VMEM] * (len(sums) + len(proj_pieces) + len(out_pieces)),
-        out_specs=VMEM,
-        out_shape=jax.ShapeDtypeStruct(noise.shape, jnp.float32),
+        in_specs=[SMEM] + [VMEM] * (len(dense) + len(prepared) + len(pieces)),
+        out_specs=[VMEM] * len(shapes),
+        out_shape=shapes,
+        input_output_aliases={first + k: 1 + k for k in range(4)},
         scratch_shapes=[
-            pltpu.VMEM((proj_depth, proj_width), jnp.bfloat16),
-            pltpu.VMEM((out_depth, out_width), jnp.bfloat16),
-            pltpu.VMEM((groups, total, HEAD), jnp.bfloat16),
-            pltpu.VMEM((groups, total, HEAD), jnp.bfloat16),
             pltpu.VMEM((rows, heads * HEAD), jnp.bfloat16),
-            pltpu.VMEM((rows, stack * width), jnp.float32),
-            pltpu.VMEM((stack * width, rows), jnp.float32),
-            pltpu.VMEM((stack * width, out_width), jnp.bfloat16),
-            pltpu.VMEM((stack * width, out_width), jnp.bfloat16),
-            pltpu.VMEM((2, prefix, sum_width), jnp.float32),
-            pltpu.VMEM((prefix, sum_width), jnp.bfloat16),
-            pltpu.SemaphoreType.DMA((SUMS + len(proj_pieces) + 2 * len(out_pieces),)),
+            pltpu.VMEM((rows * heads, prepared[2].shape[1]), jnp.float32),
+            pltpu.VMEM((rows * heads, prepared[2].shape[1]), jnp.bfloat16),
+            pltpu.VMEM(prepared[6].shape, jnp.float32),
+            pltpu.VMEM(prepared[6].shape[::-1], jnp.float32),
+            pltpu.SemaphoreType.DMA((len(proj_pieces) + 2 * len(out_pieces),)),
         ],
-        compiler_params=room(20),
+        compiler_params=room(8),
         name="expert_steps",
-    )(
-        lengths,
-        *dense,
-        *near_memory(sums),
-        *near_memory(proj_pieces),
-        *near_memory(out_pieces),
-    )
+    )(lengths, *dense, *prepared, *pieces)[0]
 
 
 def shards(
@@ -557,23 +598,36 @@
     twinned = lax.ppermute(twin_sum, "groups", facing)
     sums = (own_part, lax.ppermute(core_part, "wide", beside), twinned)
 
-    dense = (
-        action_noise[0].T,
-        input_weight,
-        tables[0],
-        expert_gain[None, :],
-        final_gain[None, :],
-        output_weight.T,
-        *tables[1:],
-        row_scale,
+    span, width = action_noise.shape[1:]
+    last = columns - 1
+    proj_all = {
+        (k // (2 * columns), k % (2 * columns)): piece for k, piece in enumerate(proj_pieces)
+    }
+    out_all = {(k // columns, k % columns): piece for k, piece in enumerate(out_pieces)}
+    split = lambda pieces, ends: {
+        key: piece for key, piece in pieces.items() if (key[1] % columns == last) == ends
+    }
+    prefix_tables = tables[1:]
+    prefix_keys, prefix_values = cache(*prefix_tables, row_scale, sums, rows)
+    proj, mix, *constants = prepare(
+        (action_noise[0].T, input_weight, output_weight.T),
+        split(proj_all, False),
+        split(out_all, False),
+        proj_own.shape[0] * wide_count,
+        expert_output.shape[0] * wide_count,
+        columns,
+        rows,
+        span,
     )
     actions = expert(
         prefix_lengths,
-        dense,
-        sums,
-        proj_pieces,
-        out_pieces,
+        (tables[0], expert_gain[None, :], final_gain[None, :], *prefix_tables),
+        (proj, mix, prefix_keys, prefix_values, *constants),
+        split(proj_all, True),
+        split(out_all, True),
         columns,
+        hidden.shape[0],
+        width,
         span,
     )
     return actions.T[None]

time: 151 us -> 141 us (0.934)
  starting transfers between devices: 32.5 us -> 25.7 us
  Pallas kernels: 27.4 us -> 24.1 us
    ppermute x1, waiting for transfers between devices: 3.13 us -> 15 us  [shards(): from_twin = lax.ppermute(to_twin, 'groups', facing)]
    ppermute x1, waiting for transfers between devices: 9.46 us -> 0.01 us  [shards(): twinned = lax.ppermute(twin_sum, 'groups', facing)]
    ppermute x13, starting transfers between devices: 17 us -> 11.2 us  [over(): return [lax.ppermute(slot, 'wide', across) for slot in slots]]
    pallas_call x1 -> x3, Pallas kernels: 18.3 us -> 14.9 us  [the longest x1 11.2 us: expert(): pl.pallas_call(functools.partial(expert_kernel, columns=columns, prefix=p...]
    ppermute x12, waiting for transfers between devices: 1.86 us -> 0.03 us  [swap(): return [lax.ppermute(piece, 'wide', beside) for piece in pieces]]
    ppermute x12, waiting for transfers between devices: 44.4 us -> 46.2 us  [round_ring(): slots.append(lax.ppermute(slots[-1], 'wide', ring))]
  transfers between devices with their start and end apart: 43 -> 43, of which waited for: 21 -> 19; matrix products, arithmetic and copies ran while one was open for 1% -> 1% of each run, Pallas kernels for 6% -> 9%
where the time goes in v4:
time: 141 us
  waiting for transfers between devices  84.7 us (60%)
  starting transfers between devices  25.7 us (18%)
  Pallas kernels  24.1 us (17%)
  local copies, waits for them, and re-layouts  3.02 us (2%)
  other arithmetic  2.33 us (2%)
    ppermute x12, waiting for transfers between devices, round_ring(): slots.append(lax.ppermute(slots[-1], 'wide', ring))  46.2 us
    ppermute x13, waiting for transfers between devices, over(): return [lax.ppermute(slot, 'wide', across) for slot in slots]  23.5 us
    ppermute x1, waiting for transfers between devices, shards(): from_twin = lax.ppermute(to_twin, 'groups', facing)  15 us
    pallas_call x1, Pallas kernels, expert(): pl.pallas_call(functools.partial(expert_kernel, columns=columns, prefix=p...  11.2 us
    ppermute x13, starting transfers between devices, over(): return [lax.ppermute(slot, 'wide', across) for slot in slots]  11.2 us
    ppermute x12, starting transfers between devices, round_ring(): slots.append(lax.ppermute(slots[-1], 'wide', ring))  10.1 us
    pallas_call x2, Pallas kernels, project(): pl.pallas_call(functools.partial(project_kernel, count=count, width=width...  6.37 us
    pallas_call x1, Pallas kernels, prepare(): pl.pallas_call(functools.partial(prepare_kernel, columns=columns, span=sp...  3.11 us
  transfers between devices with their start and end apart: 43, of which 19 were waited for; matrix products, arithmetic and copies ran while one was open for 1% of the time, Pallas kernels for 9%

profile of v4, /device:TPU:0, one launch (start us, length us, event | category | flops | bytes accessed | tf_op | source)
XLA Modules:
  0.0 141.0 jit_solution(5959780919621626537)
XLA Ops:
  1.9 3.1 %collective-permute-start.25 = (bf16[256,512]{1,0:T(8,128)(2,1)S(1)}, bf16[256,512]{1,0:T(8,128)(2,1)S(1)}, u32[]{:S(2)}, u32[]{:S(2)}) collective-permute-start(bf16[256,512]{1,0:T(8,128)(2,1)S(1)} %get-tuple-element.43.refs_8_), channel_id=1, source_target_pairs={{0,4},{1,5},{2,6},{3,7},{4,8},{5,9},{6,10},{7,11},{8,12},{9,13},{1... | collective-permute-start | bytes 786440 | tf_op jit(solution)/shard_map/ppermute | solution.py:542
  8.7 5.6 %collective-permute-done.25.refs_9_ = bf16[256,512]{1,0:T(8,128)(2,1)S(1)} collective-permute-done((bf16[256,512]{1,0:T(8,128)(2,1)S(1)}, bf16[256,512]{1,0:T(8,128)(2,1)S(1)}, u32[]{:S(2)}, u32[]{:S(2)}) %collective-permute-start.25) | collective-permute-done | bytes 262176 | tf_op jit(solution)/shard_map/ppermute | solution.py:542
  14.2 1.7 %collective-permute-start.29 = (bf16[256,512]{1,0:T(8,128)(2,1)S(1)}, bf16[256,512]{1,0:T(8,128)(2,1)S(1)}, u32[]{:S(2)}, u32[]{:S(2)}) collective-permute-start(bf16[256,512]{1,0:T(8,128)(2,1)S(1)} %collective-permute-done.25.refs_9_), channel_id=1, source_target_pairs={{0,2},{1,3},{2,0},{3,1},{4,6},{5,7},{6,4},{7,5},{8,10},{9,11},{10,... | collective-permute-start | bytes 786440 | tf_op jit(solution)/shard_map/ppermute | solution.py:546
  16.6 3.2 %collective-permute-done.18.refs_1_ = bf16[256,512]{1,0:T(8,128)(2,1)S(1)} collective-permute-done((bf16[256,512]{1,0:T(8,128)(2,1)S(1)}, bf16[256,512]{1,0:T(8,128)(2,1)S(1)}, u32[]{:S(2)}, u32[]{:S(2)}) %collective-permute-start.18) | collective-permute-done | bytes 262176 | tf_op jit(solution)/shard_map/ppermute | solution.py:542
  21.6 2.2 %copy-done = bf16[1,256,8192]{2,1,0:T(8,128)(2,1)S(1)} copy-done((bf16[1,256,8192]{2,1,0:T(8,128)(2,1)S(1)}, bf16[1,256,8192]{2,1,0:T(8,128)(2,1)}, u32[]{:S(2)}) %copy-start) | copy-done | bytes 4194328
  30.2 2.3 %collective-permute-done.22.refs_5_ = bf16[256,512]{1,0:T(8,128)(2,1)S(1)} collective-permute-done((bf16[256,512]{1,0:T(8,128)(2,1)S(1)}, bf16[256,512]{1,0:T(8,128)(2,1)S(1)}, u32[]{:S(2)}, u32[]{:S(2)}) %collective-permute-start.22) | collective-permute-done | bytes 262176 | tf_op jit(solution)/shard_map/ppermute | solution.py:546
  32.5 1.7 %collective-permute-start.27 = (bf16[256,512]{1,0:T(8,128)(2,1)S(1)}, bf16[256,512]{1,0:T(8,128)(2,1)S(1)}, u32[]{:S(2)}, u32[]{:S(2)}) collective-permute-start(bf16[256,512]{1,0:T(8,128)(2,1)S(1)} %collective-permute-done.26.refs_10_), channel_id=1, source_target_pairs={{0,4},{1,5},{2,6},{3,7},{4,8},{5,9},{6,10},{7,11},{8,12},{9,13},{1... | collective-permute-start | bytes 786440 | tf_op jit(solution)/shard_map/ppermute | solution.py:542
  34.9 3.1 %collective-permute-done.19.refs_2_ = bf16[256,512]{1,0:T(8,128)(2,1)S(1)} collective-permute-done((bf16[256,512]{1,0:T(8,128)(2,1)S(1)}, bf16[256,512]{1,0:T(8,128)(2,1)S(1)}, u32[]{:S(2)}, u32[]{:S(2)}) %collective-permute-start.19) | collective-permute-done | bytes 262176 | tf_op jit(solution)/shard_map/ppermute | solution.py:542
  39.9 3.7 %collective-permute-done.27.refs_11_ = bf16[256,512]{1,0:T(8,128)(2,1)S(1)} collective-permute-done((bf16[256,512]{1,0:T(8,128)(2,1)S(1)}, bf16[256,512]{1,0:T(8,128)(2,1)S(1)}, u32[]{:S(2)}, u32[]{:S(2)}) %collective-permute-start.27) | collective-permute-done | bytes 262176 | tf_op jit(solution)/shard_map/ppermute | solution.py:542
  44.9 3.1 %collective-permute-done.20.refs_3_ = bf16[256,512]{1,0:T(8,128)(2,1)S(1)} collective-permute-done((bf16[256,512]{1,0:T(8,128)(2,1)S(1)}, bf16[256,512]{1,0:T(8,128)(2,1)S(1)}, u32[]{:S(2)}, u32[]{:S(2)}) %collective-permute-start.20) | collective-permute-done | bytes 262176 | tf_op jit(solution)/shard_map/ppermute | solution.py:542
  48.3 2.8 %collective-permute-done.31.refs_15_ = bf16[256,512]{1,0:T(8,128)(2,1)S(1)} collective-permute-done((bf16[256,512]{1,0:T(8,128)(2,1)S(1)}, bf16[256,512]{1,0:T(8,128)(2,1)S(1)}, u32[]{:S(2)}, u32[]{:S(2)}) %collective-permute-start.31) | collective-permute-done | bytes 262176 | tf_op jit(solution)/shard_map/ppermute | solution.py:546
  52.4 4.6 %collective-permute-done.24.refs_7_ = bf16[256,512]{1,0:T(8,128)(2,1)S(1)} collective-permute-done((bf16[256,512]{1,0:T(8,128)(2,1)S(1)}, bf16[256,512]{1,0:T(8,128)(2,1)S(1)}, u32[]{:S(2)}, u32[]{:S(2)}) %collective-permute-start.24) | collective-permute-done | bytes 262176 | tf_op jit(solution)/shard_map/ppermute | solution.py:546
  57.8 15.0 %collective-permute-done.34.second = bf16[256,2048]{1,0:T(8,128)(2,1)S(1)} collective-permute-done((bf16[256,2048]{1,0:T(8,128)(2,1)S(1)}, bf16[256,2048]{1,0:T(8,128)(2,1)S(1)}, u32[]{:S(2)}, u32[]{:S(2)}) %collective-permute-start.34) | collective-permute-done | bytes 1048608 | tf_op jit(solution)/shard_map/ppermute | solution.py:555
  72.8 3.2 %prefix_project.3 = (f32[256,1024]{1,0:T(8,128)S(1)}, f32[256,1024]{1,0:T(8,128)S(1)}) custom-call(bf16[256,2048]{1,0:T(8,128)(2,1)S(1)} %collective-permute-done.33.first, bf16[256,2048]{1,0:T(8,128)(2,1)S(1)} %collective-permute-done.34.second, bf16[256,512]{1,0:T(8,128)(2,1)S(1)} %get-tuple-element.44.refs_0_, ...), custom_call_target="tpu_custom_call" | custom-call | tf_op jit(solution)/shard_map/prefix_project/pallas_call | solution.py:190
  77.8 9.4 %collective-permute-done.refs_1_ = bf16[64,2048]{1,0:T(8,128)(2,1)S(1)} collective-permute-done((bf16[64,2048]{1,0:T(8,128)(2,1)S(1)}, bf16[64,2048]{1,0:T(8,128)(2,1)S(1)}, u32[]{:S(2)}, u32[]{:S(2)}) %collective-permute-start) | collective-permute-done | bytes 262176 | tf_op jit(solution)/shard_map/ppermute | solution.py:542
  87.6 4.6 %collective-permute-done.12.refs_13_ = bf16[128,1024]{1,0:T(8,128)(2,1)S(1)} collective-permute-done((bf16[128,1024]{1,0:T(8,128)(2,1)S(1)}, bf16[128,1024]{1,0:T(8,128)(2,1)S(1)}, u32[]{:S(2)}, u32[]{:S(2)}) %collective-permute-start.12) | collective-permute-done | bytes 262176 | tf_op jit(solution)/shard_map/ppermute | solution.py:542
  92.6 7.4 %collective-permute-done.3.refs_4_ = bf16[64,2048]{1,0:T(8,128)(2,1)S(1)} collective-permute-done((bf16[64,2048]{1,0:T(8,128)(2,1)S(1)}, bf16[64,2048]{1,0:T(8,128)(2,1)S(1)}, u32[]{:S(2)}, u32[]{:S(2)}) %collective-permute-start.3) | collective-permute-done | bytes 262176 | tf_op jit(solution)/shard_map/ppermute | solution.py:546
  101.3 3.2 %prefix_project.2 = (f32[256,1024]{1,0:T(8,128)S(1)}, f32[256,1024]{1,0:T(8,128)S(1)}) custom-call(bf16[256,2048]{1,0:T(8,128)(2,1)S(1)} %collective-permute-done.17.first, bf16[256,2048]{1,0:T(8,128)(2,1)S(1)} %get-tuple-element.30.second, bf16[256,512]{1,0:T(8,128)(2,1)S(1)} %get-tuple-element.44.refs_0_, ...), custom_call_target="tpu_custom_call" | custom-call | tf_op jit(solution)/shard_map/prefix_project/pallas_call | solution.py:190
  105.1 3.7 %collective-permute-done.13.refs_14_ = bf16[128,1024]{1,0:T(8,128)(2,1)S(1)} collective-permute-done((bf16[128,1024]{1,0:T(8,128)(2,1)S(1)}, bf16[128,1024]{1,0:T(8,128)(2,1)S(1)}, u32[]{:S(2)}, u32[]{:S(2)}) %collective-permute-start.13) | collective-permute-done | bytes 262176 | tf_op jit(solution)/shard_map/ppermute | solution.py:542
  109.4 6.7 %collective-permute-done.37.refs_0_ = bf16[64,2048]{1,0:T(8,128)(2,1)S(1)} collective-permute-done((bf16[64,2048]{1,0:T(8,128)(2,1)S(1)}, bf16[64,2048]{1,0:T(8,128)(2,1)S(1)}, u32[]{:S(2)}, u32[]{:S(2)}) %collective-permute-start.37) | collective-permute-done | bytes 262176 | tf_op jit(solution)/shard_map/ppermute | solution.py:542
  117.9 3.2 %collective-permute-done.41.refs_4_ = bf16[128,1024]{1,0:T(8,128)(2,1)S(1)} collective-permute-done((bf16[128,1024]{1,0:T(8,128)(2,1)S(1)}, bf16[128,1024]{1,0:T(8,128)(2,1)S(1)}, u32[]{:S(2)}, u32[]{:S(2)}) %collective-permute-start.41) | collective-permute-done | bytes 262176 | tf_op jit(solution)/shard_map/ppermute | solution.py:542
  121.6 3.7 %collective-permute-done.38.refs_1_ = bf16[64,2048]{1,0:T(8,128)(2,1)S(1)} collective-permute-done((bf16[64,2048]{1,0:T(8,128)(2,1)S(1)}, bf16[64,2048]{1,0:T(8,128)(2,1)S(1)}, u32[]{:S(2)}, u32[]{:S(2)}) %collective-permute-start.38) | collective-permute-done | bytes 262176 | tf_op jit(solution)/shard_map/ppermute | solution.py:546
  125.8 3.1 %expert_prepare.1 = (bf16[1024,2048]{1,0:T(8,128)(2,1)S(1)}, bf16[1024,1024]{1,0:T(8,128)(2,1)S(1)}, bf16[192,1024]{1,0:T(8,128)(2,1)S(1)}, bf16[192,1024]{1,0:T(8,128)(2,1)S(1)}, f32[64,192]{1,0:T(8,128)S(1)}) custom-call(f32[32,50]{1,0:T(8,128)S(1)} %bitcast.16, f32[32,1024]{1,0:T(8,128)S(1)} %copy-done.2, bf16[32,1024]{1,0:T(8,128)(2,1)S(1)} %bitcast.15, ...), custom_call_target="tpu_custom_call" | custom-call | tf_op jit(solution)/shard_map/expert_prepare/pallas_call | solution.py:313
  129.7 11.2 %expert_steps.1 = (f32[32,50]{1,0:T(8,128)}, bf16[1024,2048]{1,0:T(8,128)(2,1)S(1)}, bf16[1024,1024]{1,0:T(8,128)(2,1)S(1)}, bf16[4,384,128]{2,1,0:T(8,128)(2,1)S(1)}, bf16[4,384,128]{2,1,0:T(8,128)(2,1)S(1)}) custom-call(s32[1]{0:T(128)S(6)} %copy.24.lengths, ...), custom_call_target="tpu_custom_call", output_to_operand_aliasing={{1}: (6, {}), {2}: (7, {}), {3}: (8, {}), {4}: (9, {})} | custom-call | tf_op jit(solution)/shard_map/expert_steps/pallas_call | solution.py:480
  (108 shorter events, 28.4 us)
Async XLA Ops:
  1.9 12.3 %collective-permute-start.25 = (bf16[256,512]{1,0:T(8,128)(2,1)S(1)}, bf16[256,512]{1,0:T(8,128)(2,1)S(1)}, u32[]{:S(2)}, u32[]{:S(2)}) collective-permute-start(bf16[256,512]{1,0:T(8,128)(2,1)S(1)} %get-tuple-element.43.refs_8_), channel_id=1, source_target_pairs={{0,4},{1,5},{2,6},{3,7},{4,8},{5,9},{6,10},{7,11},{8,12},{9,13},{1... | collective-permute-start | bytes 786440 | tf_op jit(solution)/shard_map/ppermute | solution.py:542
  5.1 14.8 %collective-permute-start.18 = (bf16[256,512]{1,0:T(8,128)(2,1)S(1)}, bf16[256,512]{1,0:T(8,128)(2,1)S(1)}, u32[]{:S(2)}, u32[]{:S(2)}) collective-permute-start(bf16[256,512]{1,0:T(8,128)(2,1)S(1)} %get-tuple-element.44.refs_0_), channel_id=1, source_target_pairs={{0,4},{1,5},{2,6},{3,7},{4,8},{5,9},{6,10},{7,11},{8,12},{9,13},{1... | collective-permute-start | bytes 786440 | tf_op jit(solution)/shard_map/ppermute | solution.py:542
  6.6 18.3 %collective-permute-start.28 = (bf16[256,512]{1,0:T(8,128)(2,1)S(1)}, bf16[256,512]{1,0:T(8,128)(2,1)S(1)}, u32[]{:S(2)}, u32[]{:S(2)}) collective-permute-start(bf16[256,512]{1,0:T(8,128)(2,1)S(1)} %get-tuple-element.43.refs_8_), channel_id=1, source_target_pairs={{0,2},{1,3},{2,0},{3,1},{4,6},{5,7},{6,4},{7,5},{8,10},{9,11},{10,... | collective-permute-start | bytes 786440 | tf_op jit(solution)/shard_map/ppermute | solution.py:546
  8.1 16.8 %collective-permute-start.21 = (bf16[256,512]{1,0:T(8,128)(2,1)S(1)}, bf16[256,512]{1,0:T(8,128)(2,1)S(1)}, u32[]{:S(2)}, u32[]{:S(2)}) collective-permute-start(bf16[256,512]{1,0:T(8,128)(2,1)S(1)} %get-tuple-element.44.refs_0_), channel_id=1, source_target_pairs={{0,2},{1,3},{2,0},{3,1},{4,6},{5,7},{6,4},{7,5},{8,10},{9,11},{10,... | collective-permute-start | bytes 786440 | tf_op jit(solution)/shard_map/ppermute | solution.py:546
  14.2 12.8 %collective-permute-start.29 = (bf16[256,512]{1,0:T(8,128)(2,1)S(1)}, bf16[256,512]{1,0:T(8,128)(2,1)S(1)}, u32[]{:S(2)}, u32[]{:S(2)}) collective-permute-start(bf16[256,512]{1,0:T(8,128)(2,1)S(1)} %collective-permute-done.25.refs_9_), channel_id=1, source_target_pairs={{0,2},{1,3},{2,0},{3,1},{4,6},{5,7},{6,4},{7,5},{8,10},{9,11},{10,... | collective-permute-start | bytes 786440 | tf_op jit(solution)/shard_map/ppermute | solution.py:546
  16.0 12.7 %collective-permute-start.26 = (bf16[256,512]{1,0:T(8,128)(2,1)S(1)}, bf16[256,512]{1,0:T(8,128)(2,1)S(1)}, u32[]{:S(2)}, u32[]{:S(2)}) collective-permute-start(bf16[256,512]{1,0:T(8,128)(2,1)S(1)} %collective-permute-done.25.refs_9_), channel_id=1, source_target_pairs={{0,4},{1,5},{2,6},{3,7},{4,8},{5,9},{6,10},{7,11},{8,12},{9,13},{1... | collective-permute-start | bytes 786440 | tf_op jit(solution)/shard_map/ppermute | solution.py:542
  19.8 12.6 %collective-permute-start.22 = (bf16[256,512]{1,0:T(8,128)(2,1)S(1)}, bf16[256,512]{1,0:T(8,128)(2,1)S(1)}, u32[]{:S(2)}, u32[]{:S(2)}) collective-permute-start(bf16[256,512]{1,0:T(8,128)(2,1)S(1)} %collective-permute-done.18.refs_1_), channel_id=1, source_target_pairs={{0,2},{1,3},{2,0},{3,1},{4,6},{5,7},{6,4},{7,5},{8,10},{9,11},{10,... | collective-permute-start | bytes 786440 | tf_op jit(solution)/shard_map/ppermute | solution.py:546
  24.9 32.1 %collective-permute-start.33 = (bf16[256,2048]{1,0:T(8,128)(2,1)S(1)}, bf16[256,2048]{1,0:T(8,128)(2,1)S(1)}, u32[]{:S(2)}, u32[]{:S(2)}) collective-permute-start(bf16[256,2048]{1,0:T(8,128)(2,1)S(1)} %pick_columns.4), channel_id=1, source_target_pairs={{0,17},{1,16},{2,19},{3,18},{4,21},{5,20},{6,23},{7,22},{8,25},{9,... | collective-permute-start | bytes 3145736 | tf_op jit(solution)/shard_map/ppermute | solution.py:553
  24.9 47.9 %collective-permute-start.34 = (bf16[256,2048]{1,0:T(8,128)(2,1)S(1)}, bf16[256,2048]{1,0:T(8,128)(2,1)S(1)}, u32[]{:S(2)}, u32[]{:S(2)}) collective-permute-start(bf16[256,2048]{1,0:T(8,128)(2,1)S(1)} %pick_columns.5), channel_id=1, source_target_pairs={{0,16},{16,0},{1,17},{17,1},{2,18},{18,2},{3,19},{19,3},{4,20},{20... | collective-permute-start | bytes 3145736 | tf_op jit(solution)/shard_map/ppermute | solution.py:555
  27.0 11.0 %collective-permute-start.19 = (bf16[256,512]{1,0:T(8,128)(2,1)S(1)}, bf16[256,512]{1,0:T(8,128)(2,1)S(1)}, u32[]{:S(2)}, u32[]{:S(2)}) collective-permute-start(bf16[256,512]{1,0:T(8,128)(2,1)S(1)} %collective-permute-done.18.refs_1_), channel_id=1, source_target_pairs={{0,4},{1,5},{2,6},{3,7},{4,8},{5,9},{6,10},{7,11},{8,12},{9,13},{1... | collective-permute-start | bytes 786440 | tf_op jit(solution)/shard_map/ppermute | solution.py:542
  32.5 11.1 %collective-permute-start.27 = (bf16[256,512]{1,0:T(8,128)(2,1)S(1)}, bf16[256,512]{1,0:T(8,128)(2,1)S(1)}, u32[]{:S(2)}, u32[]{:S(2)}) collective-permute-start(bf16[256,512]{1,0:T(8,128)(2,1)S(1)} %collective-permute-done.26.refs_10_), channel_id=1, source_target_pairs={{0,4},{1,5},{2,6},{3,7},{4,8},{5,9},{6,10},{7,11},{8,12},{9,13},{1... | collective-permute-start | bytes 786440 | tf_op jit(solution)/shard_map/ppermute | solution.py:542
  44.9 55.1 %collective-permute-start.17 = (bf16[256,2048]{1,0:T(8,128)(2,1)S(1)}, bf16[256,2048]{1,0:T(8,128)(2,1)S(1)}, u32[]{:S(2)}, u32[]{:S(2)}) collective-permute-start(bf16[256,2048]{1,0:T(8,128)(2,1)S(1)} %pick_columns.3), channel_id=1, source_target_pairs={{0,1},{1,0},{2,3},{3,2},{4,5},{5,4},{6,7},{7,6},{8,9},{9,8},{10,11... | collective-permute-start | bytes 3145736 | tf_op jit(solution)/shard_map/ppermute | solution.py:557
  51.1 25.0 %collective-permute-start.11 = (bf16[64,1024]{1,0:T(8,128)(2,1)S(1)}, bf16[64,1024]{1,0:T(8,128)(2,1)S(1)}, u32[]{:S(2)}, u32[]{:S(2)}) collective-permute-start(bf16[64,1024]{1,0:T(8,128)(2,1)S(1)} %copy-done.7), channel_id=1, source_target_pairs={{0,2},{1,3},{2,0},{3,1},{4,6},{5,7},{6,4},{7,5},{8,10},{9,11},{10,... | collective-permute-start | bytes 393224 | tf_op jit(solution)/shard_map/ppermute | solution.py:546
  57.0 19.2 %collective-permute-start.5 = (bf16[64,2048]{1,0:T(8,128)(2,1)S(1)}, bf16[64,2048]{1,0:T(8,128)(2,1)S(1)}, u32[]{:S(2)}, u32[]{:S(2)}) collective-permute-start(bf16[64,2048]{1,0:T(8,128)(2,1)S(1)} %pad_maximum_fusion.refs_0_), channel_id=1, source_target_pairs={{0,1},{1,0},{2,3},{3,2},{4,5},{5,4},{6,7},{7,6},{8,9},{9,8},{10,11... | collective-permute-start | bytes 786440 | tf_op jit(solution)/shard_map/ppermute | solution.py:549
  57.0 19.7 %collective-permute-start.2 = (bf16[64,2048]{1,0:T(8,128)(2,1)S(1)}, bf16[64,2048]{1,0:T(8,128)(2,1)S(1)}, u32[]{:S(2)}, u32[]{:S(2)}) collective-permute-start(bf16[64,2048]{1,0:T(8,128)(2,1)S(1)} %pad_maximum_fusion.refs_0_), channel_id=1, source_target_pairs={{0,2},{1,3},{2,0},{3,1},{4,6},{5,7},{6,4},{7,5},{8,10},{9,11},{10,... | collective-permute-start | bytes 786440 | tf_op jit(solution)/shard_map/ppermute | solution.py:546
  76.0 33.2 %collective-permute-start.35 = (f32[256,1024]{1,0:T(8,128)S(1)}, f32[256,1024]{1,0:T(8,128)S(1)}, u32[]{:S(2)}, u32[]{:S(2)}) collective-permute-start(f32[256,1024]{1,0:T(8,128)S(1)} %get-tuple-element.34), channel_id=1, source_target_pairs={{0,1},{1,0},{2,3},{3,2},{4,5},{5,4},{6,7},{7,6},{8,9},{9,8},{10,11... | collective-permute-start | bytes 3145736 | tf_op jit(solution)/shard_map/ppermute | solution.py:596
  76.1 11.0 %collective-permute-start = (bf16[64,2048]{1,0:T(8,128)(2,1)S(1)}, bf16[64,2048]{1,0:T(8,128)(2,1)S(1)}, u32[]{:S(2)}, u32[]{:S(2)}) collective-permute-start(bf16[64,2048]{1,0:T(8,128)(2,1)S(1)} %pad_maximum_fusion.refs_0_), channel_id=1, source_target_pairs={{0,4},{1,5},{2,6},{3,7},{4,8},{5,9},{6,10},{7,11},{8,12},{9,13},{1... | collective-permute-start | bytes 786440 | tf_op jit(solution)/shard_map/ppermute | solution.py:542
  76.7 15.5 %collective-permute-start.12 = (bf16[128,1024]{1,0:T(8,128)(2,1)S(1)}, bf16[128,1024]{1,0:T(8,128)(2,1)S(1)}, u32[]{:S(2)}, u32[]{:S(2)}) collective-permute-start(bf16[128,1024]{1,0:T(8,128)(2,1)S(1)} %constant_dynamic-update-slice_fusion.refs_12_), channel_id=1, source_target_pairs={{0,4},{1,5},{2,6},{3,7},{4,8},{5,9},{6,10},{7,11},{8,12},{9,13},{1... | collective-permute-start | bytes 786440 | tf_op jit(solution)/shard_map/ppermute | solution.py:542
  92.5 12.0 %collective-permute-start.1 = (bf16[64,2048]{1,0:T(8,128)(2,1)S(1)}, bf16[64,2048]{1,0:T(8,128)(2,1)S(1)}, u32[]{:S(2)}, u32[]{:S(2)}) collective-permute-start(bf16[64,2048]{1,0:T(8,128)(2,1)S(1)} %collective-permute-done.refs_1_), channel_id=1, source_target_pairs={{0,4},{1,5},{2,6},{3,7},{4,8},{5,9},{6,10},{7,11},{8,12},{9,13},{1... | collective-permute-start | bytes 786440 | tf_op jit(solution)/shard_map/ppermute | solution.py:542
  92.5 12.6 %collective-permute-start.15 = (bf16[128,1024]{1,0:T(8,128)(2,1)S(1)}, bf16[128,1024]{1,0:T(8,128)(2,1)S(1)}, u32[]{:S(2)}, u32[]{:S(2)}) collective-permute-start(bf16[128,1024]{1,0:T(8,128)(2,1)S(1)} %collective-permute-done.12.refs_13_), channel_id=1, source_target_pairs={{0,1},{1,0},{2,3},{3,2},{4,5},{5,4},{6,7},{7,6},{8,9},{9,8},{10,11... | collective-permute-start | bytes 786440 | tf_op jit(solution)/shard_map/ppermute | solution.py:549
  104.5 24.4 %collective-permute-start.32 = (f32[256,1024]{1,0:T(8,128)S(1)}, f32[256,1024]{1,0:T(8,128)S(1)}, u32[]{:S(2)}, u32[]{:S(2)}) collective-permute-start(f32[256,1024]{1,0:T(8,128)S(1)} %get-tuple-element.32), channel_id=1, source_target_pairs={{0,1},{1,0},{2,3},{3,2},{4,5},{5,4},{6,7},{7,6},{8,9},{9,8},{10,11... | collective-permute-start | bytes 3145736 | tf_op jit(solution)/shard_map/ppermute | solution.py:599
  105.1 11.0 %collective-permute-start.37 = (bf16[64,2048]{1,0:T(8,128)(2,1)S(1)}, bf16[64,2048]{1,0:T(8,128)(2,1)S(1)}, u32[]{:S(2)}, u32[]{:S(2)}) collective-permute-start(bf16[64,2048]{1,0:T(8,128)(2,1)S(1)} %collective-permute-done.1.refs_2_), channel_id=1, source_target_pairs={{0,4},{1,5},{2,6},{3,7},{4,8},{5,9},{6,10},{7,11},{8,12},{9,13},{1... | collective-permute-start | bytes 786440 | tf_op jit(solution)/shard_map/ppermute | solution.py:542
  109.2 11.9 %collective-permute-start.41 = (bf16[128,1024]{1,0:T(8,128)(2,1)S(1)}, bf16[128,1024]{1,0:T(8,128)(2,1)S(1)}, u32[]{:S(2)}, u32[]{:S(2)}) collective-permute-start(bf16[128,1024]{1,0:T(8,128)(2,1)S(1)} %collective-permute-done.13.refs_14_), channel_id=1, source_target_pairs={{0,4},{1,5},{2,6},{3,7},{4,8},{5,9},{6,10},{7,11},{8,12},{9,13},{1... | collective-permute-start | bytes 786440 | tf_op jit(solution)/shard_map/ppermute | solution.py:542
  116.1 12.9 %collective-permute-start.36 = (bf16[256,1024]{1,0:T(8,128)(2,1)S(1)}, bf16[256,1024]{1,0:T(8,128)(2,1)S(1)}, u32[]{:S(2)}, u32[]{:S(2)}) collective-permute-start(bf16[256,1024]{1,0:T(8,128)(2,1)S(1)} %add_convert_fusion), channel_id=1, source_target_pairs={{0,16},{16,0},{1,17},{17,1},{2,18},{18,2},{3,19},{19,3},{4,20},{20... | collective-permute-start | bytes 1572872 | tf_op jit(solution)/shard_map/ppermute | solution.py:598
  (30 other events, 350.3 us)

commit v5 on v4

--- a/solution.py
+++ b/solution.py
@@ -393,7 +393,7 @@
         if part == 2:
             is_third = is_third | here
 
-    def step(k, carry):
+    def step(k):
         state = state_ref[...]
         first = state.astype(jnp.bfloat16).astype(jnp.float32)
         rest_part = state - first
@@ -403,19 +403,17 @@
         hidden = jnp.dot(
             parts.astype(jnp.bfloat16), input_parts[...], preferred_element_type=jnp.float32
         )
-        hidden = hidden + embed[pl.ds(k, 1), :]
+        hidden = hidden + embed[k : k + 1, :]
         square = jnp.mean(hidden * hidden, axis=-1, keepdims=True)
         normed = (hidden * lax.rsqrt(square + norm_eps) * expert_gain[...]).astype(jnp.bfloat16)
 
-        @pl.when(k == 0)
-        def _():
+        if k == 0:
             for copy in early:
                 copy.wait()
 
         raw = jnp.dot(normed, proj[...], preferred_element_type=jnp.float32)
 
-        @pl.when(k == 0)
-        def _():
+        if k == 0:
             for copy in late:
                 copy.wait()
 
@@ -462,9 +460,9 @@
             normed, output_parts[...], contract, preferred_element_type=jnp.float32
         )
         state_ref[...] = state - velocity / STEPS
-        return carry
-
-    lax.fori_loop(0, STEPS, step, 0)
+
+    for k in range(STEPS):
+        step(k)
     turned[...] = state_ref[...].T
     actions[...] = turned[:width, :span]
 

time: 141 us -> 141 us (level)
  no operation moved by 1% of the time
where the time goes in v5:
time: 141 us
  waiting for transfers between devices  84.7 us (60%)
  starting transfers between devices  25.7 us (18%)
  Pallas kernels  23.9 us (17%)
  local copies, waits for them, and re-layouts  3.02 us (2%)
  other arithmetic  2.33 us (2%)
    ppermute x12, waiting for transfers between devices, round_ring(): slots.append(lax.ppermute(slots[-1], 'wide', ring))  46.2 us
    ppermute x13, waiting for transfers between devices, over(): return [lax.ppermute(slot, 'wide', across) for slot in slots]  23.5 us
    ppermute x1, waiting for transfers between devices, shards(): from_twin = lax.ppermute(to_twin, 'groups', facing)  15 us
    ppermute x13, starting transfers between devices, over(): return [lax.ppermute(slot, 'wide', across) for slot in slots]  11.2 us
    pallas_call x1, Pallas kernels, expert(): pl.pallas_call(functools.partial(expert_kernel, columns=columns, prefix=p...  11 us
    ppermute x12, starting transfers between devices, round_ring(): slots.append(lax.ppermute(slots[-1], 'wide', ring))  10.1 us
    pallas_call x2, Pallas kernels, project(): pl.pallas_call(functools.partial(project_kernel, count=count, width=width...  6.37 us
    pallas_call x1, Pallas kernels, prepare(): pl.pallas_call(functools.partial(prepare_kernel, columns=columns, span=sp...  3.11 us
  transfers between devices with their start and end apart: 43, of which 19 were waited for; matrix products, arithmetic and copies ran while one was open for 1% of the time, Pallas kernels for 9%

profile of v5, /device:TPU:0, one launch (start us, length us, event | category | flops | bytes accessed | tf_op | source)
XLA Modules:
  0.0 140.8 jit_solution(18349319927082482152)
XLA Ops:
  1.9 3.1 %collective-permute-start.25 = (bf16[256,512]{1,0:T(8,128)(2,1)S(1)}, bf16[256,512]{1,0:T(8,128)(2,1)S(1)}, u32[]{:S(2)}, u32[]{:S(2)}) collective-permute-start(bf16[256,512]{1,0:T(8,128)(2,1)S(1)} %get-tuple-element.43.refs_8_), channel_id=1, source_target_pairs={{0,4},{1,5},{2,6},{3,7},{4,8},{5,9},{6,10},{7,11},{8,12},{9,13},{1... | collective-permute-start | bytes 786440 | tf_op jit(solution)/shard_map/ppermute | solution.py:540
  8.7 5.6 %collective-permute-done.25.refs_9_ = bf16[256,512]{1,0:T(8,128)(2,1)S(1)} collective-permute-done((bf16[256,512]{1,0:T(8,128)(2,1)S(1)}, bf16[256,512]{1,0:T(8,128)(2,1)S(1)}, u32[]{:S(2)}, u32[]{:S(2)}) %collective-permute-start.25) | collective-permute-done | bytes 262176 | tf_op jit(solution)/shard_map/ppermute | solution.py:540
  14.2 1.7 %collective-permute-start.29 = (bf16[256,512]{1,0:T(8,128)(2,1)S(1)}, bf16[256,512]{1,0:T(8,128)(2,1)S(1)}, u32[]{:S(2)}, u32[]{:S(2)}) collective-permute-start(bf16[256,512]{1,0:T(8,128)(2,1)S(1)} %collective-permute-done.25.refs_9_), channel_id=1, source_target_pairs={{0,2},{1,3},{2,0},{3,1},{4,6},{5,7},{6,4},{7,5},{8,10},{9,11},{10,... | collective-permute-start | bytes 786440 | tf_op jit(solution)/shard_map/ppermute | solution.py:544
  16.6 3.2 %collective-permute-done.18.refs_1_ = bf16[256,512]{1,0:T(8,128)(2,1)S(1)} collective-permute-done((bf16[256,512]{1,0:T(8,128)(2,1)S(1)}, bf16[256,512]{1,0:T(8,128)(2,1)S(1)}, u32[]{:S(2)}, u32[]{:S(2)}) %collective-permute-start.18) | collective-permute-done | bytes 262176 | tf_op jit(solution)/shard_map/ppermute | solution.py:540
  21.6 2.2 %copy-done = bf16[1,256,8192]{2,1,0:T(8,128)(2,1)S(1)} copy-done((bf16[1,256,8192]{2,1,0:T(8,128)(2,1)S(1)}, bf16[1,256,8192]{2,1,0:T(8,128)(2,1)}, u32[]{:S(2)}) %copy-start) | copy-done | bytes 4194328
  30.2 2.3 %collective-permute-done.22.refs_5_ = bf16[256,512]{1,0:T(8,128)(2,1)S(1)} collective-permute-done((bf16[256,512]{1,0:T(8,128)(2,1)S(1)}, bf16[256,512]{1,0:T(8,128)(2,1)S(1)}, u32[]{:S(2)}, u32[]{:S(2)}) %collective-permute-start.22) | collective-permute-done | bytes 262176 | tf_op jit(solution)/shard_map/ppermute | solution.py:544
  32.5 1.7 %collective-permute-start.27 = (bf16[256,512]{1,0:T(8,128)(2,1)S(1)}, bf16[256,512]{1,0:T(8,128)(2,1)S(1)}, u32[]{:S(2)}, u32[]{:S(2)}) collective-permute-start(bf16[256,512]{1,0:T(8,128)(2,1)S(1)} %collective-permute-done.26.refs_10_), channel_id=1, source_target_pairs={{0,4},{1,5},{2,6},{3,7},{4,8},{5,9},{6,10},{7,11},{8,12},{9,13},{1... | collective-permute-start | bytes 786440 | tf_op jit(solution)/shard_map/ppermute | solution.py:540
  34.9 3.1 %collective-permute-done.19.refs_2_ = bf16[256,512]{1,0:T(8,128)(2,1)S(1)} collective-permute-done((bf16[256,512]{1,0:T(8,128)(2,1)S(1)}, bf16[256,512]{1,0:T(8,128)(2,1)S(1)}, u32[]{:S(2)}, u32[]{:S(2)}) %collective-permute-start.19) | collective-permute-done | bytes 262176 | tf_op jit(solution)/shard_map/ppermute | solution.py:540
  39.9 3.7 %collective-permute-done.27.refs_11_ = bf16[256,512]{1,0:T(8,128)(2,1)S(1)} collective-permute-done((bf16[256,512]{1,0:T(8,128)(2,1)S(1)}, bf16[256,512]{1,0:T(8,128)(2,1)S(1)}, u32[]{:S(2)}, u32[]{:S(2)}) %collective-permute-start.27) | collective-permute-done | bytes 262176 | tf_op jit(solution)/shard_map/ppermute | solution.py:540
  44.9 3.1 %collective-permute-done.20.refs_3_ = bf16[256,512]{1,0:T(8,128)(2,1)S(1)} collective-permute-done((bf16[256,512]{1,0:T(8,128)(2,1)S(1)}, bf16[256,512]{1,0:T(8,128)(2,1)S(1)}, u32[]{:S(2)}, u32[]{:S(2)}) %collective-permute-start.20) | collective-permute-done | bytes 262176 | tf_op jit(solution)/shard_map/ppermute | solution.py:540
  48.3 2.8 %collective-permute-done.31.refs_15_ = bf16[256,512]{1,0:T(8,128)(2,1)S(1)} collective-permute-done((bf16[256,512]{1,0:T(8,128)(2,1)S(1)}, bf16[256,512]{1,0:T(8,128)(2,1)S(1)}, u32[]{:S(2)}, u32[]{:S(2)}) %collective-permute-start.31) | collective-permute-done | bytes 262176 | tf_op jit(solution)/shard_map/ppermute | solution.py:544
  52.4 4.6 %collective-permute-done.24.refs_7_ = bf16[256,512]{1,0:T(8,128)(2,1)S(1)} collective-permute-done((bf16[256,512]{1,0:T(8,128)(2,1)S(1)}, bf16[256,512]{1,0:T(8,128)(2,1)S(1)}, u32[]{:S(2)}, u32[]{:S(2)}) %collective-permute-start.24) | collective-permute-done | bytes 262176 | tf_op jit(solution)/shard_map/ppermute | solution.py:544
  57.8 15.0 %collective-permute-done.34.second = bf16[256,2048]{1,0:T(8,128)(2,1)S(1)} collective-permute-done((bf16[256,2048]{1,0:T(8,128)(2,1)S(1)}, bf16[256,2048]{1,0:T(8,128)(2,1)S(1)}, u32[]{:S(2)}, u32[]{:S(2)}) %collective-permute-start.34) | collective-permute-done | bytes 1048608 | tf_op jit(solution)/shard_map/ppermute | solution.py:553
  72.8 3.2 %prefix_project.3 = (f32[256,1024]{1,0:T(8,128)S(1)}, f32[256,1024]{1,0:T(8,128)S(1)}) custom-call(bf16[256,2048]{1,0:T(8,128)(2,1)S(1)} %collective-permute-done.33.first, bf16[256,2048]{1,0:T(8,128)(2,1)S(1)} %collective-permute-done.34.second, bf16[256,512]{1,0:T(8,128)(2,1)S(1)} %get-tuple-element.44.refs_0_, ...), custom_call_target="tpu_custom_call" | custom-call | tf_op jit(solution)/shard_map/prefix_project/pallas_call | solution.py:190
  77.8 9.4 %collective-permute-done.refs_1_ = bf16[64,2048]{1,0:T(8,128)(2,1)S(1)} collective-permute-done((bf16[64,2048]{1,0:T(8,128)(2,1)S(1)}, bf16[64,2048]{1,0:T(8,128)(2,1)S(1)}, u32[]{:S(2)}, u32[]{:S(2)}) %collective-permute-start) | collective-permute-done | bytes 262176 | tf_op jit(solution)/shard_map/ppermute | solution.py:540
  87.6 4.6 %collective-permute-done.12.refs_13_ = bf16[128,1024]{1,0:T(8,128)(2,1)S(1)} collective-permute-done((bf16[128,1024]{1,0:T(8,128)(2,1)S(1)}, bf16[128,1024]{1,0:T(8,128)(2,1)S(1)}, u32[]{:S(2)}, u32[]{:S(2)}) %collective-permute-start.12) | collective-permute-done | bytes 262176 | tf_op jit(solution)/shard_map/ppermute | solution.py:540
  92.6 7.4 %collective-permute-done.3.refs_4_ = bf16[64,2048]{1,0:T(8,128)(2,1)S(1)} collective-permute-done((bf16[64,2048]{1,0:T(8,128)(2,1)S(1)}, bf16[64,2048]{1,0:T(8,128)(2,1)S(1)}, u32[]{:S(2)}, u32[]{:S(2)}) %collective-permute-start.3) | collective-permute-done | bytes 262176 | tf_op jit(solution)/shard_map/ppermute | solution.py:544
  101.3 3.2 %prefix_project.2 = (f32[256,1024]{1,0:T(8,128)S(1)}, f32[256,1024]{1,0:T(8,128)S(1)}) custom-call(bf16[256,2048]{1,0:T(8,128)(2,1)S(1)} %collective-permute-done.17.first, bf16[256,2048]{1,0:T(8,128)(2,1)S(1)} %get-tuple-element.30.second, bf16[256,512]{1,0:T(8,128)(2,1)S(1)} %get-tuple-element.44.refs_0_, ...), custom_call_target="tpu_custom_call" | custom-call | tf_op jit(solution)/shard_map/prefix_project/pallas_call | solution.py:190
  105.1 3.7 %collective-permute-done.13.refs_14_ = bf16[128,1024]{1,0:T(8,128)(2,1)S(1)} collective-permute-done((bf16[128,1024]{1,0:T(8,128)(2,1)S(1)}, bf16[128,1024]{1,0:T(8,128)(2,1)S(1)}, u32[]{:S(2)}, u32[]{:S(2)}) %collective-permute-start.13) | collective-permute-done | bytes 262176 | tf_op jit(solution)/shard_map/ppermute | solution.py:540
  109.4 6.7 %collective-permute-done.37.refs_0_ = bf16[64,2048]{1,0:T(8,128)(2,1)S(1)} collective-permute-done((bf16[64,2048]{1,0:T(8,128)(2,1)S(1)}, bf16[64,2048]{1,0:T(8,128)(2,1)S(1)}, u32[]{:S(2)}, u32[]{:S(2)}) %collective-permute-start.37) | collective-permute-done | bytes 262176 | tf_op jit(solution)/shard_map/ppermute | solution.py:540
  117.9 3.2 %collective-permute-done.41.refs_4_ = bf16[128,1024]{1,0:T(8,128)(2,1)S(1)} collective-permute-done((bf16[128,1024]{1,0:T(8,128)(2,1)S(1)}, bf16[128,1024]{1,0:T(8,128)(2,1)S(1)}, u32[]{:S(2)}, u32[]{:S(2)}) %collective-permute-start.41) | collective-permute-done | bytes 262176 | tf_op jit(solution)/shard_map/ppermute | solution.py:540
  121.6 3.7 %collective-permute-done.38.refs_1_ = bf16[64,2048]{1,0:T(8,128)(2,1)S(1)} collective-permute-done((bf16[64,2048]{1,0:T(8,128)(2,1)S(1)}, bf16[64,2048]{1,0:T(8,128)(2,1)S(1)}, u32[]{:S(2)}, u32[]{:S(2)}) %collective-permute-start.38) | collective-permute-done | bytes 262176 | tf_op jit(solution)/shard_map/ppermute | solution.py:544
  125.8 3.1 %expert_prepare.1 = (bf16[1024,2048]{1,0:T(8,128)(2,1)S(1)}, bf16[1024,1024]{1,0:T(8,128)(2,1)S(1)}, bf16[192,1024]{1,0:T(8,128)(2,1)S(1)}, bf16[192,1024]{1,0:T(8,128)(2,1)S(1)}, f32[64,192]{1,0:T(8,128)S(1)}) custom-call(f32[32,50]{1,0:T(8,128)S(1)} %bitcast.16, f32[32,1024]{1,0:T(8,128)S(1)} %copy-done.2, bf16[32,1024]{1,0:T(8,128)(2,1)S(1)} %bitcast.15, ...), custom_call_target="tpu_custom_call" | custom-call | tf_op jit(solution)/shard_map/expert_prepare/pallas_call | solution.py:313
  129.7 11.0 %expert_steps.1 = (f32[32,50]{1,0:T(8,128)}, bf16[1024,2048]{1,0:T(8,128)(2,1)S(1)}, bf16[1024,1024]{1,0:T(8,128)(2,1)S(1)}, bf16[4,384,128]{2,1,0:T(8,128)(2,1)S(1)}, bf16[4,384,128]{2,1,0:T(8,128)(2,1)S(1)}) custom-call(s32[1]{0:T(128)S(6)} %copy.24.lengths, ...), custom_call_target="tpu_custom_call", output_to_operand_aliasing={{1}: (6, {}), {2}: (7, {}), {3}: (8, {}), {4}: (9, {})} | custom-call | tf_op jit(solution)/shard_map/expert_steps/pallas_call | solution.py:478
  (108 shorter events, 28.4 us)
Async XLA Ops:
  1.9 12.3 %collective-permute-start.25 = (bf16[256,512]{1,0:T(8,128)(2,1)S(1)}, bf16[256,512]{1,0:T(8,128)(2,1)S(1)}, u32[]{:S(2)}, u32[]{:S(2)}) collective-permute-start(bf16[256,512]{1,0:T(8,128)(2,1)S(1)} %get-tuple-element.43.refs_8_), channel_id=1, source_target_pairs={{0,4},{1,5},{2,6},{3,7},{4,8},{5,9},{6,10},{7,11},{8,12},{9,13},{1... | collective-permute-start | bytes 786440 | tf_op jit(solution)/shard_map/ppermute | solution.py:540
  5.1 14.8 %collective-permute-start.18 = (bf16[256,512]{1,0:T(8,128)(2,1)S(1)}, bf16[256,512]{1,0:T(8,128)(2,1)S(1)}, u32[]{:S(2)}, u32[]{:S(2)}) collective-permute-start(bf16[256,512]{1,0:T(8,128)(2,1)S(1)} %get-tuple-element.44.refs_0_), channel_id=1, source_target_pairs={{0,4},{1,5},{2,6},{3,7},{4,8},{5,9},{6,10},{7,11},{8,12},{9,13},{1... | collective-permute-start | bytes 786440 | tf_op jit(solution)/shard_map/ppermute | solution.py:540
  6.6 18.3 %collective-permute-start.28 = (bf16[256,512]{1,0:T(8,128)(2,1)S(1)}, bf16[256,512]{1,0:T(8,128)(2,1)S(1)}, u32[]{:S(2)}, u32[]{:S(2)}) collective-permute-start(bf16[256,512]{1,0:T(8,128)(2,1)S(1)} %get-tuple-element.43.refs_8_), channel_id=1, source_target_pairs={{0,2},{1,3},{2,0},{3,1},{4,6},{5,7},{6,4},{7,5},{8,10},{9,11},{10,... | collective-permute-start | bytes 786440 | tf_op jit(solution)/shard_map/ppermute | solution.py:544
  8.1 16.8 %collective-permute-start.21 = (bf16[256,512]{1,0:T(8,128)(2,1)S(1)}, bf16[256,512]{1,0:T(8,128)(2,1)S(1)}, u32[]{:S(2)}, u32[]{:S(2)}) collective-permute-start(bf16[256,512]{1,0:T(8,128)(2,1)S(1)} %get-tuple-element.44.refs_0_), channel_id=1, source_target_pairs={{0,2},{1,3},{2,0},{3,1},{4,6},{5,7},{6,4},{7,5},{8,10},{9,11},{10,... | collective-permute-start | bytes 786440 | tf_op jit(solution)/shard_map/ppermute | solution.py:544
  14.2 12.8 %collective-permute-start.29 = (bf16[256,512]{1,0:T(8,128)(2,1)S(1)}, bf16[256,512]{1,0:T(8,128)(2,1)S(1)}, u32[]{:S(2)}, u32[]{:S(2)}) collective-permute-start(bf16[256,512]{1,0:T(8,128)(2,1)S(1)} %collective-permute-done.25.refs_9_), channel_id=1, source_target_pairs={{0,2},{1,3},{2,0},{3,1},{4,6},{5,7},{6,4},{7,5},{8,10},{9,11},{10,... | collective-permute-start | bytes 786440 | tf_op jit(solution)/shard_map/ppermute | solution.py:544
  16.0 12.7 %collective-permute-start.26 = (bf16[256,512]{1,0:T(8,128)(2,1)S(1)}, bf16[256,512]{1,0:T(8,128)(2,1)S(1)}, u32[]{:S(2)}, u32[]{:S(2)}) collective-permute-start(bf16[256,512]{1,0:T(8,128)(2,1)S(1)} %collective-permute-done.25.refs_9_), channel_id=1, source_target_pairs={{0,4},{1,5},{2,6},{3,7},{4,8},{5,9},{6,10},{7,11},{8,12},{9,13},{1... | collective-permute-start | bytes 786440 | tf_op jit(solution)/shard_map/ppermute | solution.py:540
  19.8 12.6 %collective-permute-start.22 = (bf16[256,512]{1,0:T(8,128)(2,1)S(1)}, bf16[256,512]{1,0:T(8,128)(2,1)S(1)}, u32[]{:S(2)}, u32[]{:S(2)}) collective-permute-start(bf16[256,512]{1,0:T(8,128)(2,1)S(1)} %collective-permute-done.18.refs_1_), channel_id=1, source_target_pairs={{0,2},{1,3},{2,0},{3,1},{4,6},{5,7},{6,4},{7,5},{8,10},{9,11},{10,... | collective-permute-start | bytes 786440 | tf_op jit(solution)/shard_map/ppermute | solution.py:544
  24.9 32.1 %collective-permute-start.33 = (bf16[256,2048]{1,0:T(8,128)(2,1)S(1)}, bf16[256,2048]{1,0:T(8,128)(2,1)S(1)}, u32[]{:S(2)}, u32[]{:S(2)}) collective-permute-start(bf16[256,2048]{1,0:T(8,128)(2,1)S(1)} %pick_columns.4), channel_id=1, source_target_pairs={{0,17},{1,16},{2,19},{3,18},{4,21},{5,20},{6,23},{7,22},{8,25},{9,... | collective-permute-start | bytes 3145736 | tf_op jit(solution)/shard_map/ppermute | solution.py:551
  24.9 47.9 %collective-permute-start.34 = (bf16[256,2048]{1,0:T(8,128)(2,1)S(1)}, bf16[256,2048]{1,0:T(8,128)(2,1)S(1)}, u32[]{:S(2)}, u32[]{:S(2)}) collective-permute-start(bf16[256,2048]{1,0:T(8,128)(2,1)S(1)} %pick_columns.5), channel_id=1, source_target_pairs={{0,16},{16,0},{1,17},{17,1},{2,18},{18,2},{3,19},{19,3},{4,20},{20... | collective-permute-start | bytes 3145736 | tf_op jit(solution)/shard_map/ppermute | solution.py:553
  27.0 11.0 %collective-permute-start.19 = (bf16[256,512]{1,0:T(8,128)(2,1)S(1)}, bf16[256,512]{1,0:T(8,128)(2,1)S(1)}, u32[]{:S(2)}, u32[]{:S(2)}) collective-permute-start(bf16[256,512]{1,0:T(8,128)(2,1)S(1)} %collective-permute-done.18.refs_1_), channel_id=1, source_target_pairs={{0,4},{1,5},{2,6},{3,7},{4,8},{5,9},{6,10},{7,11},{8,12},{9,13},{1... | collective-permute-start | bytes 786440 | tf_op jit(solution)/shard_map/ppermute | solution.py:540
  32.5 11.1 %collective-permute-start.27 = (bf16[256,512]{1,0:T(8,128)(2,1)S(1)}, bf16[256,512]{1,0:T(8,128)(2,1)S(1)}, u32[]{:S(2)}, u32[]{:S(2)}) collective-permute-start(bf16[256,512]{1,0:T(8,128)(2,1)S(1)} %collective-permute-done.26.refs_10_), channel_id=1, source_target_pairs={{0,4},{1,5},{2,6},{3,7},{4,8},{5,9},{6,10},{7,11},{8,12},{9,13},{1... | collective-permute-start | bytes 786440 | tf_op jit(solution)/shard_map/ppermute | solution.py:540
  44.9 55.1 %collective-permute-start.17 = (bf16[256,2048]{1,0:T(8,128)(2,1)S(1)}, bf16[256,2048]{1,0:T(8,128)(2,1)S(1)}, u32[]{:S(2)}, u32[]{:S(2)}) collective-permute-start(bf16[256,2048]{1,0:T(8,128)(2,1)S(1)} %pick_columns.3), channel_id=1, source_target_pairs={{0,1},{1,0},{2,3},{3,2},{4,5},{5,4},{6,7},{7,6},{8,9},{9,8},{10,11... | collective-permute-start | bytes 3145736 | tf_op jit(solution)/shard_map/ppermute | solution.py:555
  51.1 25.0 %collective-permute-start.11 = (bf16[64,1024]{1,0:T(8,128)(2,1)S(1)}, bf16[64,1024]{1,0:T(8,128)(2,1)S(1)}, u32[]{:S(2)}, u32[]{:S(2)}) collective-permute-start(bf16[64,1024]{1,0:T(8,128)(2,1)S(1)} %copy-done.7), channel_id=1, source_target_pairs={{0,2},{1,3},{2,0},{3,1},{4,6},{5,7},{6,4},{7,5},{8,10},{9,11},{10,... | collective-permute-start | bytes 393224 | tf_op jit(solution)/shard_map/ppermute | solution.py:544
  57.0 19.2 %collective-permute-start.5 = (bf16[64,2048]{1,0:T(8,128)(2,1)S(1)}, bf16[64,2048]{1,0:T(8,128)(2,1)S(1)}, u32[]{:S(2)}, u32[]{:S(2)}) collective-permute-start(bf16[64,2048]{1,0:T(8,128)(2,1)S(1)} %pad_maximum_fusion.refs_0_), channel_id=1, source_target_pairs={{0,1},{1,0},{2,3},{3,2},{4,5},{5,4},{6,7},{7,6},{8,9},{9,8},{10,11... | collective-permute-start | bytes 786440 | tf_op jit(solution)/shard_map/ppermute | solution.py:547
  57.0 19.7 %collective-permute-start.2 = (bf16[64,2048]{1,0:T(8,128)(2,1)S(1)}, bf16[64,2048]{1,0:T(8,128)(2,1)S(1)}, u32[]{:S(2)}, u32[]{:S(2)}) collective-permute-start(bf16[64,2048]{1,0:T(8,128)(2,1)S(1)} %pad_maximum_fusion.refs_0_), channel_id=1, source_target_pairs={{0,2},{1,3},{2,0},{3,1},{4,6},{5,7},{6,4},{7,5},{8,10},{9,11},{10,... | collective-permute-start | bytes 786440 | tf_op jit(solution)/shard_map/ppermute | solution.py:544
  76.0 33.2 %collective-permute-start.35 = (f32[256,1024]{1,0:T(8,128)S(1)}, f32[256,1024]{1,0:T(8,128)S(1)}, u32[]{:S(2)}, u32[]{:S(2)}) collective-permute-start(f32[256,1024]{1,0:T(8,128)S(1)} %get-tuple-element.34), channel_id=1, source_target_pairs={{0,1},{1,0},{2,3},{3,2},{4,5},{5,4},{6,7},{7,6},{8,9},{9,8},{10,11... | collective-permute-start | bytes 3145736 | tf_op jit(solution)/shard_map/ppermute | solution.py:594
  76.1 11.0 %collective-permute-start = (bf16[64,2048]{1,0:T(8,128)(2,1)S(1)}, bf16[64,2048]{1,0:T(8,128)(2,1)S(1)}, u32[]{:S(2)}, u32[]{:S(2)}) collective-permute-start(bf16[64,2048]{1,0:T(8,128)(2,1)S(1)} %pad_maximum_fusion.refs_0_), channel_id=1, source_target_pairs={{0,4},{1,5},{2,6},{3,7},{4,8},{5,9},{6,10},{7,11},{8,12},{9,13},{1... | collective-permute-start | bytes 786440 | tf_op jit(solution)/shard_map/ppermute | solution.py:540
  76.7 15.5 %collective-permute-start.12 = (bf16[128,1024]{1,0:T(8,128)(2,1)S(1)}, bf16[128,1024]{1,0:T(8,128)(2,1)S(1)}, u32[]{:S(2)}, u32[]{:S(2)}) collective-permute-start(bf16[128,1024]{1,0:T(8,128)(2,1)S(1)} %constant_dynamic-update-slice_fusion.refs_12_), channel_id=1, source_target_pairs={{0,4},{1,5},{2,6},{3,7},{4,8},{5,9},{6,10},{7,11},{8,12},{9,13},{1... | collective-permute-start | bytes 786440 | tf_op jit(solution)/shard_map/ppermute | solution.py:540
  92.5 12.0 %collective-permute-start.1 = (bf16[64,2048]{1,0:T(8,128)(2,1)S(1)}, bf16[64,2048]{1,0:T(8,128)(2,1)S(1)}, u32[]{:S(2)}, u32[]{:S(2)}) collective-permute-start(bf16[64,2048]{1,0:T(8,128)(2,1)S(1)} %collective-permute-done.refs_1_), channel_id=1, source_target_pairs={{0,4},{1,5},{2,6},{3,7},{4,8},{5,9},{6,10},{7,11},{8,12},{9,13},{1... | collective-permute-start | bytes 786440 | tf_op jit(solution)/shard_map/ppermute | solution.py:540
  92.5 12.6 %collective-permute-start.15 = (bf16[128,1024]{1,0:T(8,128)(2,1)S(1)}, bf16[128,1024]{1,0:T(8,128)(2,1)S(1)}, u32[]{:S(2)}, u32[]{:S(2)}) collective-permute-start(bf16[128,1024]{1,0:T(8,128)(2,1)S(1)} %collective-permute-done.12.refs_13_), channel_id=1, source_target_pairs={{0,1},{1,0},{2,3},{3,2},{4,5},{5,4},{6,7},{7,6},{8,9},{9,8},{10,11... | collective-permute-start | bytes 786440 | tf_op jit(solution)/shard_map/ppermute | solution.py:547
  104.5 24.4 %collective-permute-start.32 = (f32[256,1024]{1,0:T(8,128)S(1)}, f32[256,1024]{1,0:T(8,128)S(1)}, u32[]{:S(2)}, u32[]{:S(2)}) collective-permute-start(f32[256,1024]{1,0:T(8,128)S(1)} %get-tuple-element.32), channel_id=1, source_target_pairs={{0,1},{1,0},{2,3},{3,2},{4,5},{5,4},{6,7},{7,6},{8,9},{9,8},{10,11... | collective-permute-start | bytes 3145736 | tf_op jit(solution)/shard_map/ppermute | solution.py:597
  105.1 11.0 %collective-permute-start.37 = (bf16[64,2048]{1,0:T(8,128)(2,1)S(1)}, bf16[64,2048]{1,0:T(8,128)(2,1)S(1)}, u32[]{:S(2)}, u32[]{:S(2)}) collective-permute-start(bf16[64,2048]{1,0:T(8,128)(2,1)S(1)} %collective-permute-done.1.refs_2_), channel_id=1, source_target_pairs={{0,4},{1,5},{2,6},{3,7},{4,8},{5,9},{6,10},{7,11},{8,12},{9,13},{1... | collective-permute-start | bytes 786440 | tf_op jit(solution)/shard_map/ppermute | solution.py:540
  109.2 11.9 %collective-permute-start.41 = (bf16[128,1024]{1,0:T(8,128)(2,1)S(1)}, bf16[128,1024]{1,0:T(8,128)(2,1)S(1)}, u32[]{:S(2)}, u32[]{:S(2)}) collective-permute-start(bf16[128,1024]{1,0:T(8,128)(2,1)S(1)} %collective-permute-done.13.refs_14_), channel_id=1, source_target_pairs={{0,4},{1,5},{2,6},{3,7},{4,8},{5,9},{6,10},{7,11},{8,12},{9,13},{1... | collective-permute-start | bytes 786440 | tf_op jit(solution)/shard_map/ppermute | solution.py:540
  116.1 12.9 %collective-permute-start.36 = (bf16[256,1024]{1,0:T(8,128)(2,1)S(1)}, bf16[256,1024]{1,0:T(8,128)(2,1)S(1)}, u32[]{:S(2)}, u32[]{:S(2)}) collective-permute-start(bf16[256,1024]{1,0:T(8,128)(2,1)S(1)} %add_convert_fusion), channel_id=1, source_target_pairs={{0,16},{16,0},{1,17},{17,1},{2,18},{18,2},{3,19},{19,3},{4,20},{20... | collective-permute-start | bytes 1572872 | tf_op jit(solution)/shard_map/ppermute | solution.py:596
  (30 other events, 350.3 us)
